TPU v7x, 128 devices: a whole 4x4x4 slice. The times are simulated.
128 devices in a mesh: enc: 16 (over y, x), abs: 8 (over z, core).
Axes of the slice: x: 4, y: 4, z: 4, core: 2. Of those that a mesh axis runs over, the one named last changes fastest.
Arguments:
- tiles: bfloat16 [768, 24, 24, 1024], P('enc', None, None, 'abs'), may hold values from -6 to 6
- w_in: bfloat16 [1024, 1024], replicated, may hold values from -0.1875 to 0.1875
- w_out: bfloat16 [1024, 1024], replicated, may hold values from -0.1875 to 0.1875
- se_down: bfloat16 [1024, 256], replicated, may hold values from -0.1875 to 0.1875
- se_up: bfloat16 [256, 1024], replicated, may hold values from -0.375 to 0.375
- kernel: bfloat16 [9, 1024], replicated, may hold values from -2 to 2
- gain: bfloat16 [1024], replicated, may hold values from 0.5 to 1.5
- token_grads: bfloat16 [1280, 144, 1024], P(('enc', 'abs')), may hold values from -6 to 6
- tile_counts: int32 [16, 16], replicated, may hold values from 1 to 9, as said below
- sample_owner: int32 [16, 16], replicated, may hold values from 0 to 15, as said below
- sample_rank: int32 [16, 16], replicated, may hold values from 0 to 15, as said below
Outputs:
- visual: bfloat16 [1280, 144, 1024], P(('enc', 'abs'))
- tile_grads: bfloat16 [768, 24, 24, 1024], P('enc', None, None, 'abs')
- w_in_grad: float32 [1024, 1024], P(('enc', 'abs'))
- w_out_grad: float32 [1024, 1024], P(('enc', 'abs'))
- se_down_grad: float32 [1024, 256], P(('enc', 'abs'))
- se_up_grad: float32 [256, 1024], P(('enc', 'abs'))
- kernel_grad: float32 [9, 1024], P(None, ('enc', 'abs'))
- gain_grad: float32 [1024], P(('enc', 'abs'))
Inputs may be any that keep to these rules, and one draw needn't show every extreme that they name: `tile_counts`: the samples of every encoder group hold 48 tiles together; the samples owned by one abstractor group hold at most 80 tiles together. `sample_owner`: every row names each abstractor group once. `sample_rank`: the 16 samples owned by one abstractor group have distinct ranks.
All inputs are finite; a program needn't handle non-finite values.
Results may differ from a plain program's by a relative error of at most 0.0066.
Values may be sent and summed in bfloat16 or wider, within the bound.
No kernel may reach another device: no remote copies, remote signals or barrier semaphores. Data moves between devices by JAX's collectives and lax.ppermute only.
A program may use at most 192 MiB of HBM per device.

v0:
```python
import math

import jax
import jax.numpy as jnp
from jax import lax
from jax.sharding import PartitionSpec as P

MOST = 9


NORM_EPS = 1e-06


def route_tables(counts, owners, ranks):
    groups = counts.shape[0]
    start = jnp.cumsum(counts, axis=1, dtype=jnp.int32) - counts
    flat_counts = counts.reshape(-1)
    flat_owners = owners.reshape(-1)
    flat_ranks = ranks.reshape(-1)
    ahead = (flat_owners[:, None] == flat_owners[None, :]) & (
        flat_ranks[None, :] < flat_ranks[:, None]
    )
    offset = jnp.sum(jnp.where(ahead, flat_counts[None, :], 0), axis=1, dtype=jnp.int32).reshape(
        groups, groups
    )
    owner_axis = jnp.arange(groups, dtype=jnp.int32)
    filled = jnp.sum(
        jnp.where(flat_owners[None, :] == owner_axis[:, None], flat_counts[None, :], 0),
        axis=1,
        dtype=jnp.int32,
    )
    return (start, offset, filled)


def pool_tiles(raw):
    count, grid, channels = (raw.shape[0], raw.shape[1], raw.shape[3])
    side = grid // 2
    wide = raw.astype(jnp.float32).reshape(count, side, 2, side, 2, channels)
    pooled = (jnp.sum(wide, axis=(2, 4)) * 0.25).astype(jnp.bfloat16)
    return pooled.reshape(count, side * side, channels)


def spread_back(grads, grid):
    count, cells, channels = grads.shape
    side = grid // 2
    quarter = (grads.astype(jnp.float32) * 0.25).reshape(count, side, 1, side, 1, channels)
    whole = jnp.broadcast_to(quarter, (count, side, 2, side, 2, channels))
    return whole.reshape(count, grid, grid, channels).astype(jnp.bfloat16)


def depthwise(field, taps, side):
    count, cells, channels = field.shape
    plane = field.reshape(count, side, side, channels)
    padded = jnp.pad(plane, ((0, 0), (1, 1), (1, 1), (0, 0)))
    result = jnp.zeros_like(plane)
    for row_tap in range(3):
        for col_tap in range(3):
            result = (
                result
                + taps[3 * row_tap + col_tap]
                * padded[:, row_tap : row_tap + side, col_tap : col_tap + side, :]
            )
    return result.reshape(count, cells, channels)


def depthwise_back(back, taps, side):
    count, cells, channels = back.shape
    plane = back.reshape(count, side, side, channels)
    padded = jnp.pad(plane, ((0, 0), (1, 1), (1, 1), (0, 0)))
    result = jnp.zeros_like(plane)
    for row_tap in range(3):
        for col_tap in range(3):
            result = (
                result
                + taps[3 * row_tap + col_tap]
                * padded[:, 2 - row_tap : 2 - row_tap + side, 2 - col_tap : 2 - col_tap + side, :]
            )
    return result.reshape(count, cells, channels)


def kernel_terms(back, activated, side):
    count, cells, channels = back.shape
    plane = back.reshape(count, side, side, channels)
    padded = jnp.pad(
        activated.reshape(count, side, side, channels), ((0, 0), (1, 1), (1, 1), (0, 0))
    )
    rows_out = []
    for row_tap in range(3):
        for col_tap in range(3):
            window = padded[:, row_tap : row_tap + side, col_tap : col_tap + side, :]
            rows_out.append(jnp.sum(plane * window, axis=(0, 1, 2)))
    return jnp.stack(rows_out, axis=0)


def silu_slope(value):
    sig = jax.nn.sigmoid(value)
    return sig * (1.0 + value * (1.0 - sig))


def block_forward(pooled, w_in, w_out, se_down, se_up, kernel, gain):
    count, cells, width = pooled.shape
    side = math.isqrt(cells)
    wide = pooled.astype(jnp.float32)
    average = jnp.mean(wide, axis=-1, keepdims=True)
    centred = wide - average
    variance = jnp.mean(centred * centred, axis=-1, keepdims=True)
    inverse = lax.rsqrt(variance + NORM_EPS)
    standard = centred * inverse
    normed = (standard * gain.astype(jnp.float32)).astype(jnp.bfloat16)
    hidden = jnp.dot(normed.reshape(-1, width), w_in, preferred_element_type=jnp.float32).reshape(
        count, cells, width
    )
    activated = jax.nn.silu(hidden)
    spatial = depthwise(activated, kernel.astype(jnp.float32), side)
    mixed = jax.nn.silu(spatial)
    squeeze = jnp.mean(mixed, axis=1)
    squeeze_pre = jnp.dot(squeeze, se_down.astype(jnp.float32), precision=lax.Precision.HIGHEST)
    squeeze_act = jax.nn.silu(squeeze_pre)
    excite = jax.nn.sigmoid(
        jnp.dot(squeeze_act, se_up.astype(jnp.float32), precision=lax.Precision.HIGHEST)
    )
    scaled = (mixed * excite[:, None, :]).astype(jnp.bfloat16)
    output = jnp.dot(scaled.reshape(-1, width), w_out, preferred_element_type=jnp.float32).reshape(
        count, cells, width
    )
    block = (wide + output).astype(jnp.bfloat16)
    saved = (
        standard,
        inverse,
        normed,
        hidden,
        activated,
        spatial,
        mixed,
        squeeze,
        squeeze_pre,
        squeeze_act,
        excite,
        scaled,
    )
    return (block, saved)


def block_backward(saved, upstream, w_in, w_out, se_down, se_up, kernel, gain):
    (
        standard,
        inverse,
        normed,
        hidden,
        activated,
        spatial,
        mixed,
        squeeze,
        squeeze_pre,
        squeeze_act,
        excite,
        scaled,
    ) = saved
    count, cells, width = upstream.shape
    side = math.isqrt(cells)
    flat_up = upstream.reshape(-1, width)
    w_out_term = jnp.dot(scaled.reshape(-1, width).T, flat_up, preferred_element_type=jnp.float32)
    back_scaled = jnp.dot(flat_up, w_out.T, preferred_element_type=jnp.float32).reshape(
        count, cells, width
    )
    back_excite = jnp.sum(back_scaled * mixed, axis=1)
    back_pre = back_excite * excite * (1.0 - excite)
    se_up_term = jnp.dot(squeeze_act.T, back_pre, precision=lax.Precision.HIGHEST)
    back_squeeze_act = jnp.dot(
        back_pre, se_up.astype(jnp.float32).T, precision=lax.Precision.HIGHEST
    )
    back_squeeze_pre = back_squeeze_act * silu_slope(squeeze_pre)
    se_down_term = jnp.dot(squeeze.T, back_squeeze_pre, precision=lax.Precision.HIGHEST)
    back_squeeze = jnp.dot(
        back_squeeze_pre, se_down.astype(jnp.float32).T, precision=lax.Precision.HIGHEST
    )
    back_mixed = back_scaled * excite[:, None, :] + back_squeeze[:, None, :] / cells
    back_spatial = back_mixed * silu_slope(spatial)
    kernel_term = kernel_terms(back_spatial, activated, side)
    back_act = depthwise_back(back_spatial, kernel.astype(jnp.float32), side)
    back_hidden = (back_act * silu_slope(hidden)).astype(jnp.bfloat16)
    flat_hidden = back_hidden.reshape(-1, width)
    w_in_term = jnp.dot(
        normed.reshape(-1, width).T, flat_hidden, preferred_element_type=jnp.float32
    )
    back_normed = jnp.dot(flat_hidden, w_in.T, preferred_element_type=jnp.float32).reshape(
        count, cells, width
    )
    gain_term = jnp.sum(back_normed * standard, axis=(0, 1))
    back_x = back_normed * gain.astype(jnp.float32)
    centre_term = jnp.mean(back_x, axis=-1, keepdims=True)
    along_term = jnp.mean(back_x * standard, axis=-1, keepdims=True)
    back_pooled = upstream.astype(jnp.float32) + inverse * (
        back_x - centre_term - standard * along_term
    )
    terms = (w_in_term, w_out_term, se_down_term, se_up_term, kernel_term, gain_term)
    return (back_pooled.astype(jnp.bfloat16), terms)


def take_rows(source, rows, valid):
    gathered = jnp.take(source, rows, axis=0)
    return jnp.where(valid[:, None, None], gathered, jnp.zeros_like(gathered))


def pick_row(table, chosen):
    return jnp.sum(jnp.where(chosen[:, None], table, 0), axis=0, dtype=jnp.int32)


def local(
    tiles,
    w_in,
    w_out,
    se_down,
    se_up,
    kernel,
    gain,
    token_grads,
    tile_counts,
    sample_owner,
    sample_rank,
):
    groups = lax.axis_size("enc")
    columns = lax.axis_size("abs")
    group_id = lax.axis_index("enc")
    column_id = lax.axis_index("abs")
    local_tiles = tiles.shape[0]
    owned_rows = token_grads.shape[0]
    capacity = owned_rows * columns
    cells = token_grads.shape[1]
    start, offset, filled = route_tables(tile_counts, sample_owner, sample_rank)
    sources = jnp.arange(groups, dtype=jnp.int32)
    slot_steps = jnp.arange(MOST, dtype=jnp.int32)
    this_group = sources == group_id
    owner_row = pick_row(sample_owner, this_group)
    count_row = pick_row(tile_counts, this_group)
    start_row = pick_row(start, this_group)
    chosen = owner_row[None, :] == sources[:, None]
    send_count = jnp.sum(jnp.where(chosen, count_row[None, :], 0), axis=1, dtype=jnp.int32)
    send_start = jnp.sum(jnp.where(chosen, start_row[None, :], 0), axis=1, dtype=jnp.int32)
    send_valid = slot_steps[None, :] < send_count[:, None]
    send_rows = jnp.where(send_valid, send_start[:, None] + slot_steps[None, :], 0).reshape(-1)
    arriving = sample_owner == group_id
    recv_count = jnp.sum(jnp.where(arriving, tile_counts, 0), axis=1, dtype=jnp.int32)
    recv_offset = jnp.sum(jnp.where(arriving, offset, 0), axis=1, dtype=jnp.int32)
    positions = jnp.arange(capacity, dtype=jnp.int32)
    inside = (positions[:, None] >= recv_offset[None, :]) & (
        positions[:, None] < (recv_offset + recv_count)[None, :]
    )
    gather_rows = jnp.sum(
        jnp.where(inside, sources[None, :] * MOST + positions[:, None] - recv_offset[None, :], 0),
        axis=1,
        dtype=jnp.int32,
    )
    occupied = jnp.any(inside, axis=1)
    return_valid = slot_steps[None, :] < recv_count[:, None]
    return_rows = jnp.where(return_valid, recv_offset[:, None] + slot_steps[None, :], 0).reshape(-1)
    tile_ids = jnp.arange(local_tiles, dtype=jnp.int32)
    member = (
        jnp.sum(
            (start_row[None, :] <= tile_ids[:, None]).astype(jnp.int32), axis=1, dtype=jnp.int32
        )
        - 1
    )
    which = member[:, None] == sources[None, :]
    member_owner = jnp.sum(jnp.where(which, owner_row[None, :], 0), axis=1, dtype=jnp.int32)
    member_start = jnp.sum(jnp.where(which, start_row[None, :], 0), axis=1, dtype=jnp.int32)
    unpack_rows = member_owner * MOST + tile_ids - member_start
    filled_here = jnp.sum(jnp.where(this_group, filled, 0), dtype=jnp.int32)
    live = column_id * owned_rows + jnp.arange(owned_rows, dtype=jnp.int32) < filled_here
    pooled = pool_tiles(tiles)
    narrow = pooled.shape[2]
    send = take_rows(pooled, send_rows, send_valid.reshape(-1)).reshape(groups, MOST, cells, narrow)
    received = lax.all_to_all(send, "enc", split_axis=0, concat_axis=0, tiled=True)
    compact = take_rows(received.reshape(groups * MOST, cells, narrow), gather_rows, occupied)
    owned = lax.all_to_all(compact, "abs", split_axis=0, concat_axis=2, tiled=True)
    visual, saved = block_forward(owned, w_in, w_out, se_down, se_up, kernel, gain)
    upstream = jnp.where(live[:, None, None], token_grads, jnp.zeros_like(token_grads))
    back_in, terms = block_backward(saved, upstream, w_in, w_out, se_down, se_up, kernel, gain)
    back_narrow = lax.all_to_all(back_in, "abs", split_axis=2, concat_axis=0, tiled=True)
    returned = take_rows(back_narrow, return_rows, return_valid.reshape(-1)).reshape(
        groups, MOST, cells, narrow
    )
    arrived = lax.all_to_all(returned, "enc", split_axis=0, concat_axis=0, tiled=True)
    back_source = jnp.take(arrived.reshape(groups * MOST, cells, narrow), unpack_rows, axis=0)
    tile_grads = spread_back(back_source, tiles.shape[1])
    summed = (
        lax.psum_scatter(terms[0], ("enc", "abs"), scatter_dimension=0, tiled=True),
        lax.psum_scatter(terms[1], ("enc", "abs"), scatter_dimension=0, tiled=True),
        lax.psum_scatter(terms[2], ("enc", "abs"), scatter_dimension=0, tiled=True),
        lax.psum_scatter(terms[3], ("enc", "abs"), scatter_dimension=0, tiled=True),
        lax.psum_scatter(terms[4], ("enc", "abs"), scatter_dimension=1, tiled=True),
        lax.psum_scatter(terms[5], ("enc", "abs"), scatter_dimension=0, tiled=True),
    )
    scale = 1.0 / math.sqrt(groups * local_tiles * cells)
    return (
        visual,
        tile_grads,
        summed[0] * scale,
        summed[1] * scale,
        summed[2] * scale,
        summed[3] * scale,
        summed[4] * scale,
        summed[5] * scale,
    )


def solution(mesh):
    return jax.shard_map(
        local,
        mesh=mesh,
        in_specs=(
            P("enc", None, None, "abs"),
            P(),
            P(),
            P(),
            P(),
            P(),
            P(),
            P(("enc", "abs"), None, None),
            P(),
            P(),
            P(),
        ),
        out_specs=(
            P(("enc", "abs"), None, None),
            P("enc", None, None, "abs"),
            P(("enc", "abs"), None),
            P(("enc", "abs"), None),
            P(("enc", "abs"), None),
            P(("enc", "abs"), None),
            P(None, ("enc", "abs")),
            P(("enc", "abs")),
        ),
        check_vma=False,
    )
```

profile of v0, /device:TPU:0, one launch (start us, length us, event | category | flops | bytes accessed | tf_op | source)
XLA Modules:
  0.0 2362.6 jit_solution(3114259339975368703)
XLA Ops:
  13.4 15.8 convert_reduce_fusion
  34.9 9.6 gather_fusion
  44.5 6.2 select_select_fusion.1
  50.7 7.2 all-to-all-start
  58.1 78.9 %all-to-all-done = bf16[16,9,144,128]{3,2,1,0:T(8,128)(2,1)} async-done(((bf16[16,9,144,128]{3,2,1,0:T(8,128)(2,1)}), bf16[16,9,144,128]{3,2,1,0:T(8,128)(2,1)}, u32[]{:S(2)}, u32[]{:S(2)}) %all-to-all-start) | async-done | bytes 5308448 | tf_op jit(solution)/shard_map/all_to_all | solution.py:273
  153.2 34.7 %all-to-all-done.1 = bf16[80,144,128]{2,1,0:T(8,128)(2,1)} async-done(((bf16[80,144,128]{2,1,0:T(8,128)(2,1)}), bf16[80,144,128]{2,1,0:T(8,128)(2,1)}, u32[]{:S(2)}, u32[]{:S(2)}) %all-to-all-start.1) | async-done | bytes 2949152 | tf_op jit(solution)/shard_map/all_to_all | solution.py:275
  193.0 10.2 fusion.23
  203.2 7.1 reshape.402
  210.2 28.2 %multiply_reduce_fusion.8 = (f32[10,1024]{1,0:T(8,128)S(1)}, f32[10,12,12,1024]{3,2,1,0:T(8,128)}) fusion(f32[1024]{0:T(1024)S(1)} %bitcast.145, f32[1024]{0:T(1024)S(1)} %bitcast.143, f32[1024]{0:T(1024)S(1)} %bitcast.141, f32[1024]{0:T(1024)S(1)} %bitcast.139, f32[10,12,12,1024]{3,2,1,0:T(8,128)} %reshape.402, f32[1024]{0:T(1024)S(1)} %bitcast.137, ...), kind=kLoop, calls=%fused_computation.45 | loop fusion | flops 32430080 | bytes 11874304 | tf_op jit(solution)/shard_map/reduce_sum | solution.py:116
  238.4 7.2 reshape.403
  246.4 10.8 multiply_reduce_fusion.12
  262.4 9.2 convolution_bitcast_fusion
  271.6 18.2 multiply_reduce_fusion.10
  289.9 7.1 reshape.404
  296.9 47.2 %multiply_reduce_fusion = (f32[1024]{0:T(1024)S(1)}, f32[1024]{0:T(1024)S(1)}, f32[1024]{0:T(1024)S(1)}, f32[1024]{0:T(1024)S(1)}, f32[1024]{0:T(1024)S(1)}, /*i...) fusion(f32[10,12,12,1024]{3,2,1,0:T(8,128)} %reshape.404, ...), kind=kLoop, calls=%fused_computation.37 | loop fusion | flops 48652288 | bytes 17764352 | tf_op jit(solution)/shard_map/reduce_sum | solution.py:91
  344.1 7.2 reshape.405
  356.8 7.2 multiply_reduce_fusion.9
  369.2 12.7 copy.49
  381.9 11.6 reshape.450
  398.2 8.5 convolution_bitcast_fusion.1
  407.0 27.6 %all-to-all-done.2 = bf16[8,2,92160]{2,1,0:T(2,128)(2,1)} async-done(((bf16[8,2,92160]{2,1,0:T(2,128)(2,1)}), bf16[8,2,92160]{2,1,0:T(2,128)(2,1)}, u32[]{:S(2)}, u32[]{:S(2)}) %all-to-all-start.2) | async-done | bytes 2949152 | tf_op jit(solution)/shard_map/all_to_all | solution.py:279
  434.6 10.8 reshape.451
  445.4 9.8 copy.51
  455.1 9.9 gather_fusion.2
  465.1 6.2 select_select_fusion
  471.3 5.5 all-to-all-start.3
  477.1 133.6 %all-reduce.5 = (f32[9,1024]{1,0:T(8,128)S(1)}, f32[1024]{0:T(1024)S(1)}) all-reduce(f32[9,1024]{1,0:T(8,128)S(1)} %stack.39, f32[1024]{0:T(1024)S(1)} %get-tuple-element.56), channel_id=6, replica_groups=mesh['enc'=16,'abs'=8] {'enc','abs'}, use_global_device_ids=true, to_apply=%region_36.37.clone | all-reduce | flops 10240 | bytes 81920
  612.0 9.3 fusion.21
  622.7 444.4 %reduce-scatter.9.cloned.1.call-done = f32[8,256]{1,0:T(8,128)} async-done(((f32[1024,256]{1,0:T(8,128)}), f32[8,256]{1,0:T(8,128)}) %reduce-scatter.9.cloned.1.call-update) | async-done | bytes 8208 | tf_op jit(solution)/shard_map/reduce_scatter | solution.py:289
  1077.2 632.3 %reduce-scatter.7.cloned.1.call-done = f32[8,1024]{1,0:T(8,128)} async-done(((f32[1024,1024]{1,0:T(8,128)}), f32[8,1024]{1,0:T(8,128)}) %reduce-scatter.7.cloned.1.call-update) | async-done | bytes 32784 | tf_op jit(solution)/shard_map/reduce_scatter | solution.py:288
  1710.9 637.2 %reduce-scatter.5.cloned.1.call-done = f32[8,1024]{1,0:T(8,128)} async-done(((f32[1024,1024]{1,0:T(8,128)}), f32[8,1024]{1,0:T(8,128)}) %reduce-scatter.5.cloned.1.call-update) | async-done | bytes 32784 | tf_op jit(solution)/shard_map/reduce_scatter | solution.py:287
  2349.4 6.2 broadcast_in_dim.242
  (101 shorter events, 70.6 us)
Async XLA Ops:
  7.2 185.8 %copy-start = (bf16[1024,1024]{1,0:T(8,128)(2,1)S(1)}, bf16[1024,1024]{1,0:T(8,128)(2,1)}, u32[]{:S(2)}) copy-start(bf16[1024,1024]{1,0:T(8,128)(2,1)} %param.12) | copy-start | bytes 6291460
  12.6 0.5 copy-start.6
  12.6 16.6 copy-start.8
  50.7 86.3 %all-to-all-start = ((bf16[16,9,144,128]{3,2,1,0:T(8,128)(2,1)}), bf16[16,9,144,128]{3,2,1,0:T(8,128)(2,1)}, u32[]{:S(2)}, u32[]{:S(2)}) async-start(bf16[16,9,144,128]{3,2,1,0:T(8,128)(2,1)} %select_select_fusion.1), calls=%async_computation | async-start | bytes 10616832 | tf_op jit(solution)/shard_map/all_to_all | solution.py:273
  142.2 9.5 copy-start.10
  142.2 10.9 copy-start.5
  146.1 41.8 %all-to-all-start.1 = ((bf16[80,144,128]{2,1,0:T(8,128)(2,1)}), bf16[80,144,128]{2,1,0:T(8,128)(2,1)}, u32[]{:S(2)}, u32[]{:S(2)}) async-start(bf16[80,144,128]{2,1,0:T(8,128)(2,1)} %select_select_fusion.2), calls=%async_computation.1 | async-start | bytes 5898240 | tf_op jit(solution)/shard_map/all_to_all | solution.py:275
  151.4 470.0 %all-reduce.8.cloned.1.call-start = ((), (), s32[]{:S(2)}) async-start(), calls=%async_computation.10 | async-start | bytes 2097152
  238.4 7.2 copy-start.3
  238.4 7.6 copy-start.4
  259.2 807.9 %reduce-scatter.9.cloned.1.call-start = ((), (), s32[]{:S(2)}) async-start(), calls=%async_computation.9 | async-start | bytes 1056768 | tf_op jit(solution)/shard_map/reduce_scatter | solution.py:289
  261.8 1447.7 %reduce-scatter.7.cloned.1.call-start = ((), (), s32[]{:S(2)}) async-start(), calls=%async_computation.8 | async-start | bytes 4227072 | tf_op jit(solution)/shard_map/reduce_scatter | solution.py:288
  356.7 7.2 copy-start.2
  356.8 7.2 copy-start.1
  393.5 41.1 %all-to-all-start.2 = ((bf16[8,2,92160]{2,1,0:T(2,128)(2,1)}), bf16[8,2,92160]{2,1,0:T(2,128)(2,1)}, u32[]{:S(2)}, u32[]{:S(2)}) async-start(bf16[8,2,92160]{2,1,0:T(2,128)(2,1)} %reshape.450), calls=%async_computation.2 | async-start | bytes 5898240 | tf_op jit(solution)/shard_map/all_to_all | solution.py:279
  397.9 1950.1 %reduce-scatter.5.cloned.1.call-start = ((), (), s32[]{:S(2)}) async-start(), calls=%async_computation.7 | async-start | bytes 4227072 | tf_op jit(solution)/shard_map/reduce_scatter | solution.py:287
  471.3 5.5 copy-start.7
  471.3 5.6 copy-start.9
  471.3 597.1 %all-to-all-start.3 = ((bf16[16,9,144,128]{3,2,1,0:T(8,128)(2,1)}), bf16[16,9,144,128]{3,2,1,0:T(8,128)(2,1)}, u32[]{:S(2)}, u32[]{:S(2)}) async-start(bf16[16,9,144,128]{3,2,1,0:T(8,128)(2,1)} %select_select_fusion), calls=%async_computation.3 | async-start | bytes 10616832 | tf_op jit(solution)/shard_map/all_to_all | solution.py:283
Sparse Core Ops, SparseCore 0:
  259.3 145.2 all-reduce.7
  407.1 660.0 reduce-scatter.8
  1069.5 639.9 reduce-scatter.6
  1711.8 636.2 reduce-scatter.4
where the time goes:
time: 2370 us; the launch traced here: 2360 us
  waiting for transfers between devices  1860 us (78%)
  other arithmetic  158 us (7%)
  blocking collectives  134 us (6%)
  local copies, waits for them, and re-layouts  118 us (5%)
  matrix products  61 us (3%)
    reduce_scatter x1, waiting for transfers between devices, local(): lax.psum_scatter(terms[0], ('enc', 'abs'), scatter_dimension=0, tiled=True)  637 us
    reduce_scatter x1, waiting for transfers between devices, local(): lax.psum_scatter(terms[1], ('enc', 'abs'), scatter_dimension=0, tiled=True)  632 us
    reduce_scatter x1, waiting for transfers between devices, local(): lax.psum_scatter(terms[2], ('enc', 'abs'), scatter_dimension=0, tiled=True)  444 us
    unnamed x1, blocking collectives  134 us
    all_to_all x1, waiting for transfers between devices, local(): lax.all_to_all(send, 'enc', split_axis=0, concat_axis=0, tiled=True)  78.9 us
    reduce_sum x2, other arithmetic, kernel_terms(): rows_out.append(jnp.sum(plane * window, axis=(0, 1, 2)))  65.4 us
  transfers between devices with their start and end apart: 8, of which 6 were waited for; matrix products, arithmetic and copies ran while one was open for 9% of the time, Pallas kernels for 0%

commit v1 on v0

v1 whole, which is shorter than its diff:
```python
import functools
import math

import jax
import jax.numpy as jnp
from jax import lax
from jax.experimental import pallas as pl
from jax.experimental.pallas import tpu as pltpu
from jax.sharding import PartitionSpec as P

F32 = jnp.float32
BF16 = jnp.bfloat16
NORM_EPS = 1e-06
LANES = 128
PAD = 16
CHUNKS = 2
VMEM_BYTES = 60 * 1024 * 1024
ANY = pl.BlockSpec(memory_space=pl.ANY)
SMEM = pl.BlockSpec(memory_space=pltpu.SMEM)
VMEM = pl.BlockSpec(memory_space=pltpu.VMEM)


def params(**more):
    return pltpu.CompilerParams(vmem_limit_bytes=VMEM_BYTES, **more)


def pool_kernel(steps, per, own_ref, pos_ref, tiles_ref, *rest):
    outs, (wide, pooled, sem) = rest[:CHUNKS], rest[CHUNKS:]
    step = pl.program_id(0)
    side = tiles_ref.shape[1] // 2
    width = 2 * side
    slots = outs[0].shape[1]
    for n in range(per):
        for row in range(side):
            pair = tiles_ref[n, 2 * row].astype(F32) + tiles_ref[n, 2 * row + 1].astype(F32)
            wide[pl.ds(row * width, width), :] = pair
        total = wide[pl.ds(0, side * side, stride=2), :] + wide[pl.ds(1, side * side, stride=2), :]
        j = step * per + n
        pooled[j] = (total * 0.25).astype(BF16)
        position = pos_ref[j]
        for h in range(CHUNKS):

            @pl.when(position // slots == h)
            def _(h=h):
                pltpu.make_async_copy(
                    pooled.at[j], outs[h].at[own_ref[j], position - h * slots], sem
                ).start()

    @pl.when(step == steps - 1)
    def _():
        @pl.loop(0, steps * per)
        def _(j):
            pltpu.make_async_copy(pooled.at[0], outs[0].at[0, 0], sem).wait()


def pool_and_pack(tiles, own, pos, groups, slots):
    count, grid, _, channels = tiles.shape
    cells = grid * grid // 4
    per = 4
    steps = count // per
    made = jax.ShapeDtypeStruct((groups, slots, cells, channels), BF16)
    return pl.pallas_call(
        functools.partial(pool_kernel, steps, per),
        grid=(steps,),
        in_specs=[SMEM, SMEM, pl.BlockSpec((per, grid, grid, channels), lambda i: (i, 0, 0, 0))],
        out_specs=[ANY] * CHUNKS,
        out_shape=[made] * CHUNKS,
        scratch_shapes=[
            pltpu.VMEM((grid * grid // 2, channels), F32),
            pltpu.VMEM((count, cells, channels), BF16),
            pltpu.SemaphoreType.DMA,
        ],
        compiler_params=params(),
        cost_estimate=pl.CostEstimate(flops=tiles.size, bytes_accessed=tiles.size * 3, transcendentals=0),
        name="pool_and_pack",
    )(own, pos, tiles)


def route_kernel(chunk, slots, per, columns, back, table_ref, filled_ref, src, dst, sem):
    filled = filled_ref[0]

    def copy(n):
        column, local = n // slots, n % slots
        q = column * per + chunk * slots + local
        group = table_ref[q]
        if back:
            one = pltpu.make_async_copy(src.at[column, local], dst.at[group, local], sem)
        else:
            one = pltpu.make_async_copy(src.at[group, local], dst.at[column, local], sem)
        return q, one

    @pl.loop(0, columns * slots)
    def _(n):
        q, one = copy(n)

        @pl.when(q < filled)
        def _():
            one.start()

    @pl.loop(0, columns * slots)
    def _(n):
        q, one = copy(n)

        @pl.when(q < filled)
        def _():
            one.wait()


def route(source, table, filled, chunk, per, columns, groups, back):
    slots, cells, channels = source.shape[1:]
    lead = groups if back else columns
    return pl.pallas_call(
        functools.partial(route_kernel, chunk, slots, per, columns, back),
        in_specs=[SMEM, SMEM, ANY],
        out_specs=ANY,
        out_shape=jax.ShapeDtypeStruct((lead, slots, cells, channels), BF16),
        scratch_shapes=[pltpu.SemaphoreType.DMA],
        compiler_params=params(),
        cost_estimate=pl.CostEstimate(
            flops=0, bytes_accessed=4 * columns * slots * cells * channels, transcendentals=0
        ),
        name="route_back" if back else "route_in",
    )(table, filled, source)


def exact_dot(left, weights):
    rows = left.shape[0]
    first = left.astype(BF16).astype(F32)
    rest = left - first
    second = rest.astype(BF16).astype(F32)
    third = rest - second
    stacked = jnp.concatenate([first, second, third, jnp.zeros_like(left)], axis=0).astype(BF16)
    made = jnp.dot(stacked, weights, preferred_element_type=F32)
    return made[:rows] + made[rows : 2 * rows] + made[2 * rows : 3 * rows]


def block_kernel(
    chunk,
    side,
    live_ref,
    x_hbm,
    up_hbm,
    w_in_hbm,
    w_out_hbm,
    w_in_t_hbm,
    w_out_t_hbm,
    se_down,
    se_up,
    se_down_t,
    se_up_t,
    taps,
    gain,
    *rest,
):
    (vis_hbm, normed_hbm, scaled_hbm, hidden_hbm, back_hbm, small_a, small_b, small_k) = rest[-25:-17]
    (
        x,
        up,
        w_in,
        w_out,
        w_in_t,
        w_out_t,
        standard,
        inverse,
        slope_h,
        act,
        mixed,
        slope_s,
        wide,
        tmp,
        masks,
        stage,
        sem,
    ) = rest[-17:]
    (rows_v, squeeze, excite, extra, kacc, gacc, normed, scaled, vis) = stage
    blocks, tiles, cells, lanes = x.shape
    width = blocks * lanes
    flat = tiles * cells
    loads = [
        pltpu.make_async_copy(a, b, sem.at[n])
        for n, (a, b) in enumerate(
            [
                (x_hbm, x),
                (w_in_hbm, w_in),
                (up_hbm.at[pl.ds(chunk * tiles, tiles)], up),
                (w_out_hbm, w_out),
                (w_out_t_hbm, w_out_t),
                (w_in_t_hbm, w_in_t),
            ]
        )
    ]
    for one in loads:
        one.start()

    column = lax.rem(lax.broadcasted_iota(jnp.int32, (cells, lanes), 0), side)
    masks[0] = jnp.where(column != 0, 1.0, 0.0).astype(F32)
    masks[1] = jnp.where(column != side - 1, 1.0, 0.0).astype(F32)
    edge = jnp.zeros((PAD, lanes), F32)
    tmp[pl.ds(0, PAD), :] = edge
    tmp[pl.ds(PAD + cells, PAD), :] = edge
    kacc[...] = jnp.zeros_like(kacc)
    gacc[...] = jnp.zeros_like(gacc)
    squeeze[...] = jnp.zeros_like(squeeze)
    extra[...] = jnp.zeros_like(extra)

    @pl.loop(0, blocks * tiles)
    def _(n):
        c, t = n % blocks, n // blocks
        act[c, t, pl.ds(0, PAD), :] = edge
        act[c, t, pl.ds(PAD + cells, PAD), :] = edge

    loads[0].wait()
    loads[2].wait()
    for t in range(tiles):

        @pl.when(chunk * tiles + t >= live_ref[0])
        def _(t=t):
            up[t] = jnp.zeros(up.shape[1:], BF16)
            for c in range(blocks):
                x[c, t] = jnp.zeros((cells, lanes), BF16)

    @pl.loop(0, tiles)
    def _(t):
        total = x[0, t].astype(F32)
        for c in range(1, blocks):
            total = total + x[c, t].astype(F32)
        average = jnp.sum(total, axis=1, keepdims=True) * (1.0 / width)
        square = jnp.zeros((cells, lanes), F32)
        for c in range(blocks):
            centred = x[c, t].astype(F32) - average
            square = square + centred * centred
        variance = jnp.sum(square, axis=1, keepdims=True) * (1.0 / width)
        inv = lax.rsqrt(variance + NORM_EPS)
        inverse[t] = jnp.broadcast_to(inv, (cells, lanes))
        for c in range(blocks):
            std = (x[c, t].astype(F32) - average) * inv
            standard[c, t] = std
            normed[t, :, c * lanes : (c + 1) * lanes] = (std * gain[c, 0:1, :]).astype(BF16)

    def product(left, right, put):
        wide_n = 256
        value = left[...].reshape(flat, width)
        for n in range(width // wide_n):
            made = jnp.dot(value, right[:, n * wide_n : (n + 1) * wide_n], preferred_element_type=F32)
            for half in range(wide_n // lanes):
                c = n * (wide_n // lanes) + half
                put(c, made[:, half * lanes : (half + 1) * lanes].reshape(tiles, cells, lanes))

    def put_hidden(c, value):
        slope_h[c] = value

    loads[1].wait()
    product(normed, w_in, put_hidden)
    save_normed = pltpu.make_async_copy(normed, normed_hbm.at[pl.ds(chunk * tiles, tiles)], sem.at[6])
    save_normed.start()

    @pl.loop(0, blocks * tiles)
    def _(n):
        c, t = n % blocks, n // blocks
        h = slope_h[c, t]
        sig = jax.nn.sigmoid(h)
        a = h * sig
        slope_h[c, t] = sig * (1.0 + h * (1.0 - sig))
        act[c, t, pl.ds(PAD, cells), :] = a

        def column_sum(b):
            made = None
            for r in range(3):
                term = taps[c, 3 * r + b : 3 * r + b + 1, :] * act[c, t, pl.ds(PAD + side * (r - 1) + b - 1, cells), :]
                made = term if made is None else made + term
            return made

        spatial = column_sum(1) + masks[0] * column_sum(0) + masks[1] * column_sum(2)
        sig = jax.nn.sigmoid(spatial)
        mix = spatial * sig
        mixed[c, t] = mix
        slope_s[c, t] = sig * (1.0 + spatial * (1.0 - sig))
        squeeze[c, pl.ds(t, 1), :] = jnp.sum(mix, axis=0, keepdims=True) * (1.0 / cells)

    def joined(ref):
        return jnp.concatenate([ref[c] for c in range(blocks)], axis=1)

    squeezed = joined(squeeze)
    squeeze_pre = exact_dot(squeezed, se_down[...])
    sig_pre = jax.nn.sigmoid(squeeze_pre)
    squeeze_act = squeeze_pre * sig_pre
    excited = jax.nn.sigmoid(exact_dot(squeeze_act, se_up[...]))
    for c in range(blocks):
        excite[c] = excited[:, c * lanes : (c + 1) * lanes]

    def put_back(c, value):
        wide[c] = value

    loads[4].wait()
    product(up, w_out_t, put_back)

    @pl.loop(0, tiles)
    def _(t):
        for c in range(blocks):
            mix = mixed[c, t]
            scaled[t, :, c * lanes : (c + 1) * lanes] = (mix * excite[c, pl.ds(t, 1), :]).astype(BF16)
            extra[c, pl.ds(t, 1), :] = jnp.sum(wide[c, t] * mix, axis=0, keepdims=True)

    back_pre = joined(extra) * excited * (1.0 - excited)
    back_squeeze_pre = exact_dot(back_pre, se_up_t[...]) * (
        sig_pre * (1.0 + squeeze_pre * (1.0 - sig_pre))
    )
    back_squeeze = exact_dot(back_squeeze_pre, se_down_t[...]) * (1.0 / cells)
    for c in range(blocks):
        extra[c] = back_squeeze[:, c * lanes : (c + 1) * lanes]
    small_a[0] = squeezed
    small_a[1] = back_pre
    small_b[0] = back_squeeze_pre
    small_b[1] = squeeze_act

    def put_visual(c, value):
        vis[:, :, c * lanes : (c + 1) * lanes] = (x[c].astype(F32) + value).astype(BF16)

    loads[3].wait()
    product(scaled, w_out, put_visual)
    save_scaled = pltpu.make_async_copy(scaled, scaled_hbm.at[pl.ds(chunk * tiles, tiles)], sem.at[7])
    save_scaled.start()
    save_vis = pltpu.make_async_copy(vis, vis_hbm.at[pl.ds(chunk * tiles, tiles)], sem.at[8])
    save_vis.start()
    save_normed.wait()

    @pl.loop(0, tiles)
    def _(t):
        for c in range(blocks):
            back = (wide[c, t] * excite[c, pl.ds(t, 1), :] + extra[c, pl.ds(t, 1), :]) * slope_s[c, t]
            tmp[pl.ds(PAD, cells), :] = back
            sides = (back * masks[0], back, back * masks[1])
            for r in range(3):
                for b in range(3):
                    term = sides[b] * act[c, t, pl.ds(PAD + side * (r - 1) + b - 1, cells), :]
                    kacc[c, 3 * r + b] += jnp.sum(term.reshape(cells // 8, 8, lanes), axis=0)

            def column_sum(b, c=c):
                made = None
                for r in range(3):
                    term = taps[c, 3 * r + b : 3 * r + b + 1, :] * tmp[pl.ds(PAD - side * (r - 1) - (b - 1), cells), :]
                    made = term if made is None else made + term
                return made

            back_act = column_sum(1) + masks[1] * column_sum(0) + masks[0] * column_sum(2)
            normed[t, :, c * lanes : (c + 1) * lanes] = (back_act * slope_h[c, t]).astype(BF16)

    loads[5].wait()
    product(normed, w_in_t, put_back)
    save_hidden = pltpu.make_async_copy(normed, hidden_hbm.at[pl.ds(chunk * tiles, tiles)], sem.at[9])
    save_hidden.start()

    @pl.loop(0, tiles)
    def _(t):
        centre = jnp.zeros((cells, lanes), F32)
        along = jnp.zeros((cells, lanes), F32)
        for c in range(blocks):
            along_n = wide[c, t] * standard[c, t]
            gacc[c] += jnp.sum(along_n.reshape(cells // 8, 8, lanes), axis=0)
            centre = centre + wide[c, t] * gain[c, 0:1, :]
            along = along + along_n * gain[c, 0:1, :]
        centre = jnp.sum(centre, axis=1, keepdims=True) * (1.0 / width)
        along = jnp.sum(along, axis=1, keepdims=True) * (1.0 / width)
        inv = inverse[t]
        for c in range(blocks):
            made = up[t, :, c * lanes : (c + 1) * lanes].astype(F32) + inv * (
                wide[c, t] * gain[c, 0:1, :] - centre - standard[c, t] * along
            )
            rows_v[c, t] = made.astype(BF16)

    save_back = pltpu.make_async_copy(rows_v, back_hbm, sem.at[10])
    save_back.start()
    small_k[...] = jnp.zeros_like(small_k)
    for c in range(blocks):
        for r in range(9):
            small_k[r : r + 1, c * lanes : (c + 1) * lanes] = jnp.sum(kacc[c, r], axis=0, keepdims=True)
        small_k[9:10, c * lanes : (c + 1) * lanes] = jnp.sum(gacc[c], axis=0, keepdims=True)
    save_scaled.wait()
    save_vis.wait()
    save_hidden.wait()
    save_back.wait()


def run_block(chunk, side, live, x, up, weights, carried):
    blocks, tiles, cells, lanes = x.shape
    width = blocks * lanes
    narrow = weights[4].shape[1]
    whole = jax.ShapeDtypeStruct(up.shape, BF16)
    fixed = [live, x, up, *weights]
    field = pltpu.VMEM((blocks, tiles, cells, lanes), F32)
    packed = pltpu.VMEM((tiles, cells, width), BF16)
    eight = pltpu.VMEM((blocks, 8, lanes), F32)
    square = pltpu.VMEM((width, width), BF16)
    flops = 8 * tiles * cells * width * width
    return pl.pallas_call(
        functools.partial(block_kernel, chunk, side),
        in_specs=[SMEM] + [ANY] * 6 + [VMEM] * 6 + [ANY] * len(carried),
        out_specs=[ANY] * 5 + [VMEM] * 3,
        out_shape=[whole] * 4
        + [
            jax.ShapeDtypeStruct((blocks, tiles, cells, lanes), BF16),
            jax.ShapeDtypeStruct((2, 8, width), F32),
            jax.ShapeDtypeStruct((2, 8, narrow), F32),
            jax.ShapeDtypeStruct((16, width), F32),
        ],
        input_output_aliases={len(fixed) + n: n for n in range(len(carried))},
        scratch_shapes=[
            pltpu.VMEM((blocks, tiles, cells, lanes), BF16),
            packed,
            square,
            square,
            square,
            square,
            field,
            pltpu.VMEM((tiles, cells, lanes), F32),
            field,
            pltpu.VMEM((blocks, tiles, cells + 2 * PAD, lanes), F32),
            field,
            field,
            field,
            pltpu.VMEM((cells + 2 * PAD, lanes), F32),
            pltpu.VMEM((2, cells, lanes), F32),
            [
                pltpu.VMEM((blocks, tiles, cells, lanes), BF16),
                eight,
                eight,
                eight,
                pltpu.VMEM((blocks, 9, 8, lanes), F32),
                eight,
                packed,
                packed,
                packed,
            ],
            pltpu.SemaphoreType.DMA((11,)),
        ],
        compiler_params=params(),
        cost_estimate=pl.CostEstimate(
            flops=flops, bytes_accessed=8 * x.size * 2 + 8 * width * width, transcendentals=2 * x.size
        ),
        name="block_%d" % chunk,
    )(*fixed, *carried)


def weights_kernel(normed, scaled, hidden, up, rest_ref, out):
    count, cells, columns = normed.shape
    flat = count * cells
    width = hidden.shape[2]

    def product(left, right):
        return lax.dot_general(
            left[...].reshape(flat, columns),
            right[...].reshape(flat, width),
            (((0,), (0,)), ((), ())),
            preferred_element_type=F32,
        )

    for place, (left, right) in enumerate(((normed, hidden), (scaled, up))):
        made = product(left, right).astype(BF16)
        for group in range(2):
            for z in range(4):
                for core in range(2):
                    row = 8 * (8 * group + 2 * z + core)
                    out[core, z, group, :, place * width : (place + 1) * width] = made[row : row + 8]
    out[:, :, :, :, 2 * width :] = rest_ref[...]


def weight_terms(normed, scaled, hidden, up, others):
    count, cells, width = normed.shape
    columns = 128
    lanes = 2 * width + others.shape[-1]
    left = pl.BlockSpec((count, cells, columns), lambda i: (0, 0, i))
    right = pl.BlockSpec((count, cells, width), lambda i: (0, 0, 0), pipeline_mode=pl.Buffered(1))
    return pl.pallas_call(
        weights_kernel,
        grid=(width // columns,),
        in_specs=[
            left,
            left,
            right,
            right,
            pl.BlockSpec((2, 4, 2, 8, others.shape[-1]), lambda i: (0, 0, i, 0, 0)),
        ],
        out_specs=pl.BlockSpec((2, 4, 2, 8, lanes), lambda i: (0, 0, i, 0, 0)),
        out_shape=jax.ShapeDtypeStruct((2, 4, 16, 8, lanes), BF16),
        compiler_params=params(),
        cost_estimate=pl.CostEstimate(
            flops=4 * count * cells * width * width, bytes_accessed=8 * count * cells * width, transcendentals=0
        ),
        name="weight_terms",
    )(normed, scaled, hidden, up, others)


def spread_kernel(per, own_ref, pos_ref, *rest):
    arrived, out, (held, wide, sem) = rest[:CHUNKS], rest[CHUNKS], rest[CHUNKS + 1 :]
    step = pl.program_id(0)
    slots = arrived[0].shape[1]
    count = held.shape[0]
    side = out.shape[1] // 2
    width = 2 * side

    @pl.when(step == 0)
    def _():
        @pl.loop(0, count)
        def _(j):
            position = pos_ref[j]
            for h in range(CHUNKS):

                @pl.when(position // slots == h)
                def _(h=h):
                    pltpu.make_async_copy(
                        arrived[h].at[own_ref[j], position - h * slots], held.at[j], sem
                    ).start()

        @pl.loop(0, count)
        def _(j):
            pltpu.make_async_copy(arrived[0].at[0, 0], held.at[0], sem).wait()

    for n in range(per):
        quarter = held[step * per + n].astype(F32) * 0.25
        wide[pl.ds(0, side * side, stride=2), :] = quarter
        wide[pl.ds(1, side * side, stride=2), :] = quarter
        for row in range(side):
            line = wide[pl.ds(row * width, width), :].astype(BF16)
            out[n, 2 * row] = line
            out[n, 2 * row + 1] = line


def unpack_and_spread(arrived, own, pos, count, grid):
    _, _, cells, channels = arrived[0].shape
    per = 4
    return pl.pallas_call(
        functools.partial(spread_kernel, per),
        grid=(count // per,),
        in_specs=[SMEM, SMEM] + [ANY] * CHUNKS,
        out_specs=pl.BlockSpec((per, grid, grid, channels), lambda i: (i, 0, 0, 0)),
        out_shape=jax.ShapeDtypeStruct((count, grid, grid, channels), BF16),
        scratch_shapes=[
            pltpu.VMEM((count, cells, channels), BF16),
            pltpu.VMEM((grid * grid // 2, channels), F32),
            pltpu.SemaphoreType.DMA,
        ],
        compiler_params=params(),
        cost_estimate=pl.CostEstimate(
            flops=0, bytes_accessed=10 * count * cells * channels, transcendentals=0
        ),
        name="unpack_and_spread",
    )(own, pos, *arrived)


def before(table):
    groups = table.shape[1]
    index = jnp.arange(groups, dtype=jnp.int32)
    lower = index[None, :] < index[:, None]
    return jnp.sum(jnp.where(lower[None], table[:, None, :], 0), axis=2, dtype=jnp.int32)


def routing(counts, owners, ranks, group_id, local_tiles, capacity):
    groups = counts.shape[0]
    start = before(counts)
    flat_counts, flat_owners, flat_ranks = counts.reshape(-1), owners.reshape(-1), ranks.reshape(-1)
    ahead = (flat_owners[:, None] == flat_owners[None, :]) & (flat_ranks[None, :] < flat_ranks[:, None])
    offset = jnp.sum(jnp.where(ahead, flat_counts[None, :], 0), axis=1, dtype=jnp.int32).reshape(groups, groups)
    sources = jnp.arange(groups, dtype=jnp.int32)
    mine = (sources == group_id)[:, None]

    def row(table):
        return jnp.sum(jnp.where(mine, table, 0), axis=0, dtype=jnp.int32)

    owner_row, start_row, offset_row = row(owners), row(start), row(offset)
    ids = jnp.arange(local_tiles, dtype=jnp.int32)
    member = jnp.sum((start_row[None, :] <= ids[:, None]).astype(jnp.int32), axis=1, dtype=jnp.int32) - 1
    which = member[:, None] == sources[None, :]
    own = jnp.sum(jnp.where(which, owner_row[None, :], 0), axis=1, dtype=jnp.int32)
    slot = jnp.sum(jnp.where(which, (offset_row - start_row)[None, :], 0), axis=1, dtype=jnp.int32) + ids
    arriving = owners == group_id
    recv_count = jnp.sum(jnp.where(arriving, counts, 0), axis=1, dtype=jnp.int32)
    recv_offset = jnp.sum(jnp.where(arriving, offset, 0), axis=1, dtype=jnp.int32)
    positions = jnp.arange(capacity, dtype=jnp.int32)
    inside = (positions[:, None] >= recv_offset[None, :]) & (
        positions[:, None] < (recv_offset + recv_count)[None, :]
    )
    table = jnp.sum(jnp.where(inside, sources[None, :], 0), axis=1, dtype=jnp.int32)
    filled = jnp.sum(recv_count, dtype=jnp.int32).reshape(1)
    return own, slot, table, filled


def local(
    tiles,
    w_in,
    w_out,
    se_down,
    se_up,
    kernel,
    gain,
    token_grads,
    tile_counts,
    sample_owner,
    sample_rank,
):
    groups = lax.axis_size("enc")
    columns = lax.axis_size("abs")
    group_id = lax.axis_index("enc")
    column_id = lax.axis_index("abs")
    local_tiles, grid = tiles.shape[0], tiles.shape[1]
    per, cells, width = token_grads.shape
    narrow = se_down.shape[1]
    capacity = per * columns
    side = grid // 2
    slots = per // CHUNKS
    blocks = width // LANES
    own, slot, table, filled = routing(
        tile_counts, sample_owner, sample_rank, group_id, local_tiles, capacity
    )
    pos = slot % per
    live = jnp.clip(filled - column_id * per, 0, per)
    sends = pool_and_pack(tiles, own, pos, groups, slots)

    taps = jnp.pad(kernel.astype(F32).reshape(9, blocks, LANES).transpose(1, 0, 2), ((0, 0), (0, 7), (0, 0)))
    gains = jnp.broadcast_to(gain.astype(F32).reshape(blocks, 1, LANES), (blocks, 8, LANES))
    weights = [w_in, w_out, w_in.T, w_out.T, se_down, se_up, se_down.T, se_up.T, taps, gains]

    inner = []
    for h in range(CHUNKS):
        send = sends[h]
        if h > 0:
            send, _ = lax.optimization_barrier((send, received))
        received = lax.all_to_all(send, "enc", split_axis=0, concat_axis=0, tiled=True)
        compact = route(received, table, filled, h, per, columns, groups, False)
        inner.append(lax.all_to_all(compact, "abs", split_axis=0, concat_axis=0, tiled=True))

    carried = []
    arrived, small = [], []
    for h in range(CHUNKS):
        made = run_block(h, side, live, inner[h], token_grads, weights, carried)
        carried = list(made[:4])
        small.append(made[5:])
        narrowed = lax.all_to_all(made[4], "abs", split_axis=0, concat_axis=0, tiled=True)
        back = route(narrowed, table, filled, h, per, columns, groups, True)
        arrived.append(lax.all_to_all(back, "enc", split_axis=0, concat_axis=0, tiled=True))
    visual, normed, scaled, hidden = carried
    tile_grads = unpack_and_spread(arrived, own, pos, local_tiles, grid)

    rows_a = jnp.concatenate([s[0] for s in small], axis=1)
    rows_b = jnp.concatenate([s[1] for s in small], axis=1)
    high = lax.Precision.HIGHEST
    down = jnp.dot(rows_a[0].T, rows_b[0], precision=high)
    up = jnp.dot(rows_b[1].T, rows_a[1], precision=high)
    both = sum(s[2] for s in small)[:10]
    devices = groups * columns
    down = down.reshape(devices, 8, narrow)
    up = up.reshape(devices, 8, narrow)
    both = both.reshape(10, devices, 8).transpose(1, 2, 0)
    both = jnp.pad(both, ((0, 0), (0, 0), (0, LANES - 10)))
    others = jnp.concatenate([down, up, both], axis=2).astype(BF16)
    others = others.reshape(groups, 4, 2, 8, -1).transpose(2, 1, 0, 3, 4)
    terms = weight_terms(normed, scaled, hidden, token_grads, others)

    core = column_id % 2
    away = jnp.where(core == 0, terms[1], terms[0])
    home = jnp.where(core == 0, terms[0], terms[1])
    near = lax.ppermute(away, "abs", [(n, n ^ 1) for n in range(columns)])
    pair = (home.astype(F32) + near.astype(F32)).astype(BF16)
    ring = [[2 * z + c for z in range(4)] for c in range(2)]
    column = lax.all_to_all(pair, "abs", split_axis=0, concat_axis=0, tiled=True, axis_index_groups=ring)
    column = jnp.sum(column.astype(F32), axis=0).astype(BF16)
    spread = lax.all_to_all(column, "enc", split_axis=0, concat_axis=0, tiled=True)
    scale = 1.0 / math.sqrt(groups * local_tiles * cells)
    total = jnp.sum(spread.astype(F32), axis=0) * scale
    w_in_grad = total[:, :width]
    w_out_grad = total[:, width : 2 * width]
    down_grad = total[:, 2 * width : 2 * width + narrow]
    up_grad = total[:, 2 * width + narrow : 2 * width + 2 * narrow].reshape(2, width)
    last = total[:, 2 * width + 2 * narrow : 2 * width + 2 * narrow + 10]
    return (
        visual,
        tile_grads,
        w_in_grad,
        w_out_grad,
        down_grad,
        up_grad,
        last[:, :9].T,
        last[:, 9],
    )


def solution(mesh):
    return jax.shard_map(
        local,
        mesh=mesh,
        in_specs=(
            P("enc", None, None, "abs"),
            P(),
            P(),
            P(),
            P(),
            P(),
            P(),
            P(("enc", "abs"), None, None),
            P(),
            P(),
            P(),
        ),
        out_specs=(
            P(("enc", "abs"), None, None),
            P("enc", None, None, "abs"),
            P(("enc", "abs"), None),
            P(("enc", "abs"), None),
            P(("enc", "abs"), None),
            P(("enc", "abs"), None),
            P(None, ("enc", "abs")),
            P(("enc", "abs")),
        ),
        check_vma=False,
    )
```

time: 2370 us -> 508 us (0.21)
  waiting for transfers between devices: 1860 us -> 146 us
  other arithmetic: 158 us -> 22.1 us
  Pallas kernels: 0 us -> 132 us
  starting transfers between devices: 23.1 us -> 123 us
  blocking collectives: 134 us -> 44.8 us
  local copies, waits for them, and re-layouts: 118 us -> 33.8 us
  matrix products: 61 us -> 1.98 us
    reduce_scatter x3 -> x0, waiting for transfers between devices: 1710 us -> none  [the longest x1 637 us: local(): lax.psum_scatter(terms[0], ('enc', 'abs'), scatter_dimension=0, tiled=True)]
    unnamed x1 -> x0, blocking collectives: 134 us -> none
    pallas_call x0 -> x9, Pallas kernels: none -> 132 us  [the longest x2 56.2 us: run_block(): pl.pallas_call(functools.partial(block_kernel, chunk, side), in_specs=[SM...]
    reduce_sum x15 -> x8, other arithmetic: 118 us -> 8.45 us  [the longest x1 3.23 us: local(): column = jnp.sum(column.astype(F32), axis=0).astype(BF16)]
    all_to_all x3 -> x8, starting transfers between devices: 15.3 us -> 119 us  [the longest x2 89.2 us: local(): lax.all_to_all(back, 'enc', split_axis=0, concat_axis=0, tiled=True)]
    dot_general x12 -> x2, matrix products: 61 us -> 1.98 us  [the longest x1 1.02 us: local(): up = jnp.dot(rows_b[1].T, rows_a[1], precision=high)]
    all_to_all x3 -> x8, waiting for transfers between devices: 62.3 us -> 118 us  [the longest x2 77.6 us: local(): lax.all_to_all(back, 'enc', split_axis=0, concat_axis=0, tiled=True)]
    all_to_all x1, waiting for transfers between devices: 78.9 us -> 27.6 us  [local(): lax.all_to_all(send, 'enc', split_axis=0, concat_axis=0, tiled=True)]
  transfers between devices with their start and end apart: 8 -> 10, of which waited for: 6 -> 7; matrix products, arithmetic and copies ran while one was open for 9% -> 9% of each run, Pallas kernels for 0% -> 25%
where the time goes in v1:
time: 508 us; the launch traced here: 505 us
  waiting for transfers between devices  146 us (29%)
  Pallas kernels  132 us (26%)
  starting transfers between devices  123 us (24%)
  blocking collectives  44.8 us (9%)
  local copies, waits for them, and re-layouts  33.8 us (7%)
  other arithmetic  22.1 us (4%)
    all_to_all x2, starting transfers between devices, local(): lax.all_to_all(back, 'enc', split_axis=0, concat_axis=0, tiled=True)  89.2 us
    all_to_all x2, waiting for transfers between devices, local(): lax.all_to_all(back, 'enc', split_axis=0, concat_axis=0, tiled=True)  77.6 us
    pallas_call x2, Pallas kernels, run_block(): pl.pallas_call(functools.partial(block_kernel, chunk, side), in_specs=[SM...  56.2 us
    pallas_call x4, Pallas kernels, route(): pl.pallas_call(functools.partial(route_kernel, chunk, slots, per, columns...  45.5 us
    all_to_all x1, blocking collectives, local(): lax.all_to_all(send, 'enc', split_axis=0, concat_axis=0, tiled=True)  44.8 us
    all_to_all x1, waiting for transfers between devices, local(): lax.all_to_all(send, 'enc', split_axis=0, concat_axis=0, tiled=True)  27.6 us
    all_to_all x1, waiting for transfers between devices, local(): lax.all_to_all(pair, 'abs', split_axis=0, concat_axis=0, tiled=True, axis...  24 us
    pallas_call x1, Pallas kernels, weight_terms(): pl.pallas_call(weights_kernel, grid=(width // columns,), in_specs=[left,...  13.6 us
  transfers between devices with their start and end apart: 10, of which 7 were waited for; matrix products, arithmetic and copies ran while one was open for 9% of the time, Pallas kernels for 25%

profile of v1, /device:TPU:0, one launch (start us, length us, event | category | flops | bytes accessed | tf_op | source)
XLA Modules:
  0.0 505.5 jit_solution(3421159860846084246)
XLA Ops:
  7.0 8.3 %pool_and_pack.1 = (bf16[16,5,144,128]{3,2,1,0:T(8,128)(2,1)}, bf16[16,5,144,128]{3,2,1,0:T(8,128)(2,1)}) custom-call(s32[48]{0:T(128)} %get-tuple-element.53.own_ref, s32[48]{0:T(128)} %and_select_fusion.pos_ref, bf16[48,24,24,128]{3,2,1,0:T(8,128)(2,1)} %tiles_ref.1), custom_call_target="tpu_custom_call" | custom-call | flops 3538944 | bytes 10616832 | tf_op jit(solution)/shard_map/pool_and_pack/pallas_call | solution.py:62
  15.4 44.8 %all_to_all.50.src = bf16[16,5,144,128]{3,2,1,0:T(8,128)(2,1)} all-to-all(bf16[16,5,144,128]{3,2,1,0:T(8,128)(2,1)} %get-tuple-element.28), channel_id=1, replica_groups=mesh['enc'=16,'abs'=8] {'enc'}, dimensions={0} | all-to-all | bytes 5898240 | tf_op jit(solution)/shard_map/all_to_all | solution.py:627
  60.1 3.7 all-to-all-start.1
  64.5 13.6 %route_in.3 = bf16[8,5,144,128]{3,2,1,0:T(8,128)(2,1)} custom-call(s32[80]{0:T(128)} %select_reduce_fusion.7.table_ref, s32[1]{0:T(128)} %bitcast.filled_ref, bf16[16,5,144,128]{3,2,1,0:T(8,128)(2,1)} %all_to_all.50.src), custom_call_target="tpu_custom_call" | custom-call | bytes 2949120 | tf_op jit(solution)/shard_map/route_in/pallas_call | solution.py:112
  78.1 27.6 %all-to-all-done.1.src = bf16[16,5,144,128]{3,2,1,0:T(8,128)(2,1)S(1)} async-done(((bf16[16,5,144,128]{3,2,1,0:T(8,128)(2,1)}), bf16[16,5,144,128]{3,2,1,0:T(8,128)(2,1)S(1)}, u32[]{:S(2)}, u32[]{:S(2)}) %all-to-all-start.1) | async-done | bytes 2949152 | tf_op jit(solution)/shard_map/all_to_all | solution.py:627
  105.7 5.3 %all-to-all-start.3 = ((bf16[8,5,144,128]{3,2,1,0:T(8,128)(2,1)}), bf16[8,5,144,128]{3,2,1,0:T(8,128)(2,1)}, u32[]{:S(2)}, u32[]{:S(2)}) async-start(bf16[8,5,144,128]{3,2,1,0:T(8,128)(2,1)} %route_in.3), calls=%async_computation.3 | async-start | bytes 2949120 | tf_op jit(solution)/shard_map/all_to_all | solution.py:629
  111.1 9.2 %route_in.2 = bf16[8,5,144,128]{3,2,1,0:T(8,128)(2,1)} custom-call(s32[80]{0:T(128)} %select_reduce_fusion.7.table_ref, s32[1]{0:T(128)} %bitcast.filled_ref, bf16[16,5,144,128]{3,2,1,0:T(8,128)(2,1)} %copy-done.2), custom_call_target="tpu_custom_call" | custom-call | bytes 2949120 | tf_op jit(solution)/shard_map/route_in/pallas_call | solution.py:112
  120.3 11.4 %all-to-all-done.3.x_hbm = bf16[8,5,144,128]{3,2,1,0:T(8,128)(2,1)} async-done(((bf16[8,5,144,128]{3,2,1,0:T(8,128)(2,1)}), bf16[8,5,144,128]{3,2,1,0:T(8,128)(2,1)}, u32[]{:S(2)}, u32[]{:S(2)}) %all-to-all-start.3) | async-done | bytes 1474592 | tf_op jit(solution)/shard_map/all_to_all | solution.py:629
  131.7 4.3 all-to-all-start.2
  138.7 2.5 copy.39
  141.2 4.0 copy.40
  146.4 28.0 %block_0.1 = (bf16[10,144,1024]{2,1,0:T(8,128)(2,1)}, bf16[10,144,1024]{2,1,0:T(8,128)(2,1)}, bf16[10,144,1024]{2,1,0:T(8,128)(2,1)}, bf16[10,144,1024]{2,1,0:T(...) custom-call(s32[1]{0:T(128)S(6)} %min.6.live_ref, ...), custom_call_target="tpu_custom_call" | custom-call | flops 6039797760 | bytes 20185088 | tf_op jit(solution)/shard_map/block_0/pallas_call | solution.py:395
  176.1 5.0 all-to-all-start.4
  181.1 28.2 %block_1.1 = (bf16[10,144,1024]{2,1,0:T(8,128)(2,1)}, bf16[10,144,1024]{2,1,0:T(8,128)(2,1)}, bf16[10,144,1024]{2,1,0:T(8,128)(2,1)}, bf16[10,144,1024]{2,1,0:T(...) custom-call(s32[1]{0:T(128)S(6)} %min.6.live_ref, ...), custom_call_target="tpu_custom_call", output_to_operand_aliasing={{0}: (13, {}), {1}: (14, {}), {2}: (15, {}), {3}: (16, {})} | custom-call | flops 6039797760 | bytes 20185088 | tf_op jit(solution)/shard_map/block_1/pallas_call | solution.py:395
  213.7 3.0 pad.13
  216.7 9.3 %copy.48 = bf16[16,4,2,8,128]{4,3,0,1,2:T(8,128)(2,1)S(1)} copy(bf16[16,4,2,8,128]{3,2,1,0,4:T(2,128)(2,1)} %bitcast.42) | data formatting | bytes 524288 | tf_op jit(solution)/shard_map/concatenate | solution.py:654
  228.2 13.6 %weight_terms.1 = bf16[2,4,16,8,2688]{4,3,2,1,0:T(8,128)(2,1)} custom-call(bf16[10,144,1024]{2,1,0:T(8,128)(2,1)} %get-tuple-element.37.normed, bf16[10,144,1024]{2,1,0:T(8,128)(2,1)} %get-tuple-element.38.scaled, bf16[10,144,1024]{2,1,0:T(8,128)(2,1)} %get-tuple-element.39.hidden, bf16[10,144,1024]{2,1,0:T(8,128)(2,1)} %up.1, ...), custom_call_target="tpu_custom_call" | custom-call | flops 6039797760 | bytes 11796480 | tf_op jit(solution)/shard_map/weight_terms/pallas_call | solution.py:473
  241.8 5.3 %all-to-all-start.6 = ((bf16[8,5,144,128]{3,2,1,0:T(8,128)(2,1)}), bf16[8,5,144,128]{3,2,1,0:T(8,128)(2,1)S(1)}, u32[]{:S(2)}, u32[]{:S(2)}) async-start(bf16[8,5,144,128]{3,2,1,0:T(8,128)(2,1)} %get-tuple-element.36), calls=%async_computation.6 | async-start | bytes 2949120 | tf_op jit(solution)/shard_map/all_to_all | solution.py:637
  247.0 4.4 select_bitcast_fusion
  252.0 13.6 %route_back.2 = bf16[16,5,144,128]{3,2,1,0:T(8,128)(2,1)} custom-call(s32[80]{0:T(128)} %select_reduce_fusion.7.table_ref, s32[1]{0:T(128)} %bitcast.filled_ref, bf16[8,5,144,128]{3,2,1,0:T(8,128)(2,1)} %copy-done.4), custom_call_target="tpu_custom_call" | custom-call | bytes 2949120 | tf_op jit(solution)/shard_map/route_back/pallas_call | solution.py:112
  268.8 70.9 %all-to-all-start.5 = ((bf16[16,5,144,128]{3,2,1,0:T(8,128)(2,1)}), bf16[16,5,144,128]{3,2,1,0:T(8,128)(2,1)S(1)}, u32[]{:S(2)}, u32[]{:S(2)}) async-start(bf16[16,5,144,128]{3,2,1,0:T(8,128)(2,1)} %route_back.2), calls=%async_computation.5 | async-start | bytes 5898240 | tf_op jit(solution)/shard_map/all_to_all | solution.py:639
  339.7 6.0 %fusion = bf16[4,16,8,2688]{3,2,1,0:T(8,128)(2,1)} fusion(bf16[4,16,8,2688]{3,2,1,0:T(8,128)(2,1)} %collective-permute-done, pred[]{:T(512)S(6)} %eq.63, bf16[2,4,16,8,2688]{4,3,2,1,0:T(8,128)(2,1)} %weight_terms.1), kind=kLoop, calls=%fused_computation.1 | loop fusion | flops 6881280 | bytes 11010049 | tf_op jit(solution)/shard_map/convert_element_type | solution.py:662
  345.7 39.0 %all-to-all-done.5.rest_0_ = bf16[16,5,144,128]{3,2,1,0:T(8,128)(2,1)S(1)} async-done(((bf16[16,5,144,128]{3,2,1,0:T(8,128)(2,1)}), bf16[16,5,144,128]{3,2,1,0:T(8,128)(2,1)S(1)}, u32[]{:S(2)}, u32[]{:S(2)}) %all-to-all-start.5) | async-done | bytes 2949152 | tf_op jit(solution)/shard_map/all_to_all | solution.py:639
  386.3 5.5 %all-to-all-start.8 = ((bf16[4,16,8,2688]{3,2,1,0:T(8,128)(2,1)}), bf16[4,16,8,2688]{3,2,1,0:T(8,128)(2,1)}, u32[]{:S(2)}, u32[]{:S(2)}) async-start(bf16[4,16,8,2688]{3,2,1,0:T(8,128)(2,1)} %fusion), calls=%async_computation.8 | async-start | bytes 5505024 | tf_op jit(solution)/shard_map/all_to_all | solution.py:664
  391.8 9.1 %route_back.3 = bf16[16,5,144,128]{3,2,1,0:T(8,128)(2,1)} custom-call(s32[80]{0:T(128)} %select_reduce_fusion.7.table_ref, s32[1]{0:T(128)} %bitcast.filled_ref, bf16[8,5,144,128]{3,2,1,0:T(8,128)(2,1)} %copy-done.5), custom_call_target="tpu_custom_call" | custom-call | bytes 2949120 | tf_op jit(solution)/shard_map/route_back/pallas_call | solution.py:112
  400.9 24.0 %all-to-all-done.8 = bf16[4,16,8,2688]{3,2,1,0:T(8,128)(2,1)} async-done(((bf16[4,16,8,2688]{3,2,1,0:T(8,128)(2,1)}), bf16[4,16,8,2688]{3,2,1,0:T(8,128)(2,1)}, u32[]{:S(2)}, u32[]{:S(2)}) %all-to-all-start.8) | async-done | bytes 2752544 | tf_op jit(solution)/shard_map/all_to_all | solution.py:664
  424.9 18.2 %all-to-all-start.7 = ((bf16[16,5,144,128]{3,2,1,0:T(8,128)(2,1)}), bf16[16,5,144,128]{3,2,1,0:T(8,128)(2,1)S(1)}, u32[]{:S(2)}, u32[]{:S(2)}) async-start(bf16[16,5,144,128]{3,2,1,0:T(8,128)(2,1)} %route_back.3), calls=%async_computation.7 | async-start | bytes 5898240 | tf_op jit(solution)/shard_map/all_to_all | solution.py:639
  443.2 3.2 reduce_sum.141
  446.4 38.6 %all-to-all-done.7.rest_1_ = bf16[16,5,144,128]{3,2,1,0:T(8,128)(2,1)S(1)} async-done(((bf16[16,5,144,128]{3,2,1,0:T(8,128)(2,1)}), bf16[16,5,144,128]{3,2,1,0:T(8,128)(2,1)S(1)}, u32[]{:S(2)}, u32[]{:S(2)}) %all-to-all-start.7) | async-done | bytes 2949152 | tf_op jit(solution)/shard_map/all_to_all | solution.py:639
  485.0 4.3 all-to-all-start.9
  489.3 8.5 %unpack_and_spread.1 = bf16[48,24,24,128]{3,2,1,0:T(8,128)(2,1)} custom-call(s32[48]{0:T(128)} %get-tuple-element.53.own_ref, s32[48]{0:T(128)} %and_select_fusion.pos_ref, bf16[16,5,144,128]{3,2,1,0:T(8,128)(2,1)} %copy-done, bf16[16,5,144,128]{3,2,1,0:T(8,128)(2,1)} %copy-done.1), custom_call_target="tpu_custom_call" | custom-call | bytes 8847360 | tf_op jit(solution)/shard_map/unpack_and_spread/pallas_call | solution.py:531
  497.8 3.3 all-to-all-done.9
  (70 shorter events, 28.0 us)
Async XLA Ops:
  60.1 45.6 %all-to-all-start.1 = ((bf16[16,5,144,128]{3,2,1,0:T(8,128)(2,1)}), bf16[16,5,144,128]{3,2,1,0:T(8,128)(2,1)S(1)}, u32[]{:S(2)}, u32[]{:S(2)}) async-start(bf16[16,5,144,128]{3,2,1,0:T(8,128)(2,1)} %get-tuple-element.29), calls=%async_computation.1 | async-start | bytes 5898240 | tf_op jit(solution)/shard_map/all_to_all | solution.py:627
  105.7 5.3 %copy-start.2 = (bf16[16,5,144,128]{3,2,1,0:T(8,128)(2,1)}, bf16[16,5,144,128]{3,2,1,0:T(8,128)(2,1)S(1)}, u32[]{:S(2)}) copy-start(bf16[16,5,144,128]{3,2,1,0:T(8,128)(2,1)S(1)} %all-to-all-done.1.src) | copy-start | bytes 8847364
  105.7 26.0 %all-to-all-start.3 = ((bf16[8,5,144,128]{3,2,1,0:T(8,128)(2,1)}), bf16[8,5,144,128]{3,2,1,0:T(8,128)(2,1)}, u32[]{:S(2)}, u32[]{:S(2)}) async-start(bf16[8,5,144,128]{3,2,1,0:T(8,128)(2,1)} %route_in.3), calls=%async_computation.3 | async-start | bytes 2949120 | tf_op jit(solution)/shard_map/all_to_all | solution.py:629
  111.1 25.6 %copy-start.9 = (bf16[9,1024]{1,0:T(8,128)(2,1)S(1)}, bf16[9,1024]{1,0:T(8,128)(2,1)}, u32[]{:S(2)}) copy-start(bf16[9,1024]{1,0:T(8,128)(2,1)} %param.16) | copy-start | bytes 55300
  111.1 25.6 %copy-start.6 = (bf16[1024,256]{1,0:T(8,128)(2,1)S(1)}, bf16[1024,256]{1,0:T(8,128)(2,1)}, u32[]{:S(2)}) copy-start(bf16[1024,256]{1,0:T(8,128)(2,1)} %se_down.3) | copy-start | bytes 1572868
  120.3 17.4 %copy-start.7 = (bf16[256,1024]{1,0:T(8,128)(2,1)S(1)}, bf16[256,1024]{1,0:T(8,128)(2,1)}, u32[]{:S(2)}) copy-start(bf16[256,1024]{1,0:T(8,128)(2,1)} %se_up.3) | copy-start | bytes 1572868
  120.3 18.4 %copy-start.3 = (bf16[1024,1024]{1,0:T(8,128)(2,1)S(1)}, bf16[1024,1024]{1,0:T(8,128)(2,1)}, u32[]{:S(2)}) copy-start(bf16[1024,1024]{1,0:T(8,128)(2,1)} %w_in_hbm.3) | copy-start | bytes 6291460
  131.7 44.4 %all-to-all-start.2 = ((bf16[8,5,144,128]{3,2,1,0:T(8,128)(2,1)}), bf16[8,5,144,128]{3,2,1,0:T(8,128)(2,1)}, u32[]{:S(2)}, u32[]{:S(2)}) async-start(bf16[8,5,144,128]{3,2,1,0:T(8,128)(2,1)} %route_in.2), calls=%async_computation.2 | async-start | bytes 2949120 | tf_op jit(solution)/shard_map/all_to_all | solution.py:629
  141.2 4.6 copy-start.10
  176.1 65.7 %all-to-all-start.4 = ((bf16[8,5,144,128]{3,2,1,0:T(8,128)(2,1)}), bf16[8,5,144,128]{3,2,1,0:T(8,128)(2,1)S(1)}, u32[]{:S(2)}, u32[]{:S(2)}) async-start(bf16[8,5,144,128]{3,2,1,0:T(8,128)(2,1)} %get-tuple-element.35), calls=%async_computation.4 | async-start | bytes 2949120 | tf_op jit(solution)/shard_map/all_to_all | solution.py:637
  181.1 28.2 %copy-start.8 = (f32[16,1024]{1,0:T(8,128)S(1)}, f32[16,1024]{1,0:T(8,128)}, u32[]{:S(2)}) copy-start(f32[16,1024]{1,0:T(8,128)} %get-tuple-element.44) | copy-start | bytes 196612
  241.7 9.7 %copy-start.4 = (bf16[8,5,144,128]{3,2,1,0:T(8,128)(2,1)}, bf16[8,5,144,128]{3,2,1,0:T(8,128)(2,1)S(1)}, u32[]{:S(2)}) copy-start(bf16[8,5,144,128]{3,2,1,0:T(8,128)(2,1)S(1)} %all-to-all-done.4.src) | copy-start | bytes 4423684
  241.8 25.8 %all-to-all-start.6 = ((bf16[8,5,144,128]{3,2,1,0:T(8,128)(2,1)}), bf16[8,5,144,128]{3,2,1,0:T(8,128)(2,1)S(1)}, u32[]{:S(2)}, u32[]{:S(2)}) async-start(bf16[8,5,144,128]{3,2,1,0:T(8,128)(2,1)} %get-tuple-element.36), calls=%async_computation.6 | async-start | bytes 2949120 | tf_op jit(solution)/shard_map/all_to_all | solution.py:637
  251.5 88.2 %collective-permute-start = (bf16[4,16,8,2688]{3,2,1,0:T(8,128)(2,1)}, bf16[4,16,8,2688]{3,2,1,0:T(8,128)(2,1)}, u32[]{:S(2)}, u32[]{:S(2)}) collective-permute-start(bf16[4,16,8,2688]{3,2,1,0:T(8,128)(2,1)} %select_bitcast_fusion), channel_id=1, source_target_pairs={{0,1},{1,0},{2,3},{3,2},{4,5},{5,4},{6,7},{7,6},{8,9},{9,8},{10,11... | collective-permute-start | bytes 8257544 | tf_op jit(solution)/shard_map/ppermute | solution.py:661
  267.6 1.2 copy-start.5
  268.8 115.9 %all-to-all-start.5 = ((bf16[16,5,144,128]{3,2,1,0:T(8,128)(2,1)}), bf16[16,5,144,128]{3,2,1,0:T(8,128)(2,1)S(1)}, u32[]{:S(2)}, u32[]{:S(2)}) async-start(bf16[16,5,144,128]{3,2,1,0:T(8,128)(2,1)} %route_back.2), calls=%async_computation.5 | async-start | bytes 5898240 | tf_op jit(solution)/shard_map/all_to_all | solution.py:639
  384.7 1.6 copy-start
  386.3 38.6 %all-to-all-start.8 = ((bf16[4,16,8,2688]{3,2,1,0:T(8,128)(2,1)}), bf16[4,16,8,2688]{3,2,1,0:T(8,128)(2,1)}, u32[]{:S(2)}, u32[]{:S(2)}) async-start(bf16[4,16,8,2688]{3,2,1,0:T(8,128)(2,1)} %fusion), calls=%async_computation.8 | async-start | bytes 5505024 | tf_op jit(solution)/shard_map/all_to_all | solution.py:664
  424.9 60.1 %all-to-all-start.7 = ((bf16[16,5,144,128]{3,2,1,0:T(8,128)(2,1)}), bf16[16,5,144,128]{3,2,1,0:T(8,128)(2,1)S(1)}, u32[]{:S(2)}, u32[]{:S(2)}) async-start(bf16[16,5,144,128]{3,2,1,0:T(8,128)(2,1)} %route_back.3), calls=%async_computation.7 | async-start | bytes 5898240 | tf_op jit(solution)/shard_map/all_to_all | solution.py:639
  485.0 4.3 copy-start.1
  485.0 16.1 %all-to-all-start.9 = ((bf16[16,8,2688]{2,1,0:T(8,128)(2,1)}), bf16[16,8,2688]{2,1,0:T(8,128)(2,1)}, u32[]{:S(2)}, u32[]{:S(2)}) async-start(bf16[16,8,2688]{2,1,0:T(8,128)(2,1)} %reduce_sum.141), calls=%async_computation.9 | async-start | bytes 1376256 | tf_op jit(solution)/shard_map/all_to_all | solution.py:666

commit v2 on v1

--- a/solution.py
+++ b/solution.py
@@ -76,51 +76,93 @@
     )(own, pos, tiles)
 
 
-def route_kernel(chunk, slots, per, columns, back, table_ref, filled_ref, src, dst, sem):
-    filled = filled_ref[0]
-
-    def copy(n):
-        column, local = n // slots, n % slots
-        q = column * per + chunk * slots + local
-        group = table_ref[q]
-        if back:
-            one = pltpu.make_async_copy(src.at[column, local], dst.at[group, local], sem)
-        else:
-            one = pltpu.make_async_copy(src.at[group, local], dst.at[column, local], sem)
-        return q, one
-
-    @pl.loop(0, columns * slots)
-    def _(n):
-        q, one = copy(n)
-
-        @pl.when(q < filled)
-        def _():
-            one.start()
-
-    @pl.loop(0, columns * slots)
-    def _(n):
-        q, one = copy(n)
-
-        @pl.when(q < filled)
-        def _():
-            one.wait()
-
-
-def route(source, table, filled, chunk, per, columns, groups, back):
-    slots, cells, channels = source.shape[1:]
-    lead = groups if back else columns
+def partner(me, step, columns, sign):
+    ring = columns // 2
+    z = lax.rem(me // 2 + sign * (step // 2) + ring, ring)
+    return 2 * z + lax.rem(lax.rem(me, 2) + step % 2, 2)
+
+
+def partner_pairs(step, columns):
+    ring = columns // 2
+    return [(n, 2 * ((n // 2 + step // 2) % ring) + (n % 2 + step) % 2) for n in range(columns)]
+
+
+def exchange(parts):
+    columns = len(parts)
+    return [parts[0]] + [lax.ppermute(parts[k], "abs", partner_pairs(k, columns)) for k in range(1, columns)]
+
+
+def route_in_kernel(chunk, slots, per, columns, table_ref, info_ref, src, *rest):
+    outs, (held, sem, out_sem) = rest[:columns], rest[columns:]
+    filled, me = info_ref[0], info_ref[1]
+
+    def each(act):
+        for k in range(columns):
+            first = partner(me, k, columns, 1) * per + chunk * slots
+
+            @pl.loop(0, slots)
+            def _(local, k=k, first=first):
+                q = first + local
+
+                @pl.when(q < filled)
+                def _():
+                    act(pltpu.make_async_copy(src.at[table_ref[q], local], held.at[k, local], sem))
+
+    each(lambda one: one.start())
+    each(lambda one: one.wait())
+    saves = [pltpu.make_async_copy(held.at[k], outs[k], out_sem.at[k]) for k in range(columns)]
+    for one in saves:
+        one.start()
+    for one in saves:
+        one.wait()
+
+
+def route_back_kernel(chunk, slots, per, columns, table_ref, info_ref, *rest):
+    srcs, (dst, held, sem, in_sem) = rest[:columns], rest[columns:]
+    filled, me = info_ref[0], info_ref[1]
+    loads = [pltpu.make_async_copy(srcs[k], held.at[k], in_sem.at[k]) for k in range(columns)]
+    for one in loads:
+        one.start()
+
+    def each(act, ready):
+        for k in range(columns):
+            first = partner(me, k, columns, -1) * per + chunk * slots
+            if ready:
+                loads[k].wait()
+
+            @pl.loop(0, slots)
+            def _(local, k=k, first=first):
+                q = first + local
+
+                @pl.when(q < filled)
+                def _():
+                    act(pltpu.make_async_copy(held.at[k, local], dst.at[table_ref[q], local], sem))
+
+    each(lambda one: one.start(), True)
+    each(lambda one: one.wait(), False)
+
+
+def route(sources, table, info, chunk, per, columns, groups, back):
+    slots, cells, channels = sources[0].shape[-3:]
+    part = jax.ShapeDtypeStruct((slots, cells, channels), BF16)
+    whole = jax.ShapeDtypeStruct((groups, slots, cells, channels), BF16)
+    body = route_back_kernel if back else route_in_kernel
     return pl.pallas_call(
-        functools.partial(route_kernel, chunk, slots, per, columns, back),
-        in_specs=[SMEM, SMEM, ANY],
-        out_specs=ANY,
-        out_shape=jax.ShapeDtypeStruct((lead, slots, cells, channels), BF16),
-        scratch_shapes=[pltpu.SemaphoreType.DMA],
-        compiler_params=params(),
+        functools.partial(body, chunk, slots, per, columns),
+        in_specs=[SMEM, SMEM] + [ANY] * len(sources),
+        out_specs=ANY if back else [ANY] * columns,
+        out_shape=whole if back else [part] * columns,
+        scratch_shapes=[
+            pltpu.VMEM((columns, slots, cells, channels), BF16),
+            pltpu.SemaphoreType.DMA,
+            pltpu.SemaphoreType.DMA((columns,)),
+        ],
+        compiler_params=pltpu.CompilerParams(vmem_limit_bytes=8 * 1024 * 1024),
         cost_estimate=pl.CostEstimate(
-            flops=0, bytes_accessed=4 * columns * slots * cells * channels, transcendentals=0
+            flops=0, bytes_accessed=8 * columns * slots * cells * channels, transcendentals=0
         ),
         name="route_back" if back else "route_in",
-    )(table, filled, source)
+    )(table, info, *sources)
 
 
 def exact_dot(left, weights):
@@ -137,22 +179,18 @@
 def block_kernel(
     chunk,
     side,
-    live_ref,
-    x_hbm,
-    up_hbm,
-    w_in_hbm,
-    w_out_hbm,
-    w_in_t_hbm,
-    w_out_t_hbm,
-    se_down,
-    se_up,
-    se_down_t,
-    se_up_t,
-    taps,
-    gain,
+    columns,
+    info_ref,
     *rest,
 ):
-    (vis_hbm, normed_hbm, scaled_hbm, hidden_hbm, back_hbm, small_a, small_b, small_k) = rest[-25:-17]
+    x_hbm, rest = rest[:columns], rest[columns:]
+    up_hbm, w_in_hbm, w_out_hbm, w_in_t_hbm, w_out_t_hbm = rest[:5]
+    se_down, se_up, se_down_t, se_up_t, taps, gain = rest[5:11]
+    outs = rest[-24 - columns : -17]
+    (vis_hbm, normed_hbm, scaled_hbm, hidden_hbm), back_hbm = outs[:4], outs[4 : 4 + columns]
+    small_a, small_b, small_k = outs[4 + columns :]
+    filled, me = info_ref[0], info_ref[1]
+    live = filled - me * info_ref[2]
     (
         x,
         up,
@@ -180,7 +218,6 @@
         pltpu.make_async_copy(a, b, sem.at[n])
         for n, (a, b) in enumerate(
             [
-                (x_hbm, x),
                 (w_in_hbm, w_in),
                 (up_hbm.at[pl.ds(chunk * tiles, tiles)], up),
                 (w_out_hbm, w_out),
@@ -189,7 +226,10 @@
             ]
         )
     ]
-    for one in loads:
+    x_loads = [
+        pltpu.make_async_copy(x_hbm[k], x.at[partner(me, k, columns, -1)], sem.at[10 + k]) for k in range(columns)
+    ]
+    for one in x_loads + loads:
         one.start()
 
     column = lax.rem(lax.broadcasted_iota(jnp.int32, (cells, lanes), 0), side)
@@ -209,11 +249,12 @@
         act[c, t, pl.ds(0, PAD), :] = edge
         act[c, t, pl.ds(PAD + cells, PAD), :] = edge
 
-    loads[0].wait()
-    loads[2].wait()
+    for one in x_loads:
+        one.wait()
+    loads[1].wait()
     for t in range(tiles):
 
-        @pl.when(chunk * tiles + t >= live_ref[0])
+        @pl.when(chunk * tiles + t >= live)
         def _(t=t):
             up[t] = jnp.zeros(up.shape[1:], BF16)
             for c in range(blocks):
@@ -249,7 +290,7 @@
     def put_hidden(c, value):
         slope_h[c] = value
 
-    loads[1].wait()
+    loads[0].wait()
     product(normed, w_in, put_hidden)
     save_normed = pltpu.make_async_copy(normed, normed_hbm.at[pl.ds(chunk * tiles, tiles)], sem.at[6])
     save_normed.start()
@@ -291,7 +332,7 @@
     def put_back(c, value):
         wide[c] = value
 
-    loads[4].wait()
+    loads[3].wait()
     product(up, w_out_t, put_back)
 
     @pl.loop(0, tiles)
@@ -316,7 +357,7 @@
     def put_visual(c, value):
         vis[:, :, c * lanes : (c + 1) * lanes] = (x[c].astype(F32) + value).astype(BF16)
 
-    loads[3].wait()
+    loads[2].wait()
     product(scaled, w_out, put_visual)
     save_scaled = pltpu.make_async_copy(scaled, scaled_hbm.at[pl.ds(chunk * tiles, tiles)], sem.at[7])
     save_scaled.start()
@@ -345,7 +386,7 @@
             back_act = column_sum(1) + masks[1] * column_sum(0) + masks[0] * column_sum(2)
             normed[t, :, c * lanes : (c + 1) * lanes] = (back_act * slope_h[c, t]).astype(BF16)
 
-    loads[5].wait()
+    loads[4].wait()
     product(normed, w_in_t, put_back)
     save_hidden = pltpu.make_async_copy(normed, hidden_hbm.at[pl.ds(chunk * tiles, tiles)], sem.at[9])
     save_hidden.start()
@@ -368,8 +409,12 @@
             )
             rows_v[c, t] = made.astype(BF16)
 
-    save_back = pltpu.make_async_copy(rows_v, back_hbm, sem.at[10])
-    save_back.start()
+    save_back = [
+        pltpu.make_async_copy(rows_v.at[partner(me, k, columns, 1)], back_hbm[k], sem.at[10 + columns + k])
+        for k in range(columns)
+    ]
+    for one in save_back:
+        one.start()
     small_k[...] = jnp.zeros_like(small_k)
     for c in range(blocks):
         for r in range(9):
@@ -378,27 +423,31 @@
     save_scaled.wait()
     save_vis.wait()
     save_hidden.wait()
-    save_back.wait()
-
-
-def run_block(chunk, side, live, x, up, weights, carried):
-    blocks, tiles, cells, lanes = x.shape
+    for one in save_back:
+        one.wait()
+
+
+def run_block(chunk, side, info, x, up, weights, carried):
+    columns = len(x)
+    tiles, cells, lanes = x[0].shape
+    blocks = columns
+    size = blocks * tiles * cells * lanes
     width = blocks * lanes
     narrow = weights[4].shape[1]
     whole = jax.ShapeDtypeStruct(up.shape, BF16)
-    fixed = [live, x, up, *weights]
+    fixed = [info, *x, up, *weights]
     field = pltpu.VMEM((blocks, tiles, cells, lanes), F32)
     packed = pltpu.VMEM((tiles, cells, width), BF16)
     eight = pltpu.VMEM((blocks, 8, lanes), F32)
     square = pltpu.VMEM((width, width), BF16)
     flops = 8 * tiles * cells * width * width
     return pl.pallas_call(
-        functools.partial(block_kernel, chunk, side),
-        in_specs=[SMEM] + [ANY] * 6 + [VMEM] * 6 + [ANY] * len(carried),
-        out_specs=[ANY] * 5 + [VMEM] * 3,
+        functools.partial(block_kernel, chunk, side, columns),
+        in_specs=[SMEM] + [ANY] * (columns + 5) + [VMEM] * 6 + [ANY] * len(carried),
+        out_specs=[ANY] * (4 + columns) + [VMEM] * 3,
         out_shape=[whole] * 4
+        + [jax.ShapeDtypeStruct((tiles, cells, lanes), BF16)] * columns
         + [
-            jax.ShapeDtypeStruct((blocks, tiles, cells, lanes), BF16),
             jax.ShapeDtypeStruct((2, 8, width), F32),
             jax.ShapeDtypeStruct((2, 8, narrow), F32),
             jax.ShapeDtypeStruct((16, width), F32),
@@ -431,63 +480,100 @@
                 packed,
                 packed,
             ],
-            pltpu.SemaphoreType.DMA((11,)),
+            pltpu.SemaphoreType.DMA((10 + 2 * columns,)),
         ],
         compiler_params=params(),
         cost_estimate=pl.CostEstimate(
-            flops=flops, bytes_accessed=8 * x.size * 2 + 8 * width * width, transcendentals=2 * x.size
+            flops=flops, bytes_accessed=16 * size + 8 * width * width, transcendentals=2 * size
         ),
         name="block_%d" % chunk,
     )(*fixed, *carried)
 
 
-def weights_kernel(normed, scaled, hidden, up, rest_ref, out):
-    count, cells, columns = normed.shape
+def weights_kernel(chunks, columns, info_ref, normed, scaled, hidden, up, *rest):
+    smalls, (home, away, held) = rest[: 5 * chunks], rest[5 * chunks :]
+    count, cells, wide = normed.shape
     flat = count * cells
     width = hidden.shape[2]
-
-    def product(left, right):
+    me = info_ref[1]
+    ring = columns // 2
+    made = []
+    for left, right in ((normed, hidden), (scaled, up)):
+        made.append(
+            lax.dot_general(
+                left[...].reshape(flat, wide),
+                right[...].reshape(flat, width),
+                (((0,), (0,)), ((), ())),
+                preferred_element_type=F32,
+            )
+        )
+
+    def outer(left, right):
         return lax.dot_general(
-            left[...].reshape(flat, columns),
-            right[...].reshape(flat, width),
-            (((0,), (0,)), ((), ())),
-            preferred_element_type=F32,
+            left, right, (((0,), (0,)), ((), ())), preferred_element_type=F32, precision=lax.Precision.HIGHEST
         )
 
-    for place, (left, right) in enumerate(((normed, hidden), (scaled, up))):
-        made = product(left, right).astype(BF16)
-        for group in range(2):
-            for z in range(4):
-                for core in range(2):
-                    row = 8 * (8 * group + 2 * z + core)
-                    out[core, z, group, :, place * width : (place + 1) * width] = made[row : row + 8]
-    out[:, :, :, :, 2 * width :] = rest_ref[...]
-
-
-def weight_terms(normed, scaled, hidden, up, others):
+    quarter = lax.rem(lax.broadcasted_iota(jnp.int32, (8, wide), 1), 4)
+    same = jnp.where(
+        lax.broadcasted_iota(jnp.int32, (16, wide), 0) == lax.broadcasted_iota(jnp.int32, (16, wide), 1), 1.0, 0.0
+    ).astype(F32)
+    down = lift = taps = None
+    for h in range(chunks):
+        squeeze, back_pre, back_squeeze_pre, act, terms = smalls[5 * h : 5 * h + 5]
+        narrow = back_squeeze_pre.shape[2]
+        one = outer(squeeze[0], back_squeeze_pre[0])
+        down = one if down is None else down + one
+        for m in range(4):
+            one = outer(
+                jnp.where(quarter == m, act[...], 0.0), back_pre[0, :, m * narrow : (m + 1) * narrow]
+            )
+            lift = one if lift is None else lift + one
+        one = outer(terms[...], same)
+        taps = one if taps is None else taps + one
+    place = 0
+    for value in (*made, down, lift, taps):
+        held[:, place : place + value.shape[1]] = value
+        place += value.shape[1]
+    for group in range(wide // (8 * columns)):
+        for k in range(columns):
+            row = pl.multiple_of(8 * (columns * group + partner(me, k, columns, 1)), 8)
+            target = home if k % 2 == 0 else away
+            target[k // 2, group] = held[pl.ds(row, 8), :].astype(BF16)
+
+
+def weight_terms(info, normed, scaled, hidden, up, small, columns):
     count, cells, width = normed.shape
-    columns = 128
-    lanes = 2 * width + others.shape[-1]
-    left = pl.BlockSpec((count, cells, columns), lambda i: (0, 0, i))
+    narrow = small[0][1].shape[2]
+    wide = LANES
+    lanes = 2 * width + 2 * narrow + wide
+    groups = width // (8 * columns)
+    per = wide // (8 * columns)
+    left = pl.BlockSpec((count, cells, wide), lambda i: (0, 0, i))
     right = pl.BlockSpec((count, cells, width), lambda i: (0, 0, 0), pipeline_mode=pl.Buffered(1))
+    args, specs = [], []
+    for a, b, k in small:
+        args += [a, a, b, jnp.repeat(b[1], 4, axis=1), k]
+        specs += [
+            pl.BlockSpec((1, 8, wide), lambda i: (0, 0, i)),
+            pl.BlockSpec((1, 8, width), lambda i: (1, 0, 0)),
+            pl.BlockSpec((1, 8, narrow), lambda i: (0, 0, 0)),
+            pl.BlockSpec((8, wide), lambda i: (0, i)),
+            pl.BlockSpec((16, wide), lambda i: (0, i)),
+        ]
+    part = jax.ShapeDtypeStruct((columns // 2, groups, 8, lanes), BF16)
     return pl.pallas_call(
-        weights_kernel,
-        grid=(width // columns,),
-        in_specs=[
-            left,
-            left,
-            right,
-            right,
-            pl.BlockSpec((2, 4, 2, 8, others.shape[-1]), lambda i: (0, 0, i, 0, 0)),
-        ],
-        out_specs=pl.BlockSpec((2, 4, 2, 8, lanes), lambda i: (0, 0, i, 0, 0)),
-        out_shape=jax.ShapeDtypeStruct((2, 4, 16, 8, lanes), BF16),
+        functools.partial(weights_kernel, len(small), columns),
+        grid=(width // wide,),
+        in_specs=[SMEM, left, left, right, right] + specs,
+        out_specs=[pl.BlockSpec((columns // 2, per, 8, lanes), lambda i: (0, i, 0, 0))] * 2,
+        out_shape=[part] * 2,
+        scratch_shapes=[pltpu.VMEM((wide, lanes), F32)],
         compiler_params=params(),
         cost_estimate=pl.CostEstimate(
             flops=4 * count * cells * width * width, bytes_accessed=8 * count * cells * width, transcendentals=0
         ),
         name="weight_terms",
-    )(normed, scaled, hidden, up, others)
+    )(info, normed, scaled, hidden, up, *args)
 
 
 def spread_kernel(per, own_ref, pos_ref, *rest):
@@ -603,7 +689,6 @@
     column_id = lax.axis_index("abs")
     local_tiles, grid = tiles.shape[0], tiles.shape[1]
     per, cells, width = token_grads.shape
-    narrow = se_down.shape[1]
     capacity = per * columns
     side = grid // 2
     slots = per // CHUNKS
@@ -612,7 +697,7 @@
         tile_counts, sample_owner, sample_rank, group_id, local_tiles, capacity
     )
     pos = slot % per
-    live = jnp.clip(filled - column_id * per, 0, per)
+    info = jnp.stack([filled[0], column_id.astype(jnp.int32), jnp.int32(per)])
     sends = pool_and_pack(tiles, own, pos, groups, slots)
 
     taps = jnp.pad(kernel.astype(F32).reshape(9, blocks, LANES).transpose(1, 0, 2), ((0, 0), (0, 7), (0, 0)))
@@ -625,59 +710,43 @@
         if h > 0:
             send, _ = lax.optimization_barrier((send, received))
         received = lax.all_to_all(send, "enc", split_axis=0, concat_axis=0, tiled=True)
-        compact = route(received, table, filled, h, per, columns, groups, False)
-        inner.append(lax.all_to_all(compact, "abs", split_axis=0, concat_axis=0, tiled=True))
+        if h == 0:
+            received, *weights = lax.optimization_barrier((received, *weights))
+        parts = route([received], table, info, h, per, columns, groups, False)
+        inner.append(exchange(parts))
 
     carried = []
     arrived, small = [], []
     for h in range(CHUNKS):
-        made = run_block(h, side, live, inner[h], token_grads, weights, carried)
+        made = run_block(h, side, info, inner[h], token_grads, weights, carried)
         carried = list(made[:4])
-        small.append(made[5:])
-        narrowed = lax.all_to_all(made[4], "abs", split_axis=0, concat_axis=0, tiled=True)
-        back = route(narrowed, table, filled, h, per, columns, groups, True)
+        small.append(made[4 + columns :])
+        narrowed = exchange(made[4 : 4 + columns])
+        back = route(narrowed, table, info, h, per, columns, groups, True)
         arrived.append(lax.all_to_all(back, "enc", split_axis=0, concat_axis=0, tiled=True))
     visual, normed, scaled, hidden = carried
     tile_grads = unpack_and_spread(arrived, own, pos, local_tiles, grid)
 
-    rows_a = jnp.concatenate([s[0] for s in small], axis=1)
-    rows_b = jnp.concatenate([s[1] for s in small], axis=1)
-    high = lax.Precision.HIGHEST
-    down = jnp.dot(rows_a[0].T, rows_b[0], precision=high)
-    up = jnp.dot(rows_b[1].T, rows_a[1], precision=high)
-    both = sum(s[2] for s in small)[:10]
-    devices = groups * columns
-    down = down.reshape(devices, 8, narrow)
-    up = up.reshape(devices, 8, narrow)
-    both = both.reshape(10, devices, 8).transpose(1, 2, 0)
-    both = jnp.pad(both, ((0, 0), (0, 0), (0, LANES - 10)))
-    others = jnp.concatenate([down, up, both], axis=2).astype(BF16)
-    others = others.reshape(groups, 4, 2, 8, -1).transpose(2, 1, 0, 3, 4)
-    terms = weight_terms(normed, scaled, hidden, token_grads, others)
-
-    core = column_id % 2
-    away = jnp.where(core == 0, terms[1], terms[0])
-    home = jnp.where(core == 0, terms[0], terms[1])
-    near = lax.ppermute(away, "abs", [(n, n ^ 1) for n in range(columns)])
-    pair = (home.astype(F32) + near.astype(F32)).astype(BF16)
-    ring = [[2 * z + c for z in range(4)] for c in range(2)]
-    column = lax.all_to_all(pair, "abs", split_axis=0, concat_axis=0, tiled=True, axis_index_groups=ring)
-    column = jnp.sum(column.astype(F32), axis=0).astype(BF16)
+    home, away = weight_terms(info, normed, scaled, hidden, token_grads, small, columns)
+    near = lax.ppermute(away, "abs", partner_pairs(1, columns))
+    pair = [(home[k].astype(F32) + near[k].astype(F32)).astype(BF16) for k in range(columns // 2)]
+    rows = [pair[0]] + [
+        lax.ppermute(pair[k], "abs", partner_pairs(2 * k, columns)) for k in range(1, columns // 2)
+    ]
+    column = sum(r.astype(F32) for r in rows).astype(BF16)
     spread = lax.all_to_all(column, "enc", split_axis=0, concat_axis=0, tiled=True)
     scale = 1.0 / math.sqrt(groups * local_tiles * cells)
     total = jnp.sum(spread.astype(F32), axis=0) * scale
-    w_in_grad = total[:, :width]
-    w_out_grad = total[:, width : 2 * width]
-    down_grad = total[:, 2 * width : 2 * width + narrow]
-    up_grad = total[:, 2 * width + narrow : 2 * width + 2 * narrow].reshape(2, width)
-    last = total[:, 2 * width + 2 * narrow : 2 * width + 2 * narrow + 10]
+    narrow = se_down.shape[1]
+    ends = [width, 2 * width, 2 * width + narrow, 2 * width + 2 * narrow]
+    last = total[:, ends[3] : ends[3] + 10]
     return (
         visual,
         tile_grads,
-        w_in_grad,
-        w_out_grad,
-        down_grad,
-        up_grad,
+        total[:, : ends[0]],
+        total[:, ends[0] : ends[1]],
+        total[:, ends[1] : ends[2]],
+        total[:, ends[2] : ends[3]].reshape(2, width),
         last[:, :9].T,
         last[:, 9],
     )

time: 508 us -> 333 us (0.66)
  starting transfers between devices: 123 us -> 72.2 us
  blocking collectives: 44.8 us -> 0 us
  waiting for transfers between devices: 146 us -> 103 us
  Pallas kernels: 132 us -> 114 us
  other arithmetic: 22.1 us -> 10.7 us
    all_to_all x2, starting transfers between devices: 89.2 us -> 14.7 us  [local(): lax.all_to_all(back, 'enc', split_axis=0, concat_axis=0, tiled=True)]
    all_to_all x2, waiting for transfers between devices: 77.6 us -> 5.89 us  [local(): lax.all_to_all(back, 'enc', split_axis=0, concat_axis=0, tiled=True)]
    ppermute x1 -> x32, waiting for transfers between devices: 0.01 us -> 60.8 us  [the longest x28 31.1 us: exchange(): lax.ppermute(parts[k], 'abs', partner_pairs(k, columns))]
    all_to_all x1 -> x0, blocking collectives: 44.8 us -> none  [local(): lax.all_to_all(send, 'enc', split_axis=0, concat_axis=0, tiled=True)]
    ppermute x1 -> x32, starting transfers between devices: 0.51 us -> 41.6 us  [the longest x28 36.8 us: exchange(): lax.ppermute(parts[k], 'abs', partner_pairs(k, columns))]
    all_to_all x5 -> x0, waiting for transfers between devices: 37.4 us -> none  [the longest x1 24 us: local(): lax.all_to_all(pair, 'abs', split_axis=0, concat_axis=0, tiled=True, axis...]
    all_to_all x5 -> x0, starting transfers between devices: 25.4 us -> none  [the longest x2 10.3 us: local(): lax.all_to_all(made[4], 'abs', split_axis=0, concat_axis=0, tiled=True)]
    pallas_call x7, Pallas kernels: 115 us -> 97.3 us  [the longest x2 57.4 us: run_block(): pl.pallas_call(functools.partial(block_kernel, chunk, side, columns), in_...]
  transfers between devices with their start and end apart: 10 -> 37, of which waited for: 7 -> 19; matrix products, arithmetic and copies ran while one was open for 9% -> 7% of each run, Pallas kernels for 25% -> 32%
where the time goes in v2:
time: 333 us; the launch traced here: 332 us
  Pallas kernels  114 us (34%)
  waiting for transfers between devices  103 us (31%)
  starting transfers between devices  72.2 us (22%)
  local copies, waits for them, and re-layouts  29.9 us (9%)
  other arithmetic  10.7 us (3%)
    pallas_call x2, Pallas kernels, run_block(): pl.pallas_call(functools.partial(block_kernel, chunk, side, columns), in_...  57.4 us
    ppermute x28, starting transfers between devices, exchange(): lax.ppermute(parts[k], 'abs', partner_pairs(k, columns))  36.8 us
    all_to_all x2, waiting for transfers between devices, local(): lax.all_to_all(send, 'enc', split_axis=0, concat_axis=0, tiled=True)  32.8 us
    ppermute x28, waiting for transfers between devices, exchange(): lax.ppermute(parts[k], 'abs', partner_pairs(k, columns))  31.1 us
    ppermute x3, waiting for transfers between devices, local(): lax.ppermute(pair[k], 'abs', partner_pairs(2 * k, columns))  29.7 us
    pallas_call x1, Pallas kernels, weight_terms(): pl.pallas_call(functools.partial(weights_kernel, len(small), columns), gr...  22.4 us
    unnamed x63, local copies, waits for them, and re-layouts  19.5 us
    pallas_call x4, Pallas kernels, route(): pl.pallas_call(functools.partial(body, chunk, slots, per, columns), in_sp...  17.5 us
  transfers between devices with their start and end apart: 37, of which 19 were waited for; matrix products, arithmetic and copies ran while one was open for 7% of the time, Pallas kernels for 32%

profile of v2, /device:TPU:0, one launch (start us, length us, event | category | flops | bytes accessed | tf_op | source)
XLA Modules:
  0.0 331.6 jit_solution(5904591236253026692)
XLA Ops:
  7.0 8.3 %pool_and_pack.1 = (bf16[16,5,144,128]{3,2,1,0:T(8,128)(2,1)}, bf16[16,5,144,128]{3,2,1,0:T(8,128)(2,1)}) custom-call(s32[48]{0:T(128)} %get-tuple-element.139.own_ref, s32[48]{0:T(128)} %and_select_fusion.pos_ref, bf16[48,24,24,128]{3,2,1,0:T(8,128)(2,1)} %tiles_ref.1), custom_call_target="tpu_custom_call" | custom-call | flops 3538944 | bytes 10616832 | tf_op jit(solution)/shard_map/pool_and_pack/pallas_call | solution.py:62
  15.4 7.3 %all-to-all-start = ((bf16[16,5,144,128]{3,2,1,0:T(8,128)(2,1)}), bf16[16,5,144,128]{3,2,1,0:T(8,128)(2,1)S(1)}, u32[]{:S(2)}, u32[]{:S(2)}) async-start(bf16[16,5,144,128]{3,2,1,0:T(8,128)(2,1)} %get-tuple-element.71), calls=%async_computation | async-start | bytes 5898240 | tf_op jit(solution)/shard_map/all_to_all | solution.py:712
  25.8 3.9 %copy.36 = bf16[1024,1024]{0,1:T(8,128)(2,1)} copy(bf16[1024,1024]{1,0:T(8,128)(2,1)} %rest_9_.1) | data formatting | bytes 4194304 | tf_op args[1]
  29.7 4.0 %copy.37 = bf16[1024,1024]{0,1:T(8,128)(2,1)} copy(bf16[1024,1024]{1,0:T(8,128)(2,1)} %rest_10_.1) | data formatting | bytes 4194304 | tf_op args[2]
  34.3 32.8 %all-to-all-done.src = bf16[16,5,144,128]{3,2,1,0:T(8,128)(2,1)S(1)} async-done(((bf16[16,5,144,128]{3,2,1,0:T(8,128)(2,1)}), bf16[16,5,144,128]{3,2,1,0:T(8,128)(2,1)S(1)}, u32[]{:S(2)}, u32[]{:S(2)}) %all-to-all-start) | async-done | bytes 2949152 | tf_op jit(solution)/shard_map/all_to_all | solution.py:712
  69.4 4.2 %all-to-all-start.1 = ((bf16[16,5,144,128]{3,2,1,0:T(8,128)(2,1)}), bf16[16,5,144,128]{3,2,1,0:T(8,128)(2,1)S(1)}, u32[]{:S(2)}, u32[]{:S(2)}) async-start(bf16[16,5,144,128]{3,2,1,0:T(8,128)(2,1)} %get-tuple-element.73), calls=%async_computation.1 | async-start | bytes 5898240 | tf_op jit(solution)/shard_map/all_to_all | solution.py:712
  76.3 5.5 %route_in.3 = (bf16[5,144,128]{2,1,0:T(8,128)(2,1)S(1)}, bf16[5,144,128]{2,1,0:T(8,128)(2,1)S(1)}, bf16[5,144,128]{2,1,0:T(8,128)(2,1)S(1)}, bf16[5,144,128]{2,1...) custom-call(s32[80]{0:T(128)S(1)} %select_reduce_fusion.7.table_ref,, ...), custom_call_target="tpu_custom_call" | custom-call | bytes 5898240 | tf_op jit(solution)/shard_map/route_in/pallas_call | solution.py:150
  92.9 2.7 collective-permute-done.9.rest_3_
  95.6 5.7 %collective-permute-done.10.rest_4_ = bf16[5,144,128]{2,1,0:T(8,128)(2,1)S(1)} collective-permute-done((bf16[5,144,128]{2,1,0:T(8,128)(2,1)S(1)}, bf16[5,144,128]{2,1,0:T(8,128)(2,1)S(1)}, u32[]{:S(2)}, u32[]{:S(2)}) %collective-permute-start.10) | collective-permute-done | bytes 184352 | tf_op jit(solution)/shard_map/ppermute | solution.py:92
  101.3 3.2 collective-permute-done.11.rest_5_
  105.9 28.7 %block_0.1 = (bf16[10,144,1024]{2,1,0:T(8,128)(2,1)}, bf16[10,144,1024]{2,1,0:T(8,128)(2,1)}, bf16[10,144,1024]{2,1,0:T(8,128)(2,1)}, bf16[10,144,1024]{2,1,0:T(...) custom-call(s32[3]{0:T(128)} %copy-done.5, ...), custom_call_target="tpu_custom_call" | custom-call | flops 6039797760 | bytes 20185088 | tf_op jit(solution)/shard_map/block_0/pallas_call | solution.py:444
  135.0 2.7 collective-permute-start.15
  141.9 5.0 %route_in.2 = (bf16[5,144,128]{2,1,0:T(8,128)(2,1)S(1)}, bf16[5,144,128]{2,1,0:T(8,128)(2,1)S(1)}, bf16[5,144,128]{2,1,0:T(8,128)(2,1)S(1)}, bf16[5,144,128]{2,1...) custom-call(s32[80]{0:T(128)S(1)} %select_reduce_fusion.7.table_ref,, ...), custom_call_target="tpu_custom_call" | custom-call | bytes 5898240 | tf_op jit(solution)/shard_map/route_in/pallas_call | solution.py:150
  147.6 2.6 collective-permute-start.19
  152.4 2.8 collective-permute-done.18.rest_5_
  163.5 3.2 route_back.2
  166.7 7.4 %all-to-all-start.2 = ((bf16[16,5,144,128]{3,2,1,0:T(8,128)(2,1)}), bf16[16,5,144,128]{3,2,1,0:T(8,128)(2,1)S(1)}, u32[]{:S(2)}, u32[]{:S(2)}) async-start(bf16[16,5,144,128]{3,2,1,0:T(8,128)(2,1)} %route_back.2), calls=%async_computation.2 | async-start | bytes 5898240 | tf_op jit(solution)/shard_map/all_to_all | solution.py:726
  175.8 28.7 %block_1.1 = (bf16[10,144,1024]{2,1,0:T(8,128)(2,1)}, bf16[10,144,1024]{2,1,0:T(8,128)(2,1)}, bf16[10,144,1024]{2,1,0:T(8,128)(2,1)}, bf16[10,144,1024]{2,1,0:T(...) custom-call(s32[3]{0:T(128)} %copy-done.5, ...), custom_call_target="tpu_custom_call", output_to_operand_aliasing={{0}: (20, {}), {1}: (21, {}), {2}: (22, {}), {3}: (23, {})} | custom-call | flops 6039797760 | bytes 20185088 | tf_op jit(solution)/shard_map/block_1/pallas_call | solution.py:444
  207.8 22.4 %weight_terms.1 = (bf16[4,16,8,2688]{3,2,1,0:T(8,128)(2,1)}, bf16[4,16,8,2688]{3,2,1,0:T(8,128)(2,1)}) custom-call(s32[3]{0:T(128)} %copy-done.5, bf16[10,144,1024]{2,1,0:T(8,128)(2,1)} %get-tuple-element.121.normed, bf16[10,144,1024]{2,1,0:T(8,128)(2,1)} %get-tuple-element.122.scaled, bf16[10,144,1024]{2,1,0:T(8,128)(2,1)} %get-tuple-element.123.hidden, ...), custom_call_target="tpu_custom_call" | custom-call | flops 6039797760 | bytes 11796480 | tf_op jit(solution)/shard_map/weight_terms/pallas_call | solution.py:564
  235.3 2.5 collective-permute-start.25
  242.3 3.0 collective-permute-start.27
  245.2 3.7 %collective-permute-done.24.rest_4_ = bf16[5,144,128]{2,1,0:T(8,128)(2,1)S(1)} collective-permute-done((bf16[5,144,128]{2,1,0:T(8,128)(2,1)}, bf16[5,144,128]{2,1,0:T(8,128)(2,1)S(1)}, u32[]{:S(2)}, u32[]{:S(2)}) %collective-permute-start.24) | collective-permute-done | bytes 184352 | tf_op jit(solution)/shard_map/ppermute | solution.py:92
  253.5 3.7 %route_back.3 = bf16[16,5,144,128]{3,2,1,0:T(8,128)(2,1)} custom-call(s32[80]{0:T(128)S(1)} %select_reduce_fusion.7.table_ref, s32[3]{0:T(128)S(1)} %copy-done.8, bf16[5,144,128]{2,1,0:T(8,128)(2,1)S(1)} %copy-done.4, bf16[5,144,128]{2,1,0:T(8,128)(2,1)S(1)} %collective-permute-done.21.rest_1_, bf16[5,144,128]{2,1,0:T(8,128)(2,1)S(1)} %collective-permute-done.22.rest_2_, ...), custom_call_target="tpu_custom_call" | custom-call | bytes 5898240 | tf_op jit(solution)/shard_map/route_back/pallas_call | solution.py:150
  258.9 7.2 %all-to-all-start.3 = ((bf16[16,5,144,128]{3,2,1,0:T(8,128)(2,1)}), bf16[16,5,144,128]{3,2,1,0:T(8,128)(2,1)}, u32[]{:S(2)}, u32[]{:S(2)}) async-start(bf16[16,5,144,128]{3,2,1,0:T(8,128)(2,1)} %route_back.3), calls=%async_computation.3 | async-start | bytes 5898240 | tf_op jit(solution)/shard_map/all_to_all | solution.py:726
  266.1 2.6 fusion.4
  273.3 14.0 %collective-permute-done.29 = bf16[16,8,2688]{2,1,0:T(8,128)(2,1)S(1)} collective-permute-done((bf16[16,8,2688]{2,1,0:T(8,128)(2,1)S(1)}, bf16[16,8,2688]{2,1,0:T(8,128)(2,1)S(1)}, u32[]{:S(2)}, u32[]{:S(2)}) %collective-permute-start.29) | collective-permute-done | bytes 688160 | tf_op jit(solution)/shard_map/ppermute | solution.py:734
  289.1 13.8 %collective-permute-done.30 = bf16[16,8,2688]{2,1,0:T(8,128)(2,1)S(1)} collective-permute-done((bf16[16,8,2688]{2,1,0:T(8,128)(2,1)S(1)}, bf16[16,8,2688]{2,1,0:T(8,128)(2,1)S(1)}, u32[]{:S(2)}, u32[]{:S(2)}) %collective-permute-start.30) | collective-permute-done | bytes 688160 | tf_op jit(solution)/shard_map/ppermute | solution.py:734
  303.0 2.6 fusion.2
  305.6 5.9 %all-to-all-done.3.rest_1_ = bf16[16,5,144,128]{3,2,1,0:T(8,128)(2,1)} async-done(((bf16[16,5,144,128]{3,2,1,0:T(8,128)(2,1)}), bf16[16,5,144,128]{3,2,1,0:T(8,128)(2,1)}, u32[]{:S(2)}, u32[]{:S(2)}) %all-to-all-start.3) | async-done | bytes 2949152 | tf_op jit(solution)/shard_map/all_to_all | solution.py:726
  311.5 4.4 %all-to-all-start.4 = ((bf16[16,8,2688]{2,1,0:T(8,128)(2,1)}), bf16[16,8,2688]{2,1,0:T(8,128)(2,1)S(1)}, u32[]{:S(2)}, u32[]{:S(2)}) async-start(bf16[16,8,2688]{2,1,0:T(8,128)(2,1)} %fusion.2), calls=%async_computation.4 | async-start | bytes 1376256 | tf_op jit(solution)/shard_map/all_to_all | solution.py:737
  315.9 8.5 %unpack_and_spread.1 = bf16[48,24,24,128]{3,2,1,0:T(8,128)(2,1)} custom-call(s32[48]{0:T(128)} %get-tuple-element.139.own_ref, s32[48]{0:T(128)} %and_select_fusion.pos_ref, bf16[16,5,144,128]{3,2,1,0:T(8,128)(2,1)} %copy-done.10, bf16[16,5,144,128]{3,2,1,0:T(8,128)(2,1)} %all-to-all-done.3.rest_1_), custom_call_target="tpu_custom_call" | custom-call | bytes 8847360 | tf_op jit(solution)/shard_map/unpack_and_spread/pallas_call | solution.py:617
  324.4 3.9 %all-to-all-done.4 = bf16[16,8,2688]{2,1,0:T(8,128)(2,1)S(1)} async-done(((bf16[16,8,2688]{2,1,0:T(8,128)(2,1)}), bf16[16,8,2688]{2,1,0:T(8,128)(2,1)S(1)}, u32[]{:S(2)}, u32[]{:S(2)}) %all-to-all-start.4) | async-done | bytes 688160 | tf_op jit(solution)/shard_map/all_to_all | solution.py:737
  (153 shorter events, 73.4 us)
Async XLA Ops:
  15.4 51.8 %all-to-all-start = ((bf16[16,5,144,128]{3,2,1,0:T(8,128)(2,1)}), bf16[16,5,144,128]{3,2,1,0:T(8,128)(2,1)S(1)}, u32[]{:S(2)}, u32[]{:S(2)}) async-start(bf16[16,5,144,128]{3,2,1,0:T(8,128)(2,1)} %get-tuple-element.71), calls=%async_computation | async-start | bytes 5898240 | tf_op jit(solution)/shard_map/all_to_all | solution.py:712
  69.4 71.8 %all-to-all-start.1 = ((bf16[16,5,144,128]{3,2,1,0:T(8,128)(2,1)}), bf16[16,5,144,128]{3,2,1,0:T(8,128)(2,1)S(1)}, u32[]{:S(2)}, u32[]{:S(2)}) async-start(bf16[16,5,144,128]{3,2,1,0:T(8,128)(2,1)} %get-tuple-element.73), calls=%async_computation.1 | async-start | bytes 5898240 | tf_op jit(solution)/shard_map/all_to_all | solution.py:712
  82.5 9.5 %collective-permute-start.8 = (bf16[5,144,128]{2,1,0:T(8,128)(2,1)S(1)}, bf16[5,144,128]{2,1,0:T(8,128)(2,1)S(1)}, u32[]{:S(2)}, u32[]{:S(2)}) collective-permute-start(bf16[5,144,128]{2,1,0:T(8,128)(2,1)S(1)} %get-tuple-element.94), channel_id=1, source_target_pairs={{0,2},{1,3},{2,4},{3,5},{4,6},{5,7},{6,0},{7,1},{8,10},{9,11},{10,... | collective-permute-start | bytes 552968 | tf_op jit(solution)/shard_map/ppermute | solution.py:92
  84.4 11.2 %collective-permute-start.9 = (bf16[5,144,128]{2,1,0:T(8,128)(2,1)S(1)}, bf16[5,144,128]{2,1,0:T(8,128)(2,1)S(1)}, u32[]{:S(2)}, u32[]{:S(2)}) collective-permute-start(bf16[5,144,128]{2,1,0:T(8,128)(2,1)S(1)} %get-tuple-element.95), channel_id=1, source_target_pairs={{0,3},{1,2},{2,5},{3,4},{4,7},{5,6},{6,1},{7,0},{8,11},{9,10},{10,... | collective-permute-start | bytes 552968 | tf_op jit(solution)/shard_map/ppermute | solution.py:92
  86.2 15.1 %collective-permute-start.10 = (bf16[5,144,128]{2,1,0:T(8,128)(2,1)S(1)}, bf16[5,144,128]{2,1,0:T(8,128)(2,1)S(1)}, u32[]{:S(2)}, u32[]{:S(2)}) collective-permute-start(bf16[5,144,128]{2,1,0:T(8,128)(2,1)S(1)} %get-tuple-element.96), channel_id=1, source_target_pairs={{0,4},{1,5},{2,6},{3,7},{4,0},{5,1},{6,2},{7,3},{8,12},{9,13},{10,... | collective-permute-start | bytes 552968 | tf_op jit(solution)/shard_map/ppermute | solution.py:92
  88.2 16.3 %collective-permute-start.11 = (bf16[5,144,128]{2,1,0:T(8,128)(2,1)S(1)}, bf16[5,144,128]{2,1,0:T(8,128)(2,1)S(1)}, u32[]{:S(2)}, u32[]{:S(2)}) collective-permute-start(bf16[5,144,128]{2,1,0:T(8,128)(2,1)S(1)} %get-tuple-element.97), channel_id=1, source_target_pairs={{0,5},{1,4},{2,7},{3,6},{4,1},{5,0},{6,3},{7,2},{8,13},{9,12},{10,... | collective-permute-start | bytes 552968 | tf_op jit(solution)/shard_map/ppermute | solution.py:92
  89.3 15.2 %collective-permute-start.12 = (bf16[5,144,128]{2,1,0:T(8,128)(2,1)S(1)}, bf16[5,144,128]{2,1,0:T(8,128)(2,1)S(1)}, u32[]{:S(2)}, u32[]{:S(2)}) collective-permute-start(bf16[5,144,128]{2,1,0:T(8,128)(2,1)S(1)} %get-tuple-element.98), channel_id=1, source_target_pairs={{0,6},{1,7},{2,0},{3,1},{4,2},{5,3},{6,4},{7,5},{8,14},{9,15},{10,... | collective-permute-start | bytes 552968 | tf_op jit(solution)/shard_map/ppermute | solution.py:92
  92.0 12.5 %collective-permute-start.13 = (bf16[5,144,128]{2,1,0:T(8,128)(2,1)S(1)}, bf16[5,144,128]{2,1,0:T(8,128)(2,1)S(1)}, u32[]{:S(2)}, u32[]{:S(2)}) collective-permute-start(bf16[5,144,128]{2,1,0:T(8,128)(2,1)S(1)} %get-tuple-element.99), channel_id=1, source_target_pairs={{0,7},{1,6},{2,1},{3,0},{4,3},{5,2},{6,5},{7,4},{8,15},{9,14},{10,... | collective-permute-start | bytes 552968 | tf_op jit(solution)/shard_map/ppermute | solution.py:92
  134.7 12.9 %collective-permute-start.14 = (bf16[5,144,128]{2,1,0:T(8,128)(2,1)}, bf16[5,144,128]{2,1,0:T(8,128)(2,1)S(1)}, u32[]{:S(2)}, u32[]{:S(2)}) collective-permute-start(bf16[5,144,128]{2,1,0:T(8,128)(2,1)} %get-tuple-element.106), channel_id=1, source_target_pairs={{0,1},{1,0},{2,3},{3,2},{4,5},{5,4},{6,7},{7,6},{8,9},{9,8},{10,11... | collective-permute-start | bytes 552968 | tf_op jit(solution)/shard_map/ppermute | solution.py:92
  135.0 15.2 %collective-permute-start.15 = (bf16[5,144,128]{2,1,0:T(8,128)(2,1)}, bf16[5,144,128]{2,1,0:T(8,128)(2,1)S(1)}, u32[]{:S(2)}, u32[]{:S(2)}) collective-permute-start(bf16[5,144,128]{2,1,0:T(8,128)(2,1)} %get-tuple-element.107), channel_id=1, source_target_pairs={{0,2},{1,3},{2,4},{3,5},{4,6},{5,7},{6,0},{7,1},{8,10},{9,11},{10,... | collective-permute-start | bytes 552968 | tf_op jit(solution)/shard_map/ppermute | solution.py:92
  137.6 12.6 %collective-permute-start.16 = (bf16[5,144,128]{2,1,0:T(8,128)(2,1)}, bf16[5,144,128]{2,1,0:T(8,128)(2,1)}, u32[]{:S(2)}, u32[]{:S(2)}) collective-permute-start(bf16[5,144,128]{2,1,0:T(8,128)(2,1)} %get-tuple-element.108), channel_id=1, source_target_pairs={{0,3},{1,2},{2,5},{3,4},{4,7},{5,6},{6,1},{7,0},{8,11},{9,10},{10,... | collective-permute-start | bytes 552968 | tf_op jit(solution)/shard_map/ppermute | solution.py:92
  137.6 14.8 %collective-permute-start.17 = (bf16[5,144,128]{2,1,0:T(8,128)(2,1)}, bf16[5,144,128]{2,1,0:T(8,128)(2,1)}, u32[]{:S(2)}, u32[]{:S(2)}) collective-permute-start(bf16[5,144,128]{2,1,0:T(8,128)(2,1)} %get-tuple-element.109), channel_id=1, source_target_pairs={{0,4},{1,5},{2,6},{3,7},{4,0},{5,1},{6,2},{7,3},{8,12},{9,13},{10,... | collective-permute-start | bytes 552968 | tf_op jit(solution)/shard_map/ppermute | solution.py:92
  139.3 16.0 %collective-permute-start.18 = (bf16[5,144,128]{2,1,0:T(8,128)(2,1)}, bf16[5,144,128]{2,1,0:T(8,128)(2,1)}, u32[]{:S(2)}, u32[]{:S(2)}) collective-permute-start(bf16[5,144,128]{2,1,0:T(8,128)(2,1)} %get-tuple-element.110), channel_id=1, source_target_pairs={{0,5},{1,4},{2,7},{3,6},{4,1},{5,0},{6,3},{7,2},{8,13},{9,12},{10,... | collective-permute-start | bytes 552968 | tf_op jit(solution)/shard_map/ppermute | solution.py:92
  150.2 10.2 %collective-permute-start = (bf16[5,144,128]{2,1,0:T(8,128)(2,1)S(1)}, bf16[5,144,128]{2,1,0:T(8,128)(2,1)S(1)}, u32[]{:S(2)}, u32[]{:S(2)}) collective-permute-start(bf16[5,144,128]{2,1,0:T(8,128)(2,1)S(1)} %get-tuple-element.75), channel_id=1, source_target_pairs={{0,1},{1,0},{2,3},{3,2},{4,5},{5,4},{6,7},{7,6},{8,9},{9,8},{10,11... | collective-permute-start | bytes 552968 | tf_op jit(solution)/shard_map/ppermute | solution.py:92
  152.4 9.3 %collective-permute-start.1 = (bf16[5,144,128]{2,1,0:T(8,128)(2,1)S(1)}, bf16[5,144,128]{2,1,0:T(8,128)(2,1)S(1)}, u32[]{:S(2)}, u32[]{:S(2)}) collective-permute-start(bf16[5,144,128]{2,1,0:T(8,128)(2,1)S(1)} %get-tuple-element.76), channel_id=1, source_target_pairs={{0,2},{1,3},{2,4},{3,5},{4,6},{5,7},{6,0},{7,1},{8,10},{9,11},{10,... | collective-permute-start | bytes 552968 | tf_op jit(solution)/shard_map/ppermute | solution.py:92
  155.2 18.9 %collective-permute-start.2 = (bf16[5,144,128]{2,1,0:T(8,128)(2,1)}, bf16[5,144,128]{2,1,0:T(8,128)(2,1)}, u32[]{:S(2)}, u32[]{:S(2)}) collective-permute-start(bf16[5,144,128]{2,1,0:T(8,128)(2,1)} %get-tuple-element.77), channel_id=1, source_target_pairs={{0,3},{1,2},{2,5},{3,4},{4,7},{5,6},{6,1},{7,0},{8,11},{9,10},{10,... | collective-permute-start | bytes 552968 | tf_op jit(solution)/shard_map/ppermute | solution.py:92
  155.2 18.9 %collective-permute-start.3 = (bf16[5,144,128]{2,1,0:T(8,128)(2,1)}, bf16[5,144,128]{2,1,0:T(8,128)(2,1)}, u32[]{:S(2)}, u32[]{:S(2)}) collective-permute-start(bf16[5,144,128]{2,1,0:T(8,128)(2,1)} %get-tuple-element.78), channel_id=1, source_target_pairs={{0,4},{1,5},{2,6},{3,7},{4,0},{5,1},{6,2},{7,3},{8,12},{9,13},{10,... | collective-permute-start | bytes 552968 | tf_op jit(solution)/shard_map/ppermute | solution.py:92
  158.5 15.6 %collective-permute-start.4 = (bf16[5,144,128]{2,1,0:T(8,128)(2,1)}, bf16[5,144,128]{2,1,0:T(8,128)(2,1)}, u32[]{:S(2)}, u32[]{:S(2)}) collective-permute-start(bf16[5,144,128]{2,1,0:T(8,128)(2,1)} %get-tuple-element.79), channel_id=1, source_target_pairs={{0,5},{1,4},{2,7},{3,6},{4,1},{5,0},{6,3},{7,2},{8,13},{9,12},{10,... | collective-permute-start | bytes 552968 | tf_op jit(solution)/shard_map/ppermute | solution.py:92
  160.5 13.7 %collective-permute-start.5 = (bf16[5,144,128]{2,1,0:T(8,128)(2,1)}, bf16[5,144,128]{2,1,0:T(8,128)(2,1)}, u32[]{:S(2)}, u32[]{:S(2)}) collective-permute-start(bf16[5,144,128]{2,1,0:T(8,128)(2,1)} %get-tuple-element.80), channel_id=1, source_target_pairs={{0,6},{1,7},{2,0},{3,1},{4,2},{5,3},{6,4},{7,5},{8,14},{9,15},{10,... | collective-permute-start | bytes 552968 | tf_op jit(solution)/shard_map/ppermute | solution.py:92
  161.8 14.0 %collective-permute-start.6 = (bf16[5,144,128]{2,1,0:T(8,128)(2,1)}, bf16[5,144,128]{2,1,0:T(8,128)(2,1)}, u32[]{:S(2)}, u32[]{:S(2)}) collective-permute-start(bf16[5,144,128]{2,1,0:T(8,128)(2,1)} %get-tuple-element.81), channel_id=1, source_target_pairs={{0,7},{1,6},{2,1},{3,0},{4,3},{5,2},{6,5},{7,4},{8,15},{9,14},{10,... | collective-permute-start | bytes 552968 | tf_op jit(solution)/shard_map/ppermute | solution.py:92
  166.7 90.6 %all-to-all-start.2 = ((bf16[16,5,144,128]{3,2,1,0:T(8,128)(2,1)}), bf16[16,5,144,128]{3,2,1,0:T(8,128)(2,1)S(1)}, u32[]{:S(2)}, u32[]{:S(2)}) async-start(bf16[16,5,144,128]{3,2,1,0:T(8,128)(2,1)} %route_back.2), calls=%async_computation.2 | async-start | bytes 5898240 | tf_op jit(solution)/shard_map/all_to_all | solution.py:726
  230.3 35.8 %collective-permute-start.28 = (bf16[4,16,8,2688]{3,2,1,0:T(8,128)(2,1)}, bf16[4,16,8,2688]{3,2,1,0:T(8,128)(2,1)}, u32[]{:S(2)}, u32[]{:S(2)}) collective-permute-start(bf16[4,16,8,2688]{3,2,1,0:T(8,128)(2,1)} %get-tuple-element.131), channel_id=1, source_target_pairs={{0,1},{1,0},{2,3},{3,2},{4,5},{5,4},{6,7},{7,6},{8,9},{9,8},{10,11... | collective-permute-start | bytes 8257544 | tf_op jit(solution)/shard_map/ppermute | solution.py:731
  233.0 9.3 %collective-permute-start.23 = (bf16[5,144,128]{2,1,0:T(8,128)(2,1)}, bf16[5,144,128]{2,1,0:T(8,128)(2,1)S(1)}, u32[]{:S(2)}, u32[]{:S(2)}) collective-permute-start(bf16[5,144,128]{2,1,0:T(8,128)(2,1)} %get-tuple-element.116), channel_id=1, source_target_pairs={{0,3},{1,2},{2,5},{3,4},{4,7},{5,6},{6,1},{7,0},{8,11},{9,10},{10,... | collective-permute-start | bytes 552968 | tf_op jit(solution)/shard_map/ppermute | solution.py:92
  233.0 15.9 %collective-permute-start.24 = (bf16[5,144,128]{2,1,0:T(8,128)(2,1)}, bf16[5,144,128]{2,1,0:T(8,128)(2,1)S(1)}, u32[]{:S(2)}, u32[]{:S(2)}) collective-permute-start(bf16[5,144,128]{2,1,0:T(8,128)(2,1)} %get-tuple-element.117), channel_id=1, source_target_pairs={{0,4},{1,5},{2,6},{3,7},{4,0},{5,1},{6,2},{7,3},{8,12},{9,13},{10,... | collective-permute-start | bytes 552968 | tf_op jit(solution)/shard_map/ppermute | solution.py:92
  235.3 15.8 %collective-permute-start.25 = (bf16[5,144,128]{2,1,0:T(8,128)(2,1)S(1)}, bf16[5,144,128]{2,1,0:T(8,128)(2,1)S(1)}, u32[]{:S(2)}, u32[]{:S(2)}) collective-permute-start(bf16[5,144,128]{2,1,0:T(8,128)(2,1)S(1)} %copy-done.21), channel_id=1, source_target_pairs={{0,5},{1,4},{2,7},{3,6},{4,1},{5,0},{6,3},{7,2},{8,13},{9,12},{10,... | collective-permute-start | bytes 552968 | tf_op jit(solution)/shard_map/ppermute | solution.py:92
  239.7 11.4 %collective-permute-start.26 = (bf16[5,144,128]{2,1,0:T(8,128)(2,1)S(1)}, bf16[5,144,128]{2,1,0:T(8,128)(2,1)S(1)}, u32[]{:S(2)}, u32[]{:S(2)}) collective-permute-start(bf16[5,144,128]{2,1,0:T(8,128)(2,1)S(1)} %copy-done.19), channel_id=1, source_target_pairs={{0,6},{1,7},{2,0},{3,1},{4,2},{5,3},{6,4},{7,5},{8,14},{9,15},{10,... | collective-permute-start | bytes 552968 | tf_op jit(solution)/shard_map/ppermute | solution.py:92
  242.3 11.3 %collective-permute-start.27 = (bf16[5,144,128]{2,1,0:T(8,128)(2,1)S(1)}, bf16[5,144,128]{2,1,0:T(8,128)(2,1)S(1)}, u32[]{:S(2)}, u32[]{:S(2)}) collective-permute-start(bf16[5,144,128]{2,1,0:T(8,128)(2,1)S(1)} %copy-done.18), channel_id=1, source_target_pairs={{0,7},{1,6},{2,1},{3,0},{4,3},{5,2},{6,5},{7,4},{8,15},{9,14},{10,... | collective-permute-start | bytes 552968 | tf_op jit(solution)/shard_map/ppermute | solution.py:92
  258.9 52.6 %all-to-all-start.3 = ((bf16[16,5,144,128]{3,2,1,0:T(8,128)(2,1)}), bf16[16,5,144,128]{3,2,1,0:T(8,128)(2,1)}, u32[]{:S(2)}, u32[]{:S(2)}) async-start(bf16[16,5,144,128]{3,2,1,0:T(8,128)(2,1)} %route_back.3), calls=%async_computation.3 | async-start | bytes 5898240 | tf_op jit(solution)/shard_map/all_to_all | solution.py:726
  268.7 18.5 %collective-permute-start.29 = (bf16[16,8,2688]{2,1,0:T(8,128)(2,1)S(1)}, bf16[16,8,2688]{2,1,0:T(8,128)(2,1)S(1)}, u32[]{:S(2)}, u32[]{:S(2)}) collective-permute-start(bf16[16,8,2688]{2,1,0:T(8,128)(2,1)S(1)} %get-tuple-element.142), channel_id=1, source_target_pairs={{0,2},{1,3},{2,4},{3,5},{4,6},{5,7},{6,0},{7,1},{8,10},{9,11},{10,... | collective-permute-start | bytes 2064392 | tf_op jit(solution)/shard_map/ppermute | solution.py:734
  270.8 18.4 %collective-permute-start.31 = (bf16[16,8,2688]{2,1,0:T(8,128)(2,1)S(1)}, bf16[16,8,2688]{2,1,0:T(8,128)(2,1)S(1)}, u32[]{:S(2)}, u32[]{:S(2)}) collective-permute-start(bf16[16,8,2688]{2,1,0:T(8,128)(2,1)S(1)} %get-tuple-element.143), channel_id=1, source_target_pairs={{0,6},{1,7},{2,0},{3,1},{4,2},{5,3},{6,4},{7,5},{8,14},{9,15},{10,... | collective-permute-start | bytes 2064392 | tf_op jit(solution)/shard_map/ppermute | solution.py:734
  272.0 30.9 %collective-permute-start.30 = (bf16[16,8,2688]{2,1,0:T(8,128)(2,1)S(1)}, bf16[16,8,2688]{2,1,0:T(8,128)(2,1)S(1)}, u32[]{:S(2)}, u32[]{:S(2)}) collective-permute-start(bf16[16,8,2688]{2,1,0:T(8,128)(2,1)S(1)} %get-tuple-element.144), channel_id=1, source_target_pairs={{0,4},{1,5},{2,6},{3,7},{4,0},{5,1},{6,2},{7,3},{8,12},{9,13},{10,... | collective-permute-start | bytes 2064392 | tf_op jit(solution)/shard_map/ppermute | solution.py:734
  311.5 16.9 %all-to-all-start.4 = ((bf16[16,8,2688]{2,1,0:T(8,128)(2,1)}), bf16[16,8,2688]{2,1,0:T(8,128)(2,1)S(1)}, u32[]{:S(2)}, u32[]{:S(2)}) async-start(bf16[16,8,2688]{2,1,0:T(8,128)(2,1)} %fusion.2), calls=%async_computation.4 | async-start | bytes 1376256 | tf_op jit(solution)/shard_map/all_to_all | solution.py:737
  (34 other events, 413.4 us)

commit v3 on v2

--- a/solution.py
+++ b/solution.py
@@ -89,11 +89,19 @@
 
 def exchange(parts):
     columns = len(parts)
+    if columns == 1:
+        return [lax.all_to_all(parts[0], "abs", split_axis=0, concat_axis=0, tiled=True)]
     return [parts[0]] + [lax.ppermute(parts[k], "abs", partner_pairs(k, columns)) for k in range(1, columns)]
 
 
+def pick(refs, me, step, sign):
+    if len(refs) > 1:
+        return refs[step]
+    return refs[0].at[partner(me, step, refs[0].shape[0], sign)]
+
+
 def route_in_kernel(chunk, slots, per, columns, table_ref, info_ref, src, *rest):
-    outs, (held, sem, out_sem) = rest[:columns], rest[columns:]
+    outs, (held, sem, out_sem) = rest[:-3], rest[-3:]
     filled, me = info_ref[0], info_ref[1]
 
     def each(act):
@@ -110,7 +118,7 @@
 
     each(lambda one: one.start())
     each(lambda one: one.wait())
-    saves = [pltpu.make_async_copy(held.at[k], outs[k], out_sem.at[k]) for k in range(columns)]
+    saves = [pltpu.make_async_copy(held.at[k], pick(outs, me, k, 1), out_sem.at[k]) for k in range(columns)]
     for one in saves:
         one.start()
     for one in saves:
@@ -118,9 +126,9 @@
 
 
 def route_back_kernel(chunk, slots, per, columns, table_ref, info_ref, *rest):
-    srcs, (dst, held, sem, in_sem) = rest[:columns], rest[columns:]
+    srcs, (dst, held, sem, in_sem) = rest[:-4], rest[-4:]
     filled, me = info_ref[0], info_ref[1]
-    loads = [pltpu.make_async_copy(srcs[k], held.at[k], in_sem.at[k]) for k in range(columns)]
+    loads = [pltpu.make_async_copy(pick(srcs, me, k, -1), held.at[k], in_sem.at[k]) for k in range(columns)]
     for one in loads:
         one.start()
 
@@ -142,16 +150,22 @@
     each(lambda one: one.wait(), False)
 
 
-def route(sources, table, info, chunk, per, columns, groups, back):
+def parts_of(columns, shape, joined):
+    if joined:
+        return [jax.ShapeDtypeStruct((columns, *shape), BF16)]
+    return [jax.ShapeDtypeStruct(shape, BF16)] * columns
+
+
+def route(sources, table, info, chunk, per, columns, groups, back, joined=False):
     slots, cells, channels = sources[0].shape[-3:]
-    part = jax.ShapeDtypeStruct((slots, cells, channels), BF16)
+    parts = parts_of(columns, (slots, cells, channels), joined)
     whole = jax.ShapeDtypeStruct((groups, slots, cells, channels), BF16)
     body = route_back_kernel if back else route_in_kernel
     return pl.pallas_call(
         functools.partial(body, chunk, slots, per, columns),
         in_specs=[SMEM, SMEM] + [ANY] * len(sources),
-        out_specs=ANY if back else [ANY] * columns,
-        out_shape=whole if back else [part] * columns,
+        out_specs=ANY if back else [ANY] * len(parts),
+        out_shape=whole if back else parts,
         scratch_shapes=[
             pltpu.VMEM((columns, slots, cells, channels), BF16),
             pltpu.SemaphoreType.DMA,
@@ -180,15 +194,17 @@
     chunk,
     side,
     columns,
+    parts_in,
+    parts_out,
     info_ref,
     *rest,
 ):
-    x_hbm, rest = rest[:columns], rest[columns:]
+    x_hbm, rest = rest[:parts_in], rest[parts_in:]
     up_hbm, w_in_hbm, w_out_hbm, w_in_t_hbm, w_out_t_hbm = rest[:5]
     se_down, se_up, se_down_t, se_up_t, taps, gain = rest[5:11]
-    outs = rest[-24 - columns : -17]
-    (vis_hbm, normed_hbm, scaled_hbm, hidden_hbm), back_hbm = outs[:4], outs[4 : 4 + columns]
-    small_a, small_b, small_k = outs[4 + columns :]
+    outs = rest[-24 - parts_out : -17]
+    (vis_hbm, normed_hbm, scaled_hbm, hidden_hbm), back_hbm = outs[:4], outs[4 : 4 + parts_out]
+    small_a, small_b, small_k = outs[4 + parts_out :]
     filled, me = info_ref[0], info_ref[1]
     live = filled - me * info_ref[2]
     (
@@ -227,7 +243,8 @@
         )
     ]
     x_loads = [
-        pltpu.make_async_copy(x_hbm[k], x.at[partner(me, k, columns, -1)], sem.at[10 + k]) for k in range(columns)
+        pltpu.make_async_copy(pick(x_hbm, me, k, -1), x.at[partner(me, k, columns, -1)], sem.at[10 + k])
+        for k in range(columns)
     ]
     for one in x_loads + loads:
         one.start()
@@ -410,7 +427,7 @@
             rows_v[c, t] = made.astype(BF16)
 
     save_back = [
-        pltpu.make_async_copy(rows_v.at[partner(me, k, columns, 1)], back_hbm[k], sem.at[10 + columns + k])
+        pltpu.make_async_copy(rows_v.at[partner(me, k, columns, 1)], pick(back_hbm, me, k, 1), sem.at[10 + columns + k])
         for k in range(columns)
     ]
     for one in save_back:
@@ -427,10 +444,10 @@
         one.wait()
 
 
-def run_block(chunk, side, info, x, up, weights, carried):
-    columns = len(x)
-    tiles, cells, lanes = x[0].shape
-    blocks = columns
+def run_block(chunk, side, info, x, up, weights, carried, joined):
+    tiles, cells, lanes = x[0].shape[-3:]
+    blocks = columns = up.shape[-1] // lanes
+    backs = parts_of(columns, (tiles, cells, lanes), joined)
     size = blocks * tiles * cells * lanes
     width = blocks * lanes
     narrow = weights[4].shape[1]
@@ -442,11 +459,11 @@
     square = pltpu.VMEM((width, width), BF16)
     flops = 8 * tiles * cells * width * width
     return pl.pallas_call(
-        functools.partial(block_kernel, chunk, side, columns),
-        in_specs=[SMEM] + [ANY] * (columns + 5) + [VMEM] * 6 + [ANY] * len(carried),
-        out_specs=[ANY] * (4 + columns) + [VMEM] * 3,
+        functools.partial(block_kernel, chunk, side, columns, len(x), len(backs)),
+        in_specs=[SMEM] + [ANY] * (len(x) + 5) + [VMEM] * 6 + [ANY] * len(carried),
+        out_specs=[ANY] * (4 + len(backs)) + [VMEM] * 3,
         out_shape=[whole] * 4
-        + [jax.ShapeDtypeStruct((tiles, cells, lanes), BF16)] * columns
+        + backs
         + [
             jax.ShapeDtypeStruct((2, 8, width), F32),
             jax.ShapeDtypeStruct((2, 8, narrow), F32),
@@ -510,64 +527,67 @@
 
     def outer(left, right):
         return lax.dot_general(
-            left, right, (((0,), (0,)), ((), ())), preferred_element_type=F32, precision=lax.Precision.HIGHEST
+            jnp.concatenate(left, axis=0),
+            jnp.concatenate(right, axis=0),
+            (((0,), (0,)), ((), ())),
+            preferred_element_type=F32,
+            precision=lax.Precision.HIGHEST,
         )
 
     quarter = lax.rem(lax.broadcasted_iota(jnp.int32, (8, wide), 1), 4)
-    same = jnp.where(
-        lax.broadcasted_iota(jnp.int32, (16, wide), 0) == lax.broadcasted_iota(jnp.int32, (16, wide), 1), 1.0, 0.0
-    ).astype(F32)
-    down = lift = taps = None
-    for h in range(chunks):
-        squeeze, back_pre, back_squeeze_pre, act, terms = smalls[5 * h : 5 * h + 5]
-        narrow = back_squeeze_pre.shape[2]
-        one = outer(squeeze[0], back_squeeze_pre[0])
-        down = one if down is None else down + one
-        for m in range(4):
-            one = outer(
-                jnp.where(quarter == m, act[...], 0.0), back_pre[0, :, m * narrow : (m + 1) * narrow]
-            )
-            lift = one if lift is None else lift + one
-        one = outer(terms[...], same)
-        taps = one if taps is None else taps + one
+    pair = [lax.broadcasted_iota(jnp.int32, (16, LANES), n) for n in range(2)]
+    same = jnp.where(pair[0] == pair[1], 1.0, 0.0).astype(F32)
+    each = [smalls[5 * h : 5 * h + 5] for h in range(chunks)]
+    narrow = each[0][2].shape[2]
+    down = outer([e[0][0] for e in each], [e[2][0] for e in each])
+    lift = outer(
+        [jnp.where(quarter == m, e[3][...], 0.0) for e in each for m in range(4)],
+        [e[1][0, :, m * narrow : (m + 1) * narrow] for e in each for m in range(4)],
+    )
+    taps = outer([sum(e[4][...] for e in each)], [same])
     place = 0
     for value in (*made, down, lift, taps):
         held[:, place : place + value.shape[1]] = value
         place += value.shape[1]
-    for group in range(wide // (8 * columns)):
+    line = home.shape[1]
+    for step in range(line):
+        group = lax.rem(info_ref[4] + step, line)
         for k in range(columns):
             row = pl.multiple_of(8 * (columns * group + partner(me, k, columns, 1)), 8)
             target = home if k % 2 == 0 else away
-            target[k // 2, group] = held[pl.ds(row, 8), :].astype(BF16)
+            target[k // 2, step, 0] = held[pl.ds(row, 8), :].astype(BF16)
 
 
 def weight_terms(info, normed, scaled, hidden, up, small, columns):
     count, cells, width = normed.shape
     narrow = small[0][1].shape[2]
-    wide = LANES
-    lanes = 2 * width + 2 * narrow + wide
-    groups = width // (8 * columns)
-    per = wide // (8 * columns)
-    left = pl.BlockSpec((count, cells, wide), lambda i: (0, 0, i))
-    right = pl.BlockSpec((count, cells, width), lambda i: (0, 0, 0), pipeline_mode=pl.Buffered(1))
+    lanes = 2 * width + 2 * narrow + LANES
+    line = math.isqrt(width // (8 * columns))
+    wide = width // line
+    left = pl.BlockSpec((count, cells, wide), lambda i, s: (0, 0, i))
+    right = pl.BlockSpec((count, cells, width), lambda i, s: (0, 0, 0), pipeline_mode=pl.Buffered(1))
     args, specs = [], []
     for a, b, k in small:
         args += [a, a, b, jnp.repeat(b[1], 4, axis=1), k]
         specs += [
-            pl.BlockSpec((1, 8, wide), lambda i: (0, 0, i)),
-            pl.BlockSpec((1, 8, width), lambda i: (1, 0, 0)),
-            pl.BlockSpec((1, 8, narrow), lambda i: (0, 0, 0)),
-            pl.BlockSpec((8, wide), lambda i: (0, i)),
-            pl.BlockSpec((16, wide), lambda i: (0, i)),
+            pl.BlockSpec((1, 8, wide), lambda i, s: (0, 0, i)),
+            pl.BlockSpec((1, 8, width), lambda i, s: (1, 0, 0)),
+            pl.BlockSpec((1, 8, narrow), lambda i, s: (0, 0, 0)),
+            pl.BlockSpec((8, wide), lambda i, s: (0, i)),
+            pl.BlockSpec((16, wide), lambda i, s: (0, i)),
         ]
-    part = jax.ShapeDtypeStruct((columns // 2, groups, 8, lanes), BF16)
+    part = jax.ShapeDtypeStruct((columns // 2, line, line, 8, lanes), BF16)
+    out = pl.BlockSpec((columns // 2, line, 1, 8, lanes), lambda i, s: (0, 0, lax.rem(i - s[3] + line, line), 0, 0))
     return pl.pallas_call(
         functools.partial(weights_kernel, len(small), columns),
-        grid=(width // wide,),
-        in_specs=[SMEM, left, left, right, right] + specs,
-        out_specs=[pl.BlockSpec((columns // 2, per, 8, lanes), lambda i: (0, i, 0, 0))] * 2,
+        grid_spec=pltpu.PrefetchScalarGridSpec(
+            num_scalar_prefetch=1,
+            grid=(line,),
+            in_specs=[left, left, right, right] + specs,
+            out_specs=[out] * 2,
+            scratch_shapes=[pltpu.VMEM((wide, lanes), F32)],
+        ),
         out_shape=[part] * 2,
-        scratch_shapes=[pltpu.VMEM((wide, lanes), F32)],
         compiler_params=params(),
         cost_estimate=pl.CostEstimate(
             flops=4 * count * cells * width * width, bytes_accessed=8 * count * cells * width, transcendentals=0
@@ -697,7 +717,10 @@
         tile_counts, sample_owner, sample_rank, group_id, local_tiles, capacity
     )
     pos = slot % per
-    info = jnp.stack([filled[0], column_id.astype(jnp.int32), jnp.int32(per)])
+    line = math.isqrt(groups)
+    info = jnp.stack(
+        [filled[0], column_id.astype(jnp.int32), jnp.int32(per), group_id // line, lax.rem(group_id, line)]
+    )
     sends = pool_and_pack(tiles, own, pos, groups, slots)
 
     taps = jnp.pad(kernel.astype(F32).reshape(9, blocks, LANES).transpose(1, 0, 2), ((0, 0), (0, 7), (0, 0)))
@@ -712,31 +735,45 @@
         received = lax.all_to_all(send, "enc", split_axis=0, concat_axis=0, tiled=True)
         if h == 0:
             received, *weights = lax.optimization_barrier((received, *weights))
-        parts = route([received], table, info, h, per, columns, groups, False)
+        parts = route([received], table, info, h, per, columns, groups, False, h > 0)
+        if h > 0:
+            inner[-1], parts = lax.optimization_barrier((inner[-1], parts))
         inner.append(exchange(parts))
 
     carried = []
-    arrived, small = [], []
+    arrived, small, narrowed, backs = [], [], [], []
     for h in range(CHUNKS):
-        made = run_block(h, side, info, inner[h], token_grads, weights, carried)
+        made = run_block(h, side, info, inner[h], token_grads, weights, carried, h == 0)
         carried = list(made[:4])
-        small.append(made[4 + columns :])
-        narrowed = exchange(made[4 : 4 + columns])
-        back = route(narrowed, table, info, h, per, columns, groups, True)
+        small.append(made[-3:])
+        narrowed.append(exchange(made[4:-3]))
+    narrowed[0], carried = lax.optimization_barrier((narrowed[0], carried))
+    for h in range(CHUNKS):
+        back = route(narrowed[h], table, info, h, per, columns, groups, True)
+        if h == 0:
+            _, carried, narrowed[-1][1:4] = lax.optimization_barrier((back, carried, narrowed[-1][1:4]))
         arrived.append(lax.all_to_all(back, "enc", split_axis=0, concat_axis=0, tiled=True))
+    last = (back, arrived[0])
     visual, normed, scaled, hidden = carried
-    tile_grads = unpack_and_spread(arrived, own, pos, local_tiles, grid)
 
     home, away = weight_terms(info, normed, scaled, hidden, token_grads, small, columns)
+    home, (_, arrived[0]) = lax.optimization_barrier((home, last))
     near = lax.ppermute(away, "abs", partner_pairs(1, columns))
     pair = [(home[k].astype(F32) + near[k].astype(F32)).astype(BF16) for k in range(columns // 2)]
     rows = [pair[0]] + [
         lax.ppermute(pair[k], "abs", partner_pairs(2 * k, columns)) for k in range(1, columns // 2)
     ]
-    column = sum(r.astype(F32) for r in rows).astype(BF16)
-    spread = lax.all_to_all(column, "enc", split_axis=0, concat_axis=0, tiled=True)
-    scale = 1.0 / math.sqrt(groups * local_tiles * cells)
-    total = jnp.sum(spread.astype(F32), axis=0) * scale
+
+    def along(parts, pairs):
+        sent = [parts[0]] + [lax.ppermute(parts[k], "enc", pairs(k)) for k in range(1, line)]
+        return sum(r.astype(F32) for r in sent)
+
+    parts = [sum(r[k].astype(F32) for r in rows).astype(BF16) for k in range(line)]
+    row = along(parts, lambda k: [(n, n // line * line + (n + k) % line) for n in range(groups)])
+    parts = [row[k].astype(BF16) for k in range(line)]
+    total = along(parts, lambda k: [(n, (n + k * line) % groups) for n in range(groups)])
+    total = total * (1.0 / math.sqrt(groups * local_tiles * cells))
+    tile_grads = unpack_and_spread(arrived, own, pos, local_tiles, grid)
     narrow = se_down.shape[1]
     ends = [width, 2 * width, 2 * width + narrow, 2 * width + 2 * narrow]
     last = total[:, ends[3] : ends[3] + 10]

time: 333 us -> 332 us (level)
  waiting for transfers between devices: 103 us -> 123 us
  Pallas kernels: 114 us -> 103 us
  starting transfers between devices: 72.2 us -> 62.2 us
    all_to_all x2, waiting for transfers between devices: 32.8 us -> 55.8 us  [local(): lax.all_to_all(send, 'enc', split_axis=0, concat_axis=0, tiled=True)]
    ppermute x28 -> x14, starting transfers between devices: 36.8 us -> 18.6 us  [exchange(): lax.ppermute(parts[k], 'abs', partner_pairs(k, columns))]
    ppermute x0 -> x6, waiting for transfers between devices: none -> 17.9 us  [along(): lax.ppermute(parts[k], 'enc', pairs(k))]
    ppermute x28 -> x14, waiting for transfers between devices: 31.1 us -> 17.9 us  [exchange(): lax.ppermute(parts[k], 'abs', partner_pairs(k, columns))]
    ppermute x0 -> x6, starting transfers between devices: none -> 8.69 us  [along(): lax.ppermute(parts[k], 'enc', pairs(k))]
    pallas_call x1, Pallas kernels: 22.4 us -> 15.6 us  [weight_terms(): pl.pallas_call(functools.partial(weights_kernel, len(small), columns), gr...]
    all_to_all x1 -> x2, starting transfers between devices: 4.43 us -> 10.6 us  [exchange(): lax.all_to_all(parts[0], 'abs', split_axis=0, concat_axis=0, tiled=True)]
    all_to_all x2, starting transfers between devices: 14.7 us -> 8.78 us  [local(): lax.all_to_all(back, 'enc', split_axis=0, concat_axis=0, tiled=True)]
  transfers between devices with their start and end apart: 37 -> 30, of which waited for: 19 -> 15; matrix products, arithmetic and copies ran while one was open for 7% -> 6% of each run, Pallas kernels for 32% -> 28%
where the time goes in v3:
time: 332 us; the launch traced here: 330 us
  waiting for transfers between devices  123 us (37%)
  Pallas kernels  103 us (31%)
  starting transfers between devices  62.2 us (19%)
  local copies, waits for them, and re-layouts  29.1 us (9%)
  other arithmetic  11.7 us (4%)
    pallas_call x2, Pallas kernels, run_block(): pl.pallas_call(functools.partial(block_kernel, chunk, side, columns, len(...  56.8 us
    all_to_all x2, waiting for transfers between devices, local(): lax.all_to_all(send, 'enc', split_axis=0, concat_axis=0, tiled=True)  55.8 us
    ppermute x3, waiting for transfers between devices, local(): lax.ppermute(pair[k], 'abs', partner_pairs(2 * k, columns))  25.6 us
    ppermute x14, starting transfers between devices, exchange(): lax.ppermute(parts[k], 'abs', partner_pairs(k, columns))  18.6 us
    unnamed x49, local copies, waits for them, and re-layouts  18.6 us
    ppermute x14, waiting for transfers between devices, exchange(): lax.ppermute(parts[k], 'abs', partner_pairs(k, columns))  17.9 us
    ppermute x6, waiting for transfers between devices, along(): lax.ppermute(parts[k], 'enc', pairs(k))  17.9 us
    pallas_call x1, Pallas kernels, weight_terms(): pl.pallas_call(functools.partial(weights_kernel, len(small), columns), gr...  15.6 us
  transfers between devices with their start and end apart: 30, of which 15 were waited for; matrix products, arithmetic and copies ran while one was open for 6% of the time, Pallas kernels for 28%

profile of v3, /device:TPU:0, one launch (start us, length us, event | category | flops | bytes accessed | tf_op | source)
XLA Modules:
  0.0 330.3 jit_solution(14369131742117609359)
XLA Ops:
  7.1 8.3 %pool_and_pack.1 = (bf16[16,5,144,128]{3,2,1,0:T(8,128)(2,1)}, bf16[16,5,144,128]{3,2,1,0:T(8,128)(2,1)}) custom-call(s32[48]{0:T(128)} %get-tuple-element.155.own_ref, s32[48]{0:T(128)} %and_select_fusion.pos_ref, bf16[48,24,24,128]{3,2,1,0:T(8,128)(2,1)} %tiles_ref.1), custom_call_target="tpu_custom_call" | custom-call | flops 3538944 | bytes 10616832 | tf_op jit(solution)/shard_map/pool_and_pack/pallas_call | solution.py:62
  15.5 7.1 %all-to-all-start = ((bf16[16,5,144,128]{3,2,1,0:T(8,128)(2,1)}), bf16[16,5,144,128]{3,2,1,0:T(8,128)(2,1)S(1)}, u32[]{:S(2)}, u32[]{:S(2)}) async-start(bf16[16,5,144,128]{3,2,1,0:T(8,128)(2,1)} %get-tuple-element.78), calls=%async_computation | async-start | bytes 5898240 | tf_op jit(solution)/shard_map/all_to_all | solution.py:735
  22.6 3.9 %copy.36 = bf16[1024,1024]{0,1:T(8,128)(2,1)} copy(bf16[1024,1024]{1,0:T(8,128)(2,1)} %rest_2_) | data formatting | bytes 4194304 | tf_op args[1]
  26.5 4.0 %copy.37 = bf16[1024,1024]{0,1:T(8,128)(2,1)} copy(bf16[1024,1024]{1,0:T(8,128)(2,1)} %rest_3_) | data formatting | bytes 4194304 | tf_op args[2]
  34.3 32.8 %all-to-all-done.src = bf16[16,5,144,128]{3,2,1,0:T(8,128)(2,1)S(1)} async-done(((bf16[16,5,144,128]{3,2,1,0:T(8,128)(2,1)}), bf16[16,5,144,128]{3,2,1,0:T(8,128)(2,1)S(1)}, u32[]{:S(2)}, u32[]{:S(2)}) %all-to-all-start) | async-done | bytes 2949152 | tf_op jit(solution)/shard_map/all_to_all | solution.py:735
  69.3 4.2 %all-to-all-start.1 = ((bf16[16,5,144,128]{3,2,1,0:T(8,128)(2,1)}), bf16[16,5,144,128]{3,2,1,0:T(8,128)(2,1)S(1)}, u32[]{:S(2)}, u32[]{:S(2)}) async-start(bf16[16,5,144,128]{3,2,1,0:T(8,128)(2,1)} %get-tuple-element.89), calls=%async_computation.1 | async-start | bytes 5898240 | tf_op jit(solution)/shard_map/all_to_all | solution.py:735
  76.2 3.5 %route_in.2 = (bf16[5,144,128]{2,1,0:T(8,128)(2,1)S(1)}, bf16[5,144,128]{2,1,0:T(8,128)(2,1)S(1)}, bf16[5,144,128]{2,1,0:T(8,128)(2,1)S(1)}, bf16[5,144,128]{2,1...) custom-call(s32[80]{0:T(128)S(1)} %select_reduce_fusion.7.table_ref,, ...), custom_call_target="tpu_custom_call" | custom-call | bytes 5898240 | tf_op jit(solution)/shard_map/route_in/pallas_call | solution.py:164
  91.6 23.0 %all-to-all-done.1.src = bf16[16,5,144,128]{3,2,1,0:T(8,128)(2,1)S(1)} async-done(((bf16[16,5,144,128]{3,2,1,0:T(8,128)(2,1)}), bf16[16,5,144,128]{3,2,1,0:T(8,128)(2,1)S(1)}, u32[]{:S(2)}, u32[]{:S(2)}) %all-to-all-start.1) | async-done | bytes 2949152 | tf_op jit(solution)/shard_map/all_to_all | solution.py:735
  114.6 3.6 %route_in.3 = bf16[8,5,144,128]{3,2,1,0:T(8,128)(2,1)S(1)} custom-call(s32[80]{0:T(128)S(1)} %select_reduce_fusion.7.table_ref, s32[5]{0:T(128)S(1)} %stack.15.info_ref, bf16[16,5,144,128]{3,2,1,0:T(8,128)(2,1)S(1)} %all-to-all-done.1.src), custom_call_target="tpu_custom_call" | custom-call | bytes 5898240 | tf_op jit(solution)/shard_map/route_in/pallas_call | solution.py:164
  119.4 5.3 %all-to-all-start.3 = ((bf16[8,5,144,128]{3,2,1,0:T(8,128)(2,1)}), bf16[8,5,144,128]{3,2,1,0:T(8,128)(2,1)S(1)}, u32[]{:S(2)}, u32[]{:S(2)}) async-start(bf16[8,5,144,128]{3,2,1,0:T(8,128)(2,1)} %copy-done.2), calls=%async_computation.3 | async-start | bytes 2949120 | tf_op jit(solution)/shard_map/all_to_all | solution.py:93
  124.7 28.4 %block_0.1 = (bf16[10,144,1024]{2,1,0:T(8,128)(2,1)}, bf16[10,144,1024]{2,1,0:T(8,128)(2,1)}, bf16[10,144,1024]{2,1,0:T(8,128)(2,1)}, bf16[10,144,1024]{2,1,0:T(...) custom-call(s32[5]{0:T(128)} %copy-done.4, ...), custom_call_target="tpu_custom_call" | custom-call | flops 6039797760 | bytes 20185088 | tf_op jit(solution)/shard_map/block_0/pallas_call | solution.py:461
  153.1 5.3 %all-to-all-start.2 = ((bf16[8,5,144,128]{3,2,1,0:T(8,128)(2,1)}), bf16[8,5,144,128]{3,2,1,0:T(8,128)(2,1)S(1)}, u32[]{:S(2)}, u32[]{:S(2)}) async-start(bf16[8,5,144,128]{3,2,1,0:T(8,128)(2,1)} %get-tuple-element.108), calls=%async_computation.2 | async-start | bytes 2949120 | tf_op jit(solution)/shard_map/all_to_all | solution.py:93
  161.0 28.4 %block_1.1 = (bf16[10,144,1024]{2,1,0:T(8,128)(2,1)}, bf16[10,144,1024]{2,1,0:T(8,128)(2,1)}, bf16[10,144,1024]{2,1,0:T(8,128)(2,1)}, bf16[10,144,1024]{2,1,0:T(...) custom-call(s32[5]{0:T(128)} %copy-done.4, ...), custom_call_target="tpu_custom_call", output_to_operand_aliasing={{0}: (13, {}), {1}: (14, {}), {2}: (15, {}), {3}: (16, {})} | custom-call | flops 6039797760 | bytes 20185088 | tf_op jit(solution)/shard_map/block_1/pallas_call | solution.py:461
  189.5 3.4 %route_back.2 = bf16[16,5,144,128]{3,2,1,0:T(8,128)(2,1)} custom-call(s32[80]{0:T(128)S(1)} %select_reduce_fusion.7.table_ref, s32[5]{0:T(128)S(1)} %copy-done.5, bf16[8,5,144,128]{3,2,1,0:T(8,128)(2,1)S(1)} %all-to-all-done.2.rest_0_), custom_call_target="tpu_custom_call" | custom-call | bytes 5898240 | tf_op jit(solution)/shard_map/route_back/pallas_call | solution.py:164
  198.0 4.5 %all-to-all-start.4 = ((bf16[16,5,144,128]{3,2,1,0:T(8,128)(2,1)}), bf16[16,5,144,128]{3,2,1,0:T(8,128)(2,1)}, u32[]{:S(2)}, u32[]{:S(2)}) async-start(bf16[16,5,144,128]{3,2,1,0:T(8,128)(2,1)} %route_back.2), calls=%async_computation.4 | async-start | bytes 5898240 | tf_op jit(solution)/shard_map/all_to_all | solution.py:755
  202.6 3.3 %collective-permute-done.9.rest_3_ = bf16[5,144,128]{2,1,0:T(8,128)(2,1)S(1)} collective-permute-done((bf16[5,144,128]{2,1,0:T(8,128)(2,1)S(1)}, bf16[5,144,128]{2,1,0:T(8,128)(2,1)S(1)}, u32[]{:S(2)}, u32[]{:S(2)}) %collective-permute-start.9) | collective-permute-done | bytes 184352 | tf_op jit(solution)/shard_map/ppermute | solution.py:94
  205.9 15.6 %weight_terms.1 = (bf16[4,4,4,8,2688]{4,3,2,1,0:T(8,128)(2,1)}, bf16[4,4,4,8,2688]{4,3,2,1,0:T(8,128)(2,1)}) custom-call(s32[5]{0:T(128)} %copy-done.4, bf16[10,144,1024]{2,1,0:T(8,128)(2,1)} %get-tuple-element.127.normed, bf16[10,144,1024]{2,1,0:T(8,128)(2,1)} %get-tuple-element.128.scaled, bf16[10,144,1024]{2,1,0:T(8,128)(2,1)} %get-tuple-element.129.hidden, ...), custom_call_target="tpu_custom_call" | custom-call | flops 6039797760 | bytes 11796480 | tf_op jit(solution)/shard_map/weight_terms/pallas_call | solution.py:581
  227.2 3.7 %collective-permute-done.10.rest_4_ = bf16[5,144,128]{2,1,0:T(8,128)(2,1)S(1)} collective-permute-done((bf16[5,144,128]{2,1,0:T(8,128)(2,1)}, bf16[5,144,128]{2,1,0:T(8,128)(2,1)S(1)}, u32[]{:S(2)}, u32[]{:S(2)}) %collective-permute-start.10) | collective-permute-done | bytes 184352 | tf_op jit(solution)/shard_map/ppermute | solution.py:94
  231.0 2.8 collective-permute-done.11.rest_5_
  233.8 4.2 %collective-permute-done.12.rest_6_ = bf16[5,144,128]{2,1,0:T(8,128)(2,1)S(1)} collective-permute-done((bf16[5,144,128]{2,1,0:T(8,128)(2,1)}, bf16[5,144,128]{2,1,0:T(8,128)(2,1)S(1)}, u32[]{:S(2)}, u32[]{:S(2)}) %collective-permute-start.12) | collective-permute-done | bytes 184352 | tf_op jit(solution)/shard_map/ppermute | solution.py:94
  238.0 2.3 collective-permute-done.13.rest_7_
  240.3 3.2 route_back.3
  243.5 6.0 %all-to-all-done.4.rest_0_ = bf16[16,5,144,128]{3,2,1,0:T(8,128)(2,1)} async-done(((bf16[16,5,144,128]{3,2,1,0:T(8,128)(2,1)}), bf16[16,5,144,128]{3,2,1,0:T(8,128)(2,1)}, u32[]{:S(2)}, u32[]{:S(2)}) %all-to-all-start.4) | async-done | bytes 2949152 | tf_op jit(solution)/shard_map/all_to_all | solution.py:755
  249.5 3.7 %add_convert_fusion.3 = (bf16[1,4,4,8,2688]{4,3,2,1,0:T(8,128)(2,1)}, bf16[4,4,8,2688]{3,2,1,0:T(8,128)(2,1)}, bf16[4,4,8,2688]{3,2,1,0:T(8,128)(2,1)}, bf16[4,4,8,2688]{3,2,1,0:T(8,128)(2,1)}) fusion(bf16[4,4,4,8,2688]{4,3,2,1,0:T(8,128)(2,1)} %collective-permute-done.14, bf16[4,4,4,8,2688]{4,3,2,1,0:T(8,128)(2,1)S(1)} %copy-done.10), kind=kLoop, calls=%fused_computation.3 | loop fusion | flops 5505024 | bytes 8257536 | tf_op jit(solution)/shard_map/convert_element_type | solution.py:762
  257.2 4.3 %all-to-all-start.5 = ((bf16[16,5,144,128]{3,2,1,0:T(8,128)(2,1)}), bf16[16,5,144,128]{3,2,1,0:T(8,128)(2,1)S(1)}, u32[]{:S(2)}, u32[]{:S(2)}) async-start(bf16[16,5,144,128]{3,2,1,0:T(8,128)(2,1)} %route_back.3), calls=%async_computation.5 | async-start | bytes 5898240 | tf_op jit(solution)/shard_map/all_to_all | solution.py:755
  261.5 11.6 %collective-permute-done.15 = bf16[4,4,8,2688]{3,2,1,0:T(8,128)(2,1)} collective-permute-done((bf16[4,4,8,2688]{3,2,1,0:T(8,128)(2,1)}, bf16[4,4,8,2688]{3,2,1,0:T(8,128)(2,1)}, u32[]{:S(2)}, u32[]{:S(2)}) %collective-permute-start.15) | collective-permute-done | bytes 688160 | tf_op jit(solution)/shard_map/ppermute | solution.py:764
  273.1 13.4 %collective-permute-done.16 = bf16[4,4,8,2688]{3,2,1,0:T(8,128)(2,1)} collective-permute-done((bf16[4,4,8,2688]{3,2,1,0:T(8,128)(2,1)}, bf16[4,4,8,2688]{3,2,1,0:T(8,128)(2,1)}, u32[]{:S(2)}, u32[]{:S(2)}) %collective-permute-start.16) | collective-permute-done | bytes 688160 | tf_op jit(solution)/shard_map/ppermute | solution.py:764
  292.4 10.7 %collective-permute-done.18 = bf16[4,8,2688]{2,1,0:T(8,128)(2,1)S(1)} collective-permute-done((bf16[4,8,2688]{2,1,0:T(8,128)(2,1)S(1)}, bf16[4,8,2688]{2,1,0:T(8,128)(2,1)S(1)}, u32[]{:S(2)}, u32[]{:S(2)}) %collective-permute-start.18) | collective-permute-done | bytes 172064 | tf_op jit(solution)/shard_map/ppermute | solution.py:768
  303.1 7.1 %collective-permute-done.19 = bf16[4,8,2688]{2,1,0:T(8,128)(2,1)S(1)} collective-permute-done((bf16[4,8,2688]{2,1,0:T(8,128)(2,1)S(1)}, bf16[4,8,2688]{2,1,0:T(8,128)(2,1)S(1)}, u32[]{:S(2)}, u32[]{:S(2)}) %collective-permute-start.19) | collective-permute-done | bytes 172064 | tf_op jit(solution)/shard_map/ppermute | solution.py:768
  311.9 2.7 collective-permute-start.22
  314.6 2.4 collective-permute-start.23
  318.6 8.5 %unpack_and_spread.1 = bf16[48,24,24,128]{3,2,1,0:T(8,128)(2,1)} custom-call(s32[48]{0:T(128)} %get-tuple-element.155.own_ref, s32[48]{0:T(128)} %and_select_fusion.pos_ref, bf16[16,5,144,128]{3,2,1,0:T(8,128)(2,1)} %all-to-all-done.4.rest_0_, bf16[16,5,144,128]{3,2,1,0:T(8,128)(2,1)} %copy-done.8), custom_call_target="tpu_custom_call" | custom-call | bytes 8847360 | tf_op jit(solution)/shard_map/unpack_and_spread/pallas_call | solution.py:637
  (126 shorter events, 57.7 us)
Async XLA Ops:
  15.5 51.6 %all-to-all-start = ((bf16[16,5,144,128]{3,2,1,0:T(8,128)(2,1)}), bf16[16,5,144,128]{3,2,1,0:T(8,128)(2,1)S(1)}, u32[]{:S(2)}, u32[]{:S(2)}) async-start(bf16[16,5,144,128]{3,2,1,0:T(8,128)(2,1)} %get-tuple-element.78), calls=%async_computation | async-start | bytes 5898240 | tf_op jit(solution)/shard_map/all_to_all | solution.py:735
  69.3 45.3 %all-to-all-start.1 = ((bf16[16,5,144,128]{3,2,1,0:T(8,128)(2,1)}), bf16[16,5,144,128]{3,2,1,0:T(8,128)(2,1)S(1)}, u32[]{:S(2)}, u32[]{:S(2)}) async-start(bf16[16,5,144,128]{3,2,1,0:T(8,128)(2,1)} %get-tuple-element.89), calls=%async_computation.1 | async-start | bytes 5898240 | tf_op jit(solution)/shard_map/all_to_all | solution.py:735
  74.3 43.9 %copy-start.4 = (s32[5]{0:T(128)}, s32[5]{0:T(128)S(1)}, u32[]{:S(2)}) copy-start(s32[5]{0:T(128)S(1)} %stack.15.info_ref) | copy-start | bytes 64
  80.4 6.8 %collective-permute-start = (bf16[5,144,128]{2,1,0:T(8,128)(2,1)S(1)}, bf16[5,144,128]{2,1,0:T(8,128)(2,1)S(1)}, u32[]{:S(2)}, u32[]{:S(2)}) collective-permute-start(bf16[5,144,128]{2,1,0:T(8,128)(2,1)S(1)} %get-tuple-element.81), channel_id=1, source_target_pairs={{0,1},{1,0},{2,3},{3,2},{4,5},{5,4},{6,7},{7,6},{8,9},{9,8},{10,11... | collective-permute-start | bytes 552968 | tf_op jit(solution)/shard_map/ppermute | solution.py:94
  80.4 9.5 %collective-permute-start.1 = (bf16[5,144,128]{2,1,0:T(8,128)(2,1)S(1)}, bf16[5,144,128]{2,1,0:T(8,128)(2,1)S(1)}, u32[]{:S(2)}, u32[]{:S(2)}) collective-permute-start(bf16[5,144,128]{2,1,0:T(8,128)(2,1)S(1)} %get-tuple-element.82), channel_id=1, source_target_pairs={{0,2},{1,3},{2,4},{3,5},{4,6},{5,7},{6,0},{7,1},{8,10},{9,11},{10,... | collective-permute-start | bytes 552968 | tf_op jit(solution)/shard_map/ppermute | solution.py:94
  82.3 37.0 %collective-permute-start.2 = (bf16[5,144,128]{2,1,0:T(8,128)(2,1)}, bf16[5,144,128]{2,1,0:T(8,128)(2,1)}, u32[]{:S(2)}, u32[]{:S(2)}) collective-permute-start(bf16[5,144,128]{2,1,0:T(8,128)(2,1)} %get-tuple-element.83), channel_id=1, source_target_pairs={{0,3},{1,2},{2,5},{3,4},{4,7},{5,6},{6,1},{7,0},{8,11},{9,10},{10,... | collective-permute-start | bytes 552968 | tf_op jit(solution)/shard_map/ppermute | solution.py:94
  84.1 35.3 %collective-permute-start.3 = (bf16[5,144,128]{2,1,0:T(8,128)(2,1)}, bf16[5,144,128]{2,1,0:T(8,128)(2,1)}, u32[]{:S(2)}, u32[]{:S(2)}) collective-permute-start(bf16[5,144,128]{2,1,0:T(8,128)(2,1)} %get-tuple-element.84), channel_id=1, source_target_pairs={{0,4},{1,5},{2,6},{3,7},{4,0},{5,1},{6,2},{7,3},{8,12},{9,13},{10,... | collective-permute-start | bytes 552968 | tf_op jit(solution)/shard_map/ppermute | solution.py:94
  86.0 33.3 %collective-permute-start.4 = (bf16[5,144,128]{2,1,0:T(8,128)(2,1)S(1)}, bf16[5,144,128]{2,1,0:T(8,128)(2,1)}, u32[]{:S(2)}, u32[]{:S(2)}) collective-permute-start(bf16[5,144,128]{2,1,0:T(8,128)(2,1)S(1)} %get-tuple-element.85), channel_id=1, source_target_pairs={{0,5},{1,4},{2,7},{3,6},{4,1},{5,0},{6,3},{7,2},{8,13},{9,12},{10,... | collective-permute-start | bytes 552968 | tf_op jit(solution)/shard_map/ppermute | solution.py:94
  87.2 32.2 %collective-permute-start.5 = (bf16[5,144,128]{2,1,0:T(8,128)(2,1)S(1)}, bf16[5,144,128]{2,1,0:T(8,128)(2,1)}, u32[]{:S(2)}, u32[]{:S(2)}) collective-permute-start(bf16[5,144,128]{2,1,0:T(8,128)(2,1)S(1)} %get-tuple-element.86), channel_id=1, source_target_pairs={{0,6},{1,7},{2,0},{3,1},{4,2},{5,3},{6,4},{7,5},{8,14},{9,15},{10,... | collective-permute-start | bytes 552968 | tf_op jit(solution)/shard_map/ppermute | solution.py:94
  90.6 28.8 %collective-permute-start.6 = (bf16[5,144,128]{2,1,0:T(8,128)(2,1)S(1)}, bf16[5,144,128]{2,1,0:T(8,128)(2,1)}, u32[]{:S(2)}, u32[]{:S(2)}) collective-permute-start(bf16[5,144,128]{2,1,0:T(8,128)(2,1)S(1)} %get-tuple-element.87), channel_id=1, source_target_pairs={{0,7},{1,6},{2,1},{3,0},{4,3},{5,2},{6,5},{7,4},{8,15},{9,14},{10,... | collective-permute-start | bytes 552968 | tf_op jit(solution)/shard_map/ppermute | solution.py:94
  119.4 33.7 %all-to-all-start.3 = ((bf16[8,5,144,128]{3,2,1,0:T(8,128)(2,1)}), bf16[8,5,144,128]{3,2,1,0:T(8,128)(2,1)S(1)}, u32[]{:S(2)}, u32[]{:S(2)}) async-start(bf16[8,5,144,128]{3,2,1,0:T(8,128)(2,1)} %copy-done.2), calls=%async_computation.3 | async-start | bytes 2949120 | tf_op jit(solution)/shard_map/all_to_all | solution.py:93
  153.1 36.3 %all-to-all-start.2 = ((bf16[8,5,144,128]{3,2,1,0:T(8,128)(2,1)}), bf16[8,5,144,128]{3,2,1,0:T(8,128)(2,1)S(1)}, u32[]{:S(2)}, u32[]{:S(2)}) async-start(bf16[8,5,144,128]{3,2,1,0:T(8,128)(2,1)} %get-tuple-element.108), calls=%async_computation.2 | async-start | bytes 2949120 | tf_op jit(solution)/shard_map/all_to_all | solution.py:93
  192.9 9.5 %collective-permute-start.7 = (bf16[5,144,128]{2,1,0:T(8,128)(2,1)S(1)}, bf16[5,144,128]{2,1,0:T(8,128)(2,1)S(1)}, u32[]{:S(2)}, u32[]{:S(2)}) collective-permute-start(bf16[5,144,128]{2,1,0:T(8,128)(2,1)S(1)} %copy-done.21), channel_id=1, source_target_pairs={{0,1},{1,0},{2,3},{3,2},{4,5},{5,4},{6,7},{7,6},{8,9},{9,8},{10,11... | collective-permute-start | bytes 552968 | tf_op jit(solution)/shard_map/ppermute | solution.py:94
  193.9 8.6 %collective-permute-start.8 = (bf16[5,144,128]{2,1,0:T(8,128)(2,1)S(1)}, bf16[5,144,128]{2,1,0:T(8,128)(2,1)S(1)}, u32[]{:S(2)}, u32[]{:S(2)}) collective-permute-start(bf16[5,144,128]{2,1,0:T(8,128)(2,1)S(1)} %copy-done.20), channel_id=1, source_target_pairs={{0,2},{1,3},{2,4},{3,5},{4,6},{5,7},{6,0},{7,1},{8,10},{9,11},{10,... | collective-permute-start | bytes 552968 | tf_op jit(solution)/shard_map/ppermute | solution.py:94
  195.7 10.2 %collective-permute-start.9 = (bf16[5,144,128]{2,1,0:T(8,128)(2,1)S(1)}, bf16[5,144,128]{2,1,0:T(8,128)(2,1)S(1)}, u32[]{:S(2)}, u32[]{:S(2)}) collective-permute-start(bf16[5,144,128]{2,1,0:T(8,128)(2,1)S(1)} %copy-done.19), channel_id=1, source_target_pairs={{0,3},{1,2},{2,5},{3,4},{4,7},{5,6},{6,1},{7,0},{8,11},{9,10},{10,... | collective-permute-start | bytes 552968 | tf_op jit(solution)/shard_map/ppermute | solution.py:94
  198.0 51.6 %all-to-all-start.4 = ((bf16[16,5,144,128]{3,2,1,0:T(8,128)(2,1)}), bf16[16,5,144,128]{3,2,1,0:T(8,128)(2,1)}, u32[]{:S(2)}, u32[]{:S(2)}) async-start(bf16[16,5,144,128]{3,2,1,0:T(8,128)(2,1)} %route_back.2), calls=%async_computation.4 | async-start | bytes 5898240 | tf_op jit(solution)/shard_map/all_to_all | solution.py:755
  205.9 34.4 %copy-start.6 = (s32[5]{0:T(128)S(1)}, s32[5]{0:T(128)}, u32[]{:S(2)}) copy-start(s32[5]{0:T(128)} %copy-done.4) | copy-start | bytes 64
  221.6 28.0 %collective-permute-start.14 = (bf16[4,4,4,8,2688]{4,3,2,1,0:T(8,128)(2,1)}, bf16[4,4,4,8,2688]{4,3,2,1,0:T(8,128)(2,1)}, u32[]{:S(2)}, u32[]{:S(2)}) collective-permute-start(bf16[4,4,4,8,2688]{4,3,2,1,0:T(8,128)(2,1)} %get-tuple-element.147), channel_id=1, source_target_pairs={{0,1},{1,0},{2,3},{3,2},{4,5},{5,4},{6,7},{7,6},{8,9},{9,8},{10,11... | collective-permute-start | bytes 8257544 | tf_op jit(solution)/shard_map/ppermute | solution.py:761
  221.8 9.2 %collective-permute-start.10 = (bf16[5,144,128]{2,1,0:T(8,128)(2,1)}, bf16[5,144,128]{2,1,0:T(8,128)(2,1)S(1)}, u32[]{:S(2)}, u32[]{:S(2)}) collective-permute-start(bf16[5,144,128]{2,1,0:T(8,128)(2,1)} %get-tuple-element.141), channel_id=1, source_target_pairs={{0,4},{1,5},{2,6},{3,7},{4,0},{5,1},{6,2},{7,3},{8,12},{9,13},{10,... | collective-permute-start | bytes 552968 | tf_op jit(solution)/shard_map/ppermute | solution.py:94
  223.7 10.1 %collective-permute-start.11 = (bf16[5,144,128]{2,1,0:T(8,128)(2,1)}, bf16[5,144,128]{2,1,0:T(8,128)(2,1)S(1)}, u32[]{:S(2)}, u32[]{:S(2)}) collective-permute-start(bf16[5,144,128]{2,1,0:T(8,128)(2,1)} %get-tuple-element.142), channel_id=1, source_target_pairs={{0,5},{1,4},{2,7},{3,6},{4,1},{5,0},{6,3},{7,2},{8,13},{9,12},{10,... | collective-permute-start | bytes 552968 | tf_op jit(solution)/shard_map/ppermute | solution.py:94
  225.0 13.0 %collective-permute-start.12 = (bf16[5,144,128]{2,1,0:T(8,128)(2,1)}, bf16[5,144,128]{2,1,0:T(8,128)(2,1)S(1)}, u32[]{:S(2)}, u32[]{:S(2)}) collective-permute-start(bf16[5,144,128]{2,1,0:T(8,128)(2,1)} %get-tuple-element.143), channel_id=1, source_target_pairs={{0,6},{1,7},{2,0},{3,1},{4,2},{5,3},{6,4},{7,5},{8,14},{9,15},{10,... | collective-permute-start | bytes 552968 | tf_op jit(solution)/shard_map/ppermute | solution.py:94
  226.5 13.8 %collective-permute-start.13 = (bf16[5,144,128]{2,1,0:T(8,128)(2,1)S(1)}, bf16[5,144,128]{2,1,0:T(8,128)(2,1)S(1)}, u32[]{:S(2)}, u32[]{:S(2)}) collective-permute-start(bf16[5,144,128]{2,1,0:T(8,128)(2,1)S(1)} %copy-done.16), channel_id=1, source_target_pairs={{0,7},{1,6},{2,1},{3,0},{4,3},{5,2},{6,5},{7,4},{8,15},{9,14},{10,... | collective-permute-start | bytes 552968 | tf_op jit(solution)/shard_map/ppermute | solution.py:94
  253.3 19.9 %collective-permute-start.15 = (bf16[4,4,8,2688]{3,2,1,0:T(8,128)(2,1)}, bf16[4,4,8,2688]{3,2,1,0:T(8,128)(2,1)}, u32[]{:S(2)}, u32[]{:S(2)}) collective-permute-start(bf16[4,4,8,2688]{3,2,1,0:T(8,128)(2,1)} %get-tuple-element.161), channel_id=1, source_target_pairs={{0,2},{1,3},{2,4},{3,5},{4,6},{5,7},{6,0},{7,1},{8,10},{9,11},{10,... | collective-permute-start | bytes 2064392 | tf_op jit(solution)/shard_map/ppermute | solution.py:764
  254.6 32.0 %collective-permute-start.16 = (bf16[4,4,8,2688]{3,2,1,0:T(8,128)(2,1)}, bf16[4,4,8,2688]{3,2,1,0:T(8,128)(2,1)}, u32[]{:S(2)}, u32[]{:S(2)}) collective-permute-start(bf16[4,4,8,2688]{3,2,1,0:T(8,128)(2,1)} %get-tuple-element.160), channel_id=1, source_target_pairs={{0,4},{1,5},{2,6},{3,7},{4,0},{5,1},{6,2},{7,3},{8,12},{9,13},{10,... | collective-permute-start | bytes 2064392 | tf_op jit(solution)/shard_map/ppermute | solution.py:764
  256.5 30.7 %collective-permute-start.17 = (bf16[4,4,8,2688]{3,2,1,0:T(8,128)(2,1)}, bf16[4,4,8,2688]{3,2,1,0:T(8,128)(2,1)}, u32[]{:S(2)}, u32[]{:S(2)}) collective-permute-start(bf16[4,4,8,2688]{3,2,1,0:T(8,128)(2,1)} %get-tuple-element.159), channel_id=1, source_target_pairs={{0,6},{1,7},{2,0},{3,1},{4,2},{5,3},{6,4},{7,5},{8,14},{9,15},{10,... | collective-permute-start | bytes 2064392 | tf_op jit(solution)/shard_map/ppermute | solution.py:764
  257.2 59.7 %all-to-all-start.5 = ((bf16[16,5,144,128]{3,2,1,0:T(8,128)(2,1)}), bf16[16,5,144,128]{3,2,1,0:T(8,128)(2,1)S(1)}, u32[]{:S(2)}, u32[]{:S(2)}) async-start(bf16[16,5,144,128]{3,2,1,0:T(8,128)(2,1)} %route_back.3), calls=%async_computation.5 | async-start | bytes 5898240 | tf_op jit(solution)/shard_map/all_to_all | solution.py:755
  289.0 14.0 %collective-permute-start.18 = (bf16[4,8,2688]{2,1,0:T(8,128)(2,1)S(1)}, bf16[4,8,2688]{2,1,0:T(8,128)(2,1)S(1)}, u32[]{:S(2)}, u32[]{:S(2)}) collective-permute-start(bf16[4,8,2688]{2,1,0:T(8,128)(2,1)S(1)} %get-tuple-element.162), channel_id=1, source_target_pairs={{0,8},{8,16},{16,24},{24,0},{32,40},{40,48},{48,56},{56,32},{64,72... | collective-permute-start | bytes 516104 | tf_op jit(solution)/shard_map/ppermute | solution.py:768
  289.1 21.1 %collective-permute-start.19 = (bf16[4,8,2688]{2,1,0:T(8,128)(2,1)S(1)}, bf16[4,8,2688]{2,1,0:T(8,128)(2,1)S(1)}, u32[]{:S(2)}, u32[]{:S(2)}) collective-permute-start(bf16[4,8,2688]{2,1,0:T(8,128)(2,1)S(1)} %get-tuple-element.164), channel_id=1, source_target_pairs={{0,16},{8,24},{16,0},{24,8},{32,48},{40,56},{48,32},{56,40},{64,80... | collective-permute-start | bytes 516104 | tf_op jit(solution)/shard_map/ppermute | solution.py:768
  291.1 19.1 %collective-permute-start.20 = (bf16[4,8,2688]{2,1,0:T(8,128)(2,1)S(1)}, bf16[4,8,2688]{2,1,0:T(8,128)(2,1)S(1)}, u32[]{:S(2)}, u32[]{:S(2)}) collective-permute-start(bf16[4,8,2688]{2,1,0:T(8,128)(2,1)S(1)} %get-tuple-element.163), channel_id=1, source_target_pairs={{0,24},{8,0},{16,8},{24,16},{32,56},{40,32},{48,40},{56,48},{64,88... | collective-permute-start | bytes 516104 | tf_op jit(solution)/shard_map/ppermute | solution.py:768
  311.6 15.5 %collective-permute-start.21 = (bf16[8,2688]{1,0:T(8,128)(2,1)S(1)}, bf16[8,2688]{1,0:T(8,128)(2,1)S(1)}, u32[]{:S(2)}, u32[]{:S(2)}) collective-permute-start(bf16[8,2688]{1,0:T(8,128)(2,1)S(1)} %get-tuple-element.165), channel_id=1, source_target_pairs={{0,32},{8,40},{16,48},{24,56},{32,64},{40,72},{48,80},{56,88},{64,... | collective-permute-start | bytes 129032 | tf_op jit(solution)/shard_map/ppermute | solution.py:768
  311.9 15.2 %collective-permute-start.22 = (bf16[8,2688]{1,0:T(8,128)(2,1)S(1)}, bf16[8,2688]{1,0:T(8,128)(2,1)S(1)}, u32[]{:S(2)}, u32[]{:S(2)}) collective-permute-start(bf16[8,2688]{1,0:T(8,128)(2,1)S(1)} %get-tuple-element.167), channel_id=1, source_target_pairs={{0,64},{8,72},{16,80},{24,88},{32,96},{40,104},{48,112},{56,120},{... | collective-permute-start | bytes 129032 | tf_op jit(solution)/shard_map/ppermute | solution.py:768
  314.6 12.5 %collective-permute-start.23 = (bf16[8,2688]{1,0:T(8,128)(2,1)S(1)}, bf16[8,2688]{1,0:T(8,128)(2,1)S(1)}, u32[]{:S(2)}, u32[]{:S(2)}) collective-permute-start(bf16[8,2688]{1,0:T(8,128)(2,1)S(1)} %get-tuple-element.166), channel_id=1, source_target_pairs={{0,96},{8,104},{16,112},{24,120},{32,0},{40,8},{48,16},{56,24},{64... | collective-permute-start | bytes 129032 | tf_op jit(solution)/shard_map/ppermute | solution.py:768
  (20 other events, 175.5 us)

commit v4 on v3

--- a/solution.py
+++ b/solution.py
@@ -100,54 +100,30 @@
     return refs[0].at[partner(me, step, refs[0].shape[0], sign)]
 
 
-def route_in_kernel(chunk, slots, per, columns, table_ref, info_ref, src, *rest):
-    outs, (held, sem, out_sem) = rest[:-3], rest[-3:]
+def route_kernel(chunk, per, columns, back, table_ref, info_ref, *rest):
+    (srcs, outs) = (rest[:-2], rest[-2:-1]) if back else (rest[:1], rest[1:-1])
+    sem = rest[-1]
     filled, me = info_ref[0], info_ref[1]
+    whole = outs[0] if back else srcs[0]
+    slots = whole.shape[1]
 
     def each(act):
         for k in range(columns):
-            first = partner(me, k, columns, 1) * per + chunk * slots
+            first = partner(me, k, columns, -1 if back else 1) * per + chunk * slots
+            part = pick(srcs, me, k, -1) if back else pick(outs, me, k, 1)
 
             @pl.loop(0, slots)
-            def _(local, k=k, first=first):
+            def _(local, part=part, first=first):
                 q = first + local
 
                 @pl.when(q < filled)
                 def _():
-                    act(pltpu.make_async_copy(src.at[table_ref[q], local], held.at[k, local], sem))
+                    there = whole.at[table_ref[q], local]
+                    here = part.at[local]
+                    act(pltpu.make_async_copy(*((here, there) if back else (there, here)), sem))
 
     each(lambda one: one.start())
     each(lambda one: one.wait())
-    saves = [pltpu.make_async_copy(held.at[k], pick(outs, me, k, 1), out_sem.at[k]) for k in range(columns)]
-    for one in saves:
-        one.start()
-    for one in saves:
-        one.wait()
-
-
-def route_back_kernel(chunk, slots, per, columns, table_ref, info_ref, *rest):
-    srcs, (dst, held, sem, in_sem) = rest[:-4], rest[-4:]
-    filled, me = info_ref[0], info_ref[1]
-    loads = [pltpu.make_async_copy(pick(srcs, me, k, -1), held.at[k], in_sem.at[k]) for k in range(columns)]
-    for one in loads:
-        one.start()
-
-    def each(act, ready):
-        for k in range(columns):
-            first = partner(me, k, columns, -1) * per + chunk * slots
-            if ready:
-                loads[k].wait()
-
-            @pl.loop(0, slots)
-            def _(local, k=k, first=first):
-                q = first + local
-
-                @pl.when(q < filled)
-                def _():
-                    act(pltpu.make_async_copy(held.at[k, local], dst.at[table_ref[q], local], sem))
-
-    each(lambda one: one.start(), True)
-    each(lambda one: one.wait(), False)
 
 
 def parts_of(columns, shape, joined):
@@ -160,18 +136,13 @@
     slots, cells, channels = sources[0].shape[-3:]
     parts = parts_of(columns, (slots, cells, channels), joined)
     whole = jax.ShapeDtypeStruct((groups, slots, cells, channels), BF16)
-    body = route_back_kernel if back else route_in_kernel
     return pl.pallas_call(
-        functools.partial(body, chunk, slots, per, columns),
-        in_specs=[SMEM, SMEM] + [ANY] * len(sources),
+        functools.partial(route_kernel, chunk, per, columns, back),
+        in_specs=[SMEM, SMEM] + [VMEM] * len(sources),
         out_specs=ANY if back else [ANY] * len(parts),
         out_shape=whole if back else parts,
-        scratch_shapes=[
-            pltpu.VMEM((columns, slots, cells, channels), BF16),
-            pltpu.SemaphoreType.DMA,
-            pltpu.SemaphoreType.DMA((columns,)),
-        ],
-        compiler_params=pltpu.CompilerParams(vmem_limit_bytes=8 * 1024 * 1024),
+        scratch_shapes=[pltpu.SemaphoreType.DMA],
+        compiler_params=pltpu.CompilerParams(vmem_limit_bytes=16 * 1024 * 1024),
         cost_estimate=pl.CostEstimate(
             flops=0, bytes_accessed=8 * columns * slots * cells * channels, transcendentals=0
         ),
@@ -549,45 +520,40 @@
     for value in (*made, down, lift, taps):
         held[:, place : place + value.shape[1]] = value
         place += value.shape[1]
-    line = home.shape[1]
-    for step in range(line):
-        group = lax.rem(info_ref[4] + step, line)
+    for group in range(wide // (8 * columns)):
         for k in range(columns):
             row = pl.multiple_of(8 * (columns * group + partner(me, k, columns, 1)), 8)
             target = home if k % 2 == 0 else away
-            target[k // 2, step, 0] = held[pl.ds(row, 8), :].astype(BF16)
+            target[k // 2, group] = held[pl.ds(row, 8), :].astype(BF16)
 
 
 def weight_terms(info, normed, scaled, hidden, up, small, columns):
     count, cells, width = normed.shape
     narrow = small[0][1].shape[2]
+    wide = 2 * LANES
     lanes = 2 * width + 2 * narrow + LANES
-    line = math.isqrt(width // (8 * columns))
-    wide = width // line
-    left = pl.BlockSpec((count, cells, wide), lambda i, s: (0, 0, i))
-    right = pl.BlockSpec((count, cells, width), lambda i, s: (0, 0, 0), pipeline_mode=pl.Buffered(1))
+    groups = width // (8 * columns)
+    per = wide // (8 * columns)
+    left = pl.BlockSpec((count, cells, wide), lambda i: (0, 0, i))
+    right = pl.BlockSpec((count, cells, width), lambda i: (0, 0, 0), pipeline_mode=pl.Buffered(1))
     args, specs = [], []
     for a, b, k in small:
         args += [a, a, b, jnp.repeat(b[1], 4, axis=1), k]
         specs += [
-            pl.BlockSpec((1, 8, wide), lambda i, s: (0, 0, i)),
-            pl.BlockSpec((1, 8, width), lambda i, s: (1, 0, 0)),
-            pl.BlockSpec((1, 8, narrow), lambda i, s: (0, 0, 0)),
-            pl.BlockSpec((8, wide), lambda i, s: (0, i)),
-            pl.BlockSpec((16, wide), lambda i, s: (0, i)),
+            pl.BlockSpec((1, 8, wide), lambda i: (0, 0, i)),
+            pl.BlockSpec((1, 8, width), lambda i: (1, 0, 0)),
+            pl.BlockSpec((1, 8, narrow), lambda i: (0, 0, 0)),
+            pl.BlockSpec((8, wide), lambda i: (0, i)),
+            pl.BlockSpec((16, wide), lambda i: (0, i)),
         ]
-    part = jax.ShapeDtypeStruct((columns // 2, line, line, 8, lanes), BF16)
-    out = pl.BlockSpec((columns // 2, line, 1, 8, lanes), lambda i, s: (0, 0, lax.rem(i - s[3] + line, line), 0, 0))
+    part = jax.ShapeDtypeStruct((columns // 2, groups, 8, lanes), BF16)
     return pl.pallas_call(
         functools.partial(weights_kernel, len(small), columns),
-        grid_spec=pltpu.PrefetchScalarGridSpec(
-            num_scalar_prefetch=1,
-            grid=(line,),
-            in_specs=[left, left, right, right] + specs,
-            out_specs=[out] * 2,
-            scratch_shapes=[pltpu.VMEM((wide, lanes), F32)],
-        ),
+        grid=(width // wide,),
+        in_specs=[SMEM, left, left, right, right] + specs,
+        out_specs=[pl.BlockSpec((columns // 2, per, 8, lanes), lambda i: (0, i, 0, 0))] * 2,
         out_shape=[part] * 2,
+        scratch_shapes=[pltpu.VMEM((wide, lanes), F32)],
         compiler_params=params(),
         cost_estimate=pl.CostEstimate(
             flops=4 * count * cells * width * width, bytes_accessed=8 * count * cells * width, transcendentals=0
@@ -597,36 +563,23 @@
 
 
 def spread_kernel(per, own_ref, pos_ref, *rest):
-    arrived, out, (held, wide, sem) = rest[:CHUNKS], rest[CHUNKS], rest[CHUNKS + 1 :]
+    arrived, (out, wide) = rest[:CHUNKS], rest[CHUNKS:]
     step = pl.program_id(0)
     slots = arrived[0].shape[1]
-    count = held.shape[0]
     side = out.shape[1] // 2
     width = 2 * side
-
-    @pl.when(step == 0)
-    def _():
-        @pl.loop(0, count)
-        def _(j):
-            position = pos_ref[j]
-            for h in range(CHUNKS):
-
-                @pl.when(position // slots == h)
-                def _(h=h):
-                    pltpu.make_async_copy(
-                        arrived[h].at[own_ref[j], position - h * slots], held.at[j], sem
-                    ).start()
-
-        @pl.loop(0, count)
-        def _(j):
-            pltpu.make_async_copy(arrived[0].at[0, 0], held.at[0], sem).wait()
-
     for n in range(per):
-        quarter = held[step * per + n].astype(F32) * 0.25
-        wide[pl.ds(0, side * side, stride=2), :] = quarter
-        wide[pl.ds(1, side * side, stride=2), :] = quarter
+        group, position = own_ref[step * per + n], pos_ref[step * per + n]
+        for h in range(CHUNKS):
+
+            @pl.when(position // slots == h)
+            def _(h=h):
+                quarter = arrived[h][group, position - h * slots].astype(F32) * 0.25
+                wide[n, pl.ds(0, side * side, stride=2), :] = quarter
+                wide[n, pl.ds(1, side * side, stride=2), :] = quarter
+
         for row in range(side):
-            line = wide[pl.ds(row * width, width), :].astype(BF16)
+            line = wide[n, pl.ds(row * width, width), :].astype(BF16)
             out[n, 2 * row] = line
             out[n, 2 * row + 1] = line
 
@@ -637,15 +590,12 @@
     return pl.pallas_call(
         functools.partial(spread_kernel, per),
         grid=(count // per,),
-        in_specs=[SMEM, SMEM] + [ANY] * CHUNKS,
+        in_specs=[SMEM, SMEM]
+        + [pl.BlockSpec(a.shape, lambda i: (0, 0, 0, 0), pipeline_mode=pl.Buffered(1)) for a in arrived],
         out_specs=pl.BlockSpec((per, grid, grid, channels), lambda i: (i, 0, 0, 0)),
         out_shape=jax.ShapeDtypeStruct((count, grid, grid, channels), BF16),
-        scratch_shapes=[
-            pltpu.VMEM((count, cells, channels), BF16),
-            pltpu.VMEM((grid * grid // 2, channels), F32),
-            pltpu.SemaphoreType.DMA,
-        ],
-        compiler_params=params(),
+        scratch_shapes=[pltpu.VMEM((per, grid * grid // 2, channels), F32)],
+        compiler_params=pltpu.CompilerParams(vmem_limit_bytes=24 * 1024 * 1024),
         cost_estimate=pl.CostEstimate(
             flops=0, bytes_accessed=10 * count * cells * channels, transcendentals=0
         ),
@@ -717,63 +667,47 @@
         tile_counts, sample_owner, sample_rank, group_id, local_tiles, capacity
     )
     pos = slot % per
-    line = math.isqrt(groups)
-    info = jnp.stack(
-        [filled[0], column_id.astype(jnp.int32), jnp.int32(per), group_id // line, lax.rem(group_id, line)]
-    )
+    info = jnp.stack([filled[0], column_id.astype(jnp.int32), jnp.int32(per)])
     sends = pool_and_pack(tiles, own, pos, groups, slots)
 
     taps = jnp.pad(kernel.astype(F32).reshape(9, blocks, LANES).transpose(1, 0, 2), ((0, 0), (0, 7), (0, 0)))
     gains = jnp.broadcast_to(gain.astype(F32).reshape(blocks, 1, LANES), (blocks, 8, LANES))
     weights = [w_in, w_out, w_in.T, w_out.T, se_down, se_up, se_down.T, se_up.T, taps, gains]
 
-    inner = []
+    received = []
     for h in range(CHUNKS):
         send = sends[h]
         if h > 0:
-            send, _ = lax.optimization_barrier((send, received))
-        received = lax.all_to_all(send, "enc", split_axis=0, concat_axis=0, tiled=True)
+            send, received[-1] = lax.optimization_barrier((send, received[-1]))
+        received.append(lax.all_to_all(send, "enc", split_axis=0, concat_axis=0, tiled=True))
         if h == 0:
-            received, *weights = lax.optimization_barrier((received, *weights))
-        parts = route([received], table, info, h, per, columns, groups, False, h > 0)
+            received[0], *weights = lax.optimization_barrier((received[0], *weights))
+
+    carried = []
+    arrived, small = [], []
+    for h in range(CHUNKS):
         if h > 0:
-            inner[-1], parts = lax.optimization_barrier((inner[-1], parts))
-        inner.append(exchange(parts))
-
-    carried = []
-    arrived, small, narrowed, backs = [], [], [], []
-    for h in range(CHUNKS):
-        made = run_block(h, side, info, inner[h], token_grads, weights, carried, h == 0)
+            received[h], carried = lax.optimization_barrier((received[h], carried))
+        parts = route([received[h]], table, info, h, per, columns, groups, False, h > 0)
+        parts = exchange(parts)
+        made = run_block(h, side, info, parts, token_grads, weights, carried, False)
         carried = list(made[:4])
         small.append(made[-3:])
-        narrowed.append(exchange(made[4:-3]))
-    narrowed[0], carried = lax.optimization_barrier((narrowed[0], carried))
-    for h in range(CHUNKS):
-        back = route(narrowed[h], table, info, h, per, columns, groups, True)
-        if h == 0:
-            _, carried, narrowed[-1][1:4] = lax.optimization_barrier((back, carried, narrowed[-1][1:4]))
+        back = route(exchange(made[4:-3]), table, info, h, per, columns, groups, True)
         arrived.append(lax.all_to_all(back, "enc", split_axis=0, concat_axis=0, tiled=True))
-    last = (back, arrived[0])
     visual, normed, scaled, hidden = carried
+    tile_grads = unpack_and_spread(arrived, own, pos, local_tiles, grid)
 
     home, away = weight_terms(info, normed, scaled, hidden, token_grads, small, columns)
-    home, (_, arrived[0]) = lax.optimization_barrier((home, last))
     near = lax.ppermute(away, "abs", partner_pairs(1, columns))
     pair = [(home[k].astype(F32) + near[k].astype(F32)).astype(BF16) for k in range(columns // 2)]
     rows = [pair[0]] + [
         lax.ppermute(pair[k], "abs", partner_pairs(2 * k, columns)) for k in range(1, columns // 2)
     ]
-
-    def along(parts, pairs):
-        sent = [parts[0]] + [lax.ppermute(parts[k], "enc", pairs(k)) for k in range(1, line)]
-        return sum(r.astype(F32) for r in sent)
-
-    parts = [sum(r[k].astype(F32) for r in rows).astype(BF16) for k in range(line)]
-    row = along(parts, lambda k: [(n, n // line * line + (n + k) % line) for n in range(groups)])
-    parts = [row[k].astype(BF16) for k in range(line)]
-    total = along(parts, lambda k: [(n, (n + k * line) % groups) for n in range(groups)])
-    total = total * (1.0 / math.sqrt(groups * local_tiles * cells))
-    tile_grads = unpack_and_spread(arrived, own, pos, local_tiles, grid)
+    column = sum(r.astype(F32) for r in rows).astype(BF16)
+    spread = lax.all_to_all(column, "enc", split_axis=0, concat_axis=0, tiled=True)
+    scale = 1.0 / math.sqrt(groups * local_tiles * cells)
+    total = jnp.sum(spread.astype(F32), axis=0) * scale
     narrow = se_down.shape[1]
     ends = [width, 2 * width, 2 * width + narrow, 2 * width + 2 * narrow]
     last = total[:, ends[3] : ends[3] + 10]

time: 332 us -> 344 us (1.036)
  waiting for transfers between devices: 123 us -> 132 us
  local copies, waits for them, and re-layouts: 29.1 us -> 34.7 us
    ppermute x14 -> x21, waiting for transfers between devices: 17.9 us -> 57.5 us  [exchange(): lax.ppermute(parts[k], 'abs', partner_pairs(k, columns))]
    all_to_all x2, waiting for transfers between devices: 55.8 us -> 32.8 us  [local(): lax.all_to_all(send, 'enc', split_axis=0, concat_axis=0, tiled=True)]
    ppermute x6 -> x0, waiting for transfers between devices: 17.9 us -> none  [along(): lax.ppermute(parts[k], 'enc', pairs(k))]
    ppermute x6 -> x0, starting transfers between devices: 8.69 us -> none  [along(): lax.ppermute(parts[k], 'enc', pairs(k))]
    all_to_all x2 -> x1, starting transfers between devices: 10.6 us -> 4.52 us  [exchange(): lax.all_to_all(parts[0], 'abs', split_axis=0, concat_axis=0, tiled=True)]
    ppermute x3, waiting for transfers between devices: 25.6 us -> 30.6 us  [local(): lax.ppermute(pair[k], 'abs', partner_pairs(2 * k, columns))]
    ppermute x14 -> x21, starting transfers between devices: 18.6 us -> 23.6 us  [exchange(): lax.ppermute(parts[k], 'abs', partner_pairs(k, columns))]
    all_to_all x0 -> x1, waiting for transfers between devices: none -> 4.76 us  [local(): lax.all_to_all(column, 'enc', split_axis=0, concat_axis=0, tiled=True)]
  transfers between devices with their start and end apart: 30 -> 31, of which waited for: 15 -> 17; matrix products, arithmetic and copies ran while one was open for 6% -> 7% of each run, Pallas kernels for 28% -> 26%
where the time goes in v4:
time: 344 us; the launch traced here: 342 us
  waiting for transfers between devices  132 us (38%)
  Pallas kernels  101 us (29%)
  starting transfers between devices  60.8 us (18%)
  local copies, waits for them, and re-layouts  34.7 us (10%)
  other arithmetic  11.9 us (3%)
    ppermute x21, waiting for transfers between devices, exchange(): lax.ppermute(parts[k], 'abs', partner_pairs(k, columns))  57.5 us
    pallas_call x2, Pallas kernels, run_block(): pl.pallas_call(functools.partial(block_kernel, chunk, side, columns, len(...  56.9 us
    all_to_all x2, waiting for transfers between devices, local(): lax.all_to_all(send, 'enc', split_axis=0, concat_axis=0, tiled=True)  32.8 us
    ppermute x3, waiting for transfers between devices, local(): lax.ppermute(pair[k], 'abs', partner_pairs(2 * k, columns))  30.6 us
    ppermute x21, starting transfers between devices, exchange(): lax.ppermute(parts[k], 'abs', partner_pairs(k, columns))  23.6 us
    unnamed x67, local copies, waits for them, and re-layouts  22.7 us
    pallas_call x1, Pallas kernels, weight_terms(): pl.pallas_call(functools.partial(weights_kernel, len(small), columns), gr...  15 us
    pallas_call x4, Pallas kernels, route(): pl.pallas_call(functools.partial(route_kernel, chunk, per, columns, back)...  13.2 us
  transfers between devices with their start and end apart: 31, of which 17 were waited for; matrix products, arithmetic and copies ran while one was open for 7% of the time, Pallas kernels for 26%

profile of v4, /device:TPU:0, one launch (start us, length us, event | category | flops | bytes accessed | tf_op | source)
XLA Modules:
  0.0 341.9 jit_solution(7431116726244978863)
XLA Ops:
  7.0 8.3 %pool_and_pack.1 = (bf16[16,5,144,128]{3,2,1,0:T(8,128)(2,1)}, bf16[16,5,144,128]{3,2,1,0:T(8,128)(2,1)}) custom-call(s32[48]{0:T(128)} %get-tuple-element.135.own_ref, s32[48]{0:T(128)} %and_select_fusion.pos_ref, bf16[48,24,24,128]{3,2,1,0:T(8,128)(2,1)} %tiles_ref.1), custom_call_target="tpu_custom_call" | custom-call | flops 3538944 | bytes 10616832 | tf_op jit(solution)/shard_map/pool_and_pack/pallas_call | solution.py:62
  15.4 7.1 %all-to-all-start = ((bf16[16,5,144,128]{3,2,1,0:T(8,128)(2,1)}), bf16[16,5,144,128]{3,2,1,0:T(8,128)(2,1)S(1)}, u32[]{:S(2)}, u32[]{:S(2)}) async-start(bf16[16,5,144,128]{3,2,1,0:T(8,128)(2,1)} %get-tuple-element.69), calls=%async_computation | async-start | bytes 5898240 | tf_op jit(solution)/shard_map/all_to_all | solution.py:682
  22.5 4.0 %copy.36 = bf16[1024,1024]{0,1:T(8,128)(2,1)} copy(bf16[1024,1024]{1,0:T(8,128)(2,1)} %rest_2_) | data formatting | bytes 4194304 | tf_op args[1]
  26.5 4.0 %copy.37 = bf16[1024,1024]{0,1:T(8,128)(2,1)} copy(bf16[1024,1024]{1,0:T(8,128)(2,1)} %rest_3_) | data formatting | bytes 4194304 | tf_op args[2]
  34.2 32.8 %all-to-all-done.rest_0_ = bf16[16,5,144,128]{3,2,1,0:T(8,128)(2,1)S(1)} async-done(((bf16[16,5,144,128]{3,2,1,0:T(8,128)(2,1)}), bf16[16,5,144,128]{3,2,1,0:T(8,128)(2,1)S(1)}, u32[]{:S(2)}, u32[]{:S(2)}) %all-to-all-start) | async-done | bytes 2949152 | tf_op jit(solution)/shard_map/all_to_all | solution.py:682
  69.2 4.2 %all-to-all-start.1 = ((bf16[16,5,144,128]{3,2,1,0:T(8,128)(2,1)}), bf16[16,5,144,128]{3,2,1,0:T(8,128)(2,1)S(1)}, u32[]{:S(2)}, u32[]{:S(2)}) async-start(bf16[16,5,144,128]{3,2,1,0:T(8,128)(2,1)} %get-tuple-element.71), calls=%async_computation.1 | async-start | bytes 5898240 | tf_op jit(solution)/shard_map/all_to_all | solution.py:682
  76.1 3.3 route_in.2
  93.2 5.7 %collective-permute-done.3.rest_4_ = bf16[5,144,128]{2,1,0:T(8,128)(2,1)S(1)} collective-permute-done((bf16[5,144,128]{2,1,0:T(8,128)(2,1)S(1)}, bf16[5,144,128]{2,1,0:T(8,128)(2,1)S(1)}, u32[]{:S(2)}, u32[]{:S(2)}) %collective-permute-start.3) | collective-permute-done | bytes 184352 | tf_op jit(solution)/shard_map/ppermute | solution.py:94
  98.9 3.2 collective-permute-done.4.rest_5_
  103.6 28.5 %block_0.1 = (bf16[10,144,1024]{2,1,0:T(8,128)(2,1)}, bf16[10,144,1024]{2,1,0:T(8,128)(2,1)}, bf16[10,144,1024]{2,1,0:T(8,128)(2,1)}, bf16[10,144,1024]{2,1,0:T(...) custom-call(s32[3]{0:T(128)} %copy-done.7, ...), custom_call_target="tpu_custom_call" | custom-call | flops 6039797760 | bytes 20185088 | tf_op jit(solution)/shard_map/block_0/pallas_call | solution.py:432
  132.7 3.3 route_in.3
  137.1 4.5 %all-to-all-start.2 = ((bf16[8,5,144,128]{3,2,1,0:T(8,128)(2,1)}), bf16[8,5,144,128]{3,2,1,0:T(8,128)(2,1)S(1)}, u32[]{:S(2)}, u32[]{:S(2)}) async-start(bf16[8,5,144,128]{3,2,1,0:T(8,128)(2,1)} %copy-done.4), calls=%async_computation.2 | async-start | bytes 2949120 | tf_op jit(solution)/shard_map/all_to_all | solution.py:93
  141.6 3.5 %collective-permute-start.10 = (bf16[5,144,128]{2,1,0:T(8,128)(2,1)S(1)}, bf16[5,144,128]{2,1,0:T(8,128)(2,1)S(1)}, u32[]{:S(2)}, u32[]{:S(2)}) collective-permute-start(bf16[5,144,128]{2,1,0:T(8,128)(2,1)S(1)} %copy-done.28), channel_id=1, source_target_pairs={{0,4},{1,5},{2,6},{3,7},{4,0},{5,1},{6,2},{7,3},{8,12},{9,13},{10,... | collective-permute-start | bytes 552968 | tf_op jit(solution)/shard_map/ppermute | solution.py:94
  145.1 2.7 collective-permute-start.12
  148.8 17.7 %collective-permute-done.10.rest_4_ = bf16[5,144,128]{2,1,0:T(8,128)(2,1)S(1)} collective-permute-done((bf16[5,144,128]{2,1,0:T(8,128)(2,1)S(1)}, bf16[5,144,128]{2,1,0:T(8,128)(2,1)S(1)}, u32[]{:S(2)}, u32[]{:S(2)}) %collective-permute-start.10) | collective-permute-done | bytes 184352 | tf_op jit(solution)/shard_map/ppermute | solution.py:94
  173.1 2.9 collective-permute-done.13.rest_7_
  177.2 3.3 route_back.2
  183.2 6.9 %all-to-all-start.3 = ((bf16[16,5,144,128]{3,2,1,0:T(8,128)(2,1)}), bf16[16,5,144,128]{3,2,1,0:T(8,128)(2,1)S(1)}, u32[]{:S(2)}, u32[]{:S(2)}) async-start(bf16[16,5,144,128]{3,2,1,0:T(8,128)(2,1)} %copy-done), calls=%async_computation.3 | async-start | bytes 5898240 | tf_op jit(solution)/shard_map/all_to_all | solution.py:697
  190.2 28.4 %block_1.1 = (bf16[10,144,1024]{2,1,0:T(8,128)(2,1)}, bf16[10,144,1024]{2,1,0:T(8,128)(2,1)}, bf16[10,144,1024]{2,1,0:T(8,128)(2,1)}, bf16[10,144,1024]{2,1,0:T(...) custom-call(s32[3]{0:T(128)} %copy-done.7, ...), custom_call_target="tpu_custom_call", output_to_operand_aliasing={{0}: (13, {}), {1}: (14, {}), {2}: (15, {}), {3}: (16, {})} | custom-call | flops 6039797760 | bytes 20185088 | tf_op jit(solution)/shard_map/block_1/pallas_call | solution.py:432
  221.9 15.0 %weight_terms.1 = (bf16[4,16,8,2688]{3,2,1,0:T(8,128)(2,1)}, bf16[4,16,8,2688]{3,2,1,0:T(8,128)(2,1)}) custom-call(s32[3]{0:T(128)} %copy-done.7, bf16[10,144,1024]{2,1,0:T(8,128)(2,1)} %get-tuple-element.117.normed, bf16[10,144,1024]{2,1,0:T(8,128)(2,1)} %get-tuple-element.118.scaled, bf16[10,144,1024]{2,1,0:T(8,128)(2,1)} %get-tuple-element.119.hidden, ...), custom_call_target="tpu_custom_call" | custom-call | flops 6039797760 | bytes 11796480 | tf_op jit(solution)/shard_map/weight_terms/pallas_call | solution.py:550
  238.4 3.5 %collective-permute-start.17 = (bf16[5,144,128]{2,1,0:T(8,128)(2,1)}, bf16[5,144,128]{2,1,0:T(8,128)(2,1)S(1)}, u32[]{:S(2)}, u32[]{:S(2)}) collective-permute-start(bf16[5,144,128]{2,1,0:T(8,128)(2,1)} %get-tuple-element.113), channel_id=1, source_target_pairs={{0,4},{1,5},{2,6},{3,7},{4,0},{5,1},{6,2},{7,3},{8,12},{9,13},{10,... | collective-permute-start | bytes 552968 | tf_op jit(solution)/shard_map/ppermute | solution.py:94
  243.7 2.7 collective-permute-done.15.rest_2_
  246.4 10.7 %collective-permute-done.16.rest_3_ = bf16[5,144,128]{2,1,0:T(8,128)(2,1)S(1)} collective-permute-done((bf16[5,144,128]{2,1,0:T(8,128)(2,1)}, bf16[5,144,128]{2,1,0:T(8,128)(2,1)S(1)}, u32[]{:S(2)}, u32[]{:S(2)}) %collective-permute-start.16) | collective-permute-done | bytes 184352 | tf_op jit(solution)/shard_map/ppermute | solution.py:94
  257.2 6.4 %collective-permute-done.20.rest_7_ = bf16[5,144,128]{2,1,0:T(8,128)(2,1)S(1)} collective-permute-done((bf16[5,144,128]{2,1,0:T(8,128)(2,1)S(1)}, bf16[5,144,128]{2,1,0:T(8,128)(2,1)S(1)}, u32[]{:S(2)}, u32[]{:S(2)}) %collective-permute-start.20) | collective-permute-done | bytes 184352 | tf_op jit(solution)/shard_map/ppermute | solution.py:94
  263.5 3.3 route_back.3
  268.4 6.2 %all-to-all-start.4 = ((bf16[16,5,144,128]{3,2,1,0:T(8,128)(2,1)}), bf16[16,5,144,128]{3,2,1,0:T(8,128)(2,1)}, u32[]{:S(2)}, u32[]{:S(2)}) async-start(bf16[16,5,144,128]{3,2,1,0:T(8,128)(2,1)} %copy-done.1), calls=%async_computation.4 | async-start | bytes 5898240 | tf_op jit(solution)/shard_map/all_to_all | solution.py:697
  277.4 2.9 collective-permute-start.23
  280.6 30.0 %collective-permute-done.22 = bf16[16,8,2688]{2,1,0:T(8,128)(2,1)S(1)} collective-permute-done((bf16[16,8,2688]{2,1,0:T(8,128)(2,1)S(1)}, bf16[16,8,2688]{2,1,0:T(8,128)(2,1)S(1)}, u32[]{:S(2)}, u32[]{:S(2)}) %collective-permute-start.22) | collective-permute-done | bytes 688160 | tf_op jit(solution)/shard_map/ppermute | solution.py:705
  313.9 6.5 %all-to-all-done.4.rest_1_ = bf16[16,5,144,128]{3,2,1,0:T(8,128)(2,1)} async-done(((bf16[16,5,144,128]{3,2,1,0:T(8,128)(2,1)}), bf16[16,5,144,128]{3,2,1,0:T(8,128)(2,1)}, u32[]{:S(2)}, u32[]{:S(2)}) %all-to-all-start.4) | async-done | bytes 2949152 | tf_op jit(solution)/shard_map/all_to_all | solution.py:697
  320.4 4.5 %all-to-all-start.5 = ((bf16[16,8,2688]{2,1,0:T(8,128)(2,1)}), bf16[16,8,2688]{2,1,0:T(8,128)(2,1)}, u32[]{:S(2)}, u32[]{:S(2)}) async-start(bf16[16,8,2688]{2,1,0:T(8,128)(2,1)} %fusion.2), calls=%async_computation.5 | async-start | bytes 1376256 | tf_op jit(solution)/shard_map/all_to_all | solution.py:708
  324.8 7.9 %unpack_and_spread.1 = bf16[48,24,24,128]{3,2,1,0:T(8,128)(2,1)} custom-call(s32[48]{0:T(128)S(1)} %copy-done.11, s32[48]{0:T(128)S(1)} %copy-done.12, bf16[16,5,144,128]{3,2,1,0:T(8,128)(2,1)S(1)} %all-to-all-done.3.rest_0_, bf16[16,5,144,128]{3,2,1,0:T(8,128)(2,1)} %all-to-all-done.4.rest_1_), custom_call_target="tpu_custom_call" | custom-call | bytes 8847360 | tf_op jit(solution)/shard_map/unpack_and_spread/pallas_call | solution.py:590
  332.8 4.8 %all-to-all-done.5 = bf16[16,8,2688]{2,1,0:T(8,128)(2,1)} async-done(((bf16[16,8,2688]{2,1,0:T(8,128)(2,1)}), bf16[16,8,2688]{2,1,0:T(8,128)(2,1)}, u32[]{:S(2)}, u32[]{:S(2)}) %all-to-all-start.5) | async-done | bytes 688160 | tf_op jit(solution)/shard_map/all_to_all | solution.py:708
  (145 shorter events, 62.2 us)
Async XLA Ops:
  15.4 51.6 %all-to-all-start = ((bf16[16,5,144,128]{3,2,1,0:T(8,128)(2,1)}), bf16[16,5,144,128]{3,2,1,0:T(8,128)(2,1)S(1)}, u32[]{:S(2)}, u32[]{:S(2)}) async-start(bf16[16,5,144,128]{3,2,1,0:T(8,128)(2,1)} %get-tuple-element.69), calls=%async_computation | async-start | bytes 5898240 | tf_op jit(solution)/shard_map/all_to_all | solution.py:682
  69.2 62.8 %all-to-all-start.1 = ((bf16[16,5,144,128]{3,2,1,0:T(8,128)(2,1)}), bf16[16,5,144,128]{3,2,1,0:T(8,128)(2,1)S(1)}, u32[]{:S(2)}, u32[]{:S(2)}) async-start(bf16[16,5,144,128]{3,2,1,0:T(8,128)(2,1)} %get-tuple-element.71), calls=%async_computation.1 | async-start | bytes 5898240 | tf_op jit(solution)/shard_map/all_to_all | solution.py:682
  80.1 6.8 %collective-permute-start = (bf16[5,144,128]{2,1,0:T(8,128)(2,1)S(1)}, bf16[5,144,128]{2,1,0:T(8,128)(2,1)S(1)}, u32[]{:S(2)}, u32[]{:S(2)}) collective-permute-start(bf16[5,144,128]{2,1,0:T(8,128)(2,1)S(1)} %get-tuple-element.74), channel_id=1, source_target_pairs={{0,1},{1,0},{2,3},{3,2},{4,5},{5,4},{6,7},{7,6},{8,9},{9,8},{10,11... | collective-permute-start | bytes 552968 | tf_op jit(solution)/shard_map/ppermute | solution.py:94
  80.1 9.5 %collective-permute-start.1 = (bf16[5,144,128]{2,1,0:T(8,128)(2,1)S(1)}, bf16[5,144,128]{2,1,0:T(8,128)(2,1)S(1)}, u32[]{:S(2)}, u32[]{:S(2)}) collective-permute-start(bf16[5,144,128]{2,1,0:T(8,128)(2,1)S(1)} %get-tuple-element.75), channel_id=1, source_target_pairs={{0,2},{1,3},{2,4},{3,5},{4,6},{5,7},{6,0},{7,1},{8,10},{9,11},{10,... | collective-permute-start | bytes 552968 | tf_op jit(solution)/shard_map/ppermute | solution.py:94
  82.0 11.2 %collective-permute-start.2 = (bf16[5,144,128]{2,1,0:T(8,128)(2,1)S(1)}, bf16[5,144,128]{2,1,0:T(8,128)(2,1)S(1)}, u32[]{:S(2)}, u32[]{:S(2)}) collective-permute-start(bf16[5,144,128]{2,1,0:T(8,128)(2,1)S(1)} %get-tuple-element.76), channel_id=1, source_target_pairs={{0,3},{1,2},{2,5},{3,4},{4,7},{5,6},{6,1},{7,0},{8,11},{9,10},{10,... | collective-permute-start | bytes 552968 | tf_op jit(solution)/shard_map/ppermute | solution.py:94
  83.8 15.1 %collective-permute-start.3 = (bf16[5,144,128]{2,1,0:T(8,128)(2,1)S(1)}, bf16[5,144,128]{2,1,0:T(8,128)(2,1)S(1)}, u32[]{:S(2)}, u32[]{:S(2)}) collective-permute-start(bf16[5,144,128]{2,1,0:T(8,128)(2,1)S(1)} %get-tuple-element.77), channel_id=1, source_target_pairs={{0,4},{1,5},{2,6},{3,7},{4,0},{5,1},{6,2},{7,3},{8,12},{9,13},{10,... | collective-permute-start | bytes 552968 | tf_op jit(solution)/shard_map/ppermute | solution.py:94
  85.8 16.3 %collective-permute-start.4 = (bf16[5,144,128]{2,1,0:T(8,128)(2,1)S(1)}, bf16[5,144,128]{2,1,0:T(8,128)(2,1)S(1)}, u32[]{:S(2)}, u32[]{:S(2)}) collective-permute-start(bf16[5,144,128]{2,1,0:T(8,128)(2,1)S(1)} %get-tuple-element.78), channel_id=1, source_target_pairs={{0,5},{1,4},{2,7},{3,6},{4,1},{5,0},{6,3},{7,2},{8,13},{9,12},{10,... | collective-permute-start | bytes 552968 | tf_op jit(solution)/shard_map/ppermute | solution.py:94
  86.9 15.2 %collective-permute-start.5 = (bf16[5,144,128]{2,1,0:T(8,128)(2,1)S(1)}, bf16[5,144,128]{2,1,0:T(8,128)(2,1)S(1)}, u32[]{:S(2)}, u32[]{:S(2)}) collective-permute-start(bf16[5,144,128]{2,1,0:T(8,128)(2,1)S(1)} %get-tuple-element.79), channel_id=1, source_target_pairs={{0,6},{1,7},{2,0},{3,1},{4,2},{5,3},{6,4},{7,5},{8,14},{9,15},{10,... | collective-permute-start | bytes 552968 | tf_op jit(solution)/shard_map/ppermute | solution.py:94
  89.6 12.5 %collective-permute-start.6 = (bf16[5,144,128]{2,1,0:T(8,128)(2,1)S(1)}, bf16[5,144,128]{2,1,0:T(8,128)(2,1)S(1)}, u32[]{:S(2)}, u32[]{:S(2)}) collective-permute-start(bf16[5,144,128]{2,1,0:T(8,128)(2,1)S(1)} %get-tuple-element.80), channel_id=1, source_target_pairs={{0,7},{1,6},{2,1},{3,0},{4,3},{5,2},{6,5},{7,4},{8,15},{9,14},{10,... | collective-permute-start | bytes 552968 | tf_op jit(solution)/shard_map/ppermute | solution.py:94
  137.1 45.0 %all-to-all-start.2 = ((bf16[8,5,144,128]{3,2,1,0:T(8,128)(2,1)}), bf16[8,5,144,128]{3,2,1,0:T(8,128)(2,1)S(1)}, u32[]{:S(2)}, u32[]{:S(2)}) async-start(bf16[8,5,144,128]{3,2,1,0:T(8,128)(2,1)} %copy-done.4), calls=%async_computation.2 | async-start | bytes 2949120 | tf_op jit(solution)/shard_map/all_to_all | solution.py:93
  141.6 24.9 %collective-permute-start.10 = (bf16[5,144,128]{2,1,0:T(8,128)(2,1)S(1)}, bf16[5,144,128]{2,1,0:T(8,128)(2,1)S(1)}, u32[]{:S(2)}, u32[]{:S(2)}) collective-permute-start(bf16[5,144,128]{2,1,0:T(8,128)(2,1)S(1)} %copy-done.28), channel_id=1, source_target_pairs={{0,4},{1,5},{2,6},{3,7},{4,0},{5,1},{6,2},{7,3},{8,12},{9,13},{10,... | collective-permute-start | bytes 552968 | tf_op jit(solution)/shard_map/ppermute | solution.py:94
  145.1 24.4 %collective-permute-start.11 = (bf16[5,144,128]{2,1,0:T(8,128)(2,1)S(1)}, bf16[5,144,128]{2,1,0:T(8,128)(2,1)S(1)}, u32[]{:S(2)}, u32[]{:S(2)}) collective-permute-start(bf16[5,144,128]{2,1,0:T(8,128)(2,1)S(1)} %copy-done.25), channel_id=1, source_target_pairs={{0,5},{1,4},{2,7},{3,6},{4,1},{5,0},{6,3},{7,2},{8,13},{9,12},{10,... | collective-permute-start | bytes 552968 | tf_op jit(solution)/shard_map/ppermute | solution.py:94
  145.1 28.0 %collective-permute-start.12 = (bf16[5,144,128]{2,1,0:T(8,128)(2,1)}, bf16[5,144,128]{2,1,0:T(8,128)(2,1)S(1)}, u32[]{:S(2)}, u32[]{:S(2)}) collective-permute-start(bf16[5,144,128]{2,1,0:T(8,128)(2,1)} %get-tuple-element.107), channel_id=1, source_target_pairs={{0,6},{1,7},{2,0},{3,1},{4,2},{5,3},{6,4},{7,5},{8,14},{9,15},{10,... | collective-permute-start | bytes 552968 | tf_op jit(solution)/shard_map/ppermute | solution.py:94
  147.9 28.1 %collective-permute-start.13 = (bf16[5,144,128]{2,1,0:T(8,128)(2,1)}, bf16[5,144,128]{2,1,0:T(8,128)(2,1)S(1)}, u32[]{:S(2)}, u32[]{:S(2)}) collective-permute-start(bf16[5,144,128]{2,1,0:T(8,128)(2,1)} %get-tuple-element.108), channel_id=1, source_target_pairs={{0,7},{1,6},{2,1},{3,0},{4,3},{5,2},{6,5},{7,4},{8,15},{9,14},{10,... | collective-permute-start | bytes 552968 | tf_op jit(solution)/shard_map/ppermute | solution.py:94
  148.7 27.3 %collective-permute-start.7 = (bf16[5,144,128]{2,1,0:T(8,128)(2,1)}, bf16[5,144,128]{2,1,0:T(8,128)(2,1)S(1)}, u32[]{:S(2)}, u32[]{:S(2)}) collective-permute-start(bf16[5,144,128]{2,1,0:T(8,128)(2,1)} %get-tuple-element.102), channel_id=1, source_target_pairs={{0,1},{1,0},{2,3},{3,2},{4,5},{5,4},{6,7},{7,6},{8,9},{9,8},{10,11... | collective-permute-start | bytes 552968 | tf_op jit(solution)/shard_map/ppermute | solution.py:94
  166.6 9.4 %collective-permute-start.8 = (bf16[5,144,128]{2,1,0:T(8,128)(2,1)}, bf16[5,144,128]{2,1,0:T(8,128)(2,1)S(1)}, u32[]{:S(2)}, u32[]{:S(2)}) collective-permute-start(bf16[5,144,128]{2,1,0:T(8,128)(2,1)} %get-tuple-element.103), channel_id=1, source_target_pairs={{0,2},{1,3},{2,4},{3,5},{4,6},{5,7},{6,0},{7,1},{8,10},{9,11},{10,... | collective-permute-start | bytes 552968 | tf_op jit(solution)/shard_map/ppermute | solution.py:94
  169.6 7.6 %collective-permute-start.9 = (bf16[5,144,128]{2,1,0:T(8,128)(2,1)}, bf16[5,144,128]{2,1,0:T(8,128)(2,1)S(1)}, u32[]{:S(2)}, u32[]{:S(2)}) collective-permute-start(bf16[5,144,128]{2,1,0:T(8,128)(2,1)} %get-tuple-element.104), channel_id=1, source_target_pairs={{0,3},{1,2},{2,5},{3,4},{4,7},{5,6},{6,1},{7,0},{8,11},{9,10},{10,... | collective-permute-start | bytes 552968 | tf_op jit(solution)/shard_map/ppermute | solution.py:94
  183.2 85.2 %all-to-all-start.3 = ((bf16[16,5,144,128]{3,2,1,0:T(8,128)(2,1)}), bf16[16,5,144,128]{3,2,1,0:T(8,128)(2,1)S(1)}, u32[]{:S(2)}, u32[]{:S(2)}) async-start(bf16[16,5,144,128]{3,2,1,0:T(8,128)(2,1)} %copy-done), calls=%async_computation.3 | async-start | bytes 5898240 | tf_op jit(solution)/shard_map/all_to_all | solution.py:697
  236.9 37.8 %collective-permute-start.21 = (bf16[4,16,8,2688]{3,2,1,0:T(8,128)(2,1)}, bf16[4,16,8,2688]{3,2,1,0:T(8,128)(2,1)}, u32[]{:S(2)}, u32[]{:S(2)}) collective-permute-start(bf16[4,16,8,2688]{3,2,1,0:T(8,128)(2,1)} %get-tuple-element.127), channel_id=1, source_target_pairs={{0,1},{1,0},{2,3},{3,2},{4,5},{5,4},{6,7},{7,6},{8,9},{9,8},{10,11... | collective-permute-start | bytes 8257544 | tf_op jit(solution)/shard_map/ppermute | solution.py:702
  237.4 5.2 %collective-permute-start.14 = (bf16[5,144,128]{2,1,0:T(8,128)(2,1)}, bf16[5,144,128]{2,1,0:T(8,128)(2,1)S(1)}, u32[]{:S(2)}, u32[]{:S(2)}) collective-permute-start(bf16[5,144,128]{2,1,0:T(8,128)(2,1)} %get-tuple-element.110), channel_id=1, source_target_pairs={{0,1},{1,0},{2,3},{3,2},{4,5},{5,4},{6,7},{7,6},{8,9},{9,8},{10,11... | collective-permute-start | bytes 552968 | tf_op jit(solution)/shard_map/ppermute | solution.py:94
  237.5 8.9 %collective-permute-start.15 = (bf16[5,144,128]{2,1,0:T(8,128)(2,1)}, bf16[5,144,128]{2,1,0:T(8,128)(2,1)S(1)}, u32[]{:S(2)}, u32[]{:S(2)}) collective-permute-start(bf16[5,144,128]{2,1,0:T(8,128)(2,1)} %get-tuple-element.111), channel_id=1, source_target_pairs={{0,2},{1,3},{2,4},{3,5},{4,6},{5,7},{6,0},{7,1},{8,10},{9,11},{10,... | collective-permute-start | bytes 552968 | tf_op jit(solution)/shard_map/ppermute | solution.py:94
  237.8 19.4 %collective-permute-start.16 = (bf16[5,144,128]{2,1,0:T(8,128)(2,1)}, bf16[5,144,128]{2,1,0:T(8,128)(2,1)S(1)}, u32[]{:S(2)}, u32[]{:S(2)}) collective-permute-start(bf16[5,144,128]{2,1,0:T(8,128)(2,1)} %get-tuple-element.112), channel_id=1, source_target_pairs={{0,3},{1,2},{2,5},{3,4},{4,7},{5,6},{6,1},{7,0},{8,11},{9,10},{10,... | collective-permute-start | bytes 552968 | tf_op jit(solution)/shard_map/ppermute | solution.py:94
  238.4 18.7 %collective-permute-start.17 = (bf16[5,144,128]{2,1,0:T(8,128)(2,1)}, bf16[5,144,128]{2,1,0:T(8,128)(2,1)S(1)}, u32[]{:S(2)}, u32[]{:S(2)}) collective-permute-start(bf16[5,144,128]{2,1,0:T(8,128)(2,1)} %get-tuple-element.113), channel_id=1, source_target_pairs={{0,4},{1,5},{2,6},{3,7},{4,0},{5,1},{6,2},{7,3},{8,12},{9,13},{10,... | collective-permute-start | bytes 552968 | tf_op jit(solution)/shard_map/ppermute | solution.py:94
  242.6 14.6 %collective-permute-start.18 = (bf16[5,144,128]{2,1,0:T(8,128)(2,1)S(1)}, bf16[5,144,128]{2,1,0:T(8,128)(2,1)S(1)}, u32[]{:S(2)}, u32[]{:S(2)}) collective-permute-start(bf16[5,144,128]{2,1,0:T(8,128)(2,1)S(1)} %copy-done.21), channel_id=1, source_target_pairs={{0,5},{1,4},{2,7},{3,6},{4,1},{5,0},{6,3},{7,2},{8,13},{9,12},{10,... | collective-permute-start | bytes 552968 | tf_op jit(solution)/shard_map/ppermute | solution.py:94
  246.4 10.7 %collective-permute-start.19 = (bf16[5,144,128]{2,1,0:T(8,128)(2,1)S(1)}, bf16[5,144,128]{2,1,0:T(8,128)(2,1)S(1)}, u32[]{:S(2)}, u32[]{:S(2)}) collective-permute-start(bf16[5,144,128]{2,1,0:T(8,128)(2,1)S(1)} %copy-done.20), channel_id=1, source_target_pairs={{0,6},{1,7},{2,0},{3,1},{4,2},{5,3},{6,4},{7,5},{8,14},{9,15},{10,... | collective-permute-start | bytes 552968 | tf_op jit(solution)/shard_map/ppermute | solution.py:94
  257.1 6.4 %collective-permute-start.20 = (bf16[5,144,128]{2,1,0:T(8,128)(2,1)S(1)}, bf16[5,144,128]{2,1,0:T(8,128)(2,1)S(1)}, u32[]{:S(2)}, u32[]{:S(2)}) collective-permute-start(bf16[5,144,128]{2,1,0:T(8,128)(2,1)S(1)} %copy-done.19), channel_id=1, source_target_pairs={{0,7},{1,6},{2,1},{3,0},{4,3},{5,2},{6,5},{7,4},{8,15},{9,14},{10,... | collective-permute-start | bytes 552968 | tf_op jit(solution)/shard_map/ppermute | solution.py:94
  268.4 51.9 %all-to-all-start.4 = ((bf16[16,5,144,128]{3,2,1,0:T(8,128)(2,1)}), bf16[16,5,144,128]{3,2,1,0:T(8,128)(2,1)}, u32[]{:S(2)}, u32[]{:S(2)}) async-start(bf16[16,5,144,128]{3,2,1,0:T(8,128)(2,1)} %copy-done.1), calls=%async_computation.4 | async-start | bytes 5898240 | tf_op jit(solution)/shard_map/all_to_all | solution.py:697
  277.3 33.3 %collective-permute-start.22 = (bf16[16,8,2688]{2,1,0:T(8,128)(2,1)S(1)}, bf16[16,8,2688]{2,1,0:T(8,128)(2,1)S(1)}, u32[]{:S(2)}, u32[]{:S(2)}) collective-permute-start(bf16[16,8,2688]{2,1,0:T(8,128)(2,1)S(1)} %get-tuple-element.138), channel_id=1, source_target_pairs={{0,2},{1,3},{2,4},{3,5},{4,6},{5,7},{6,0},{7,1},{8,10},{9,11},{10,... | collective-permute-start | bytes 2064392 | tf_op jit(solution)/shard_map/ppermute | solution.py:705
  277.4 33.2 %collective-permute-start.23 = (bf16[16,8,2688]{2,1,0:T(8,128)(2,1)S(1)}, bf16[16,8,2688]{2,1,0:T(8,128)(2,1)S(1)}, u32[]{:S(2)}, u32[]{:S(2)}) collective-permute-start(bf16[16,8,2688]{2,1,0:T(8,128)(2,1)S(1)} %get-tuple-element.140), channel_id=1, source_target_pairs={{0,4},{1,5},{2,6},{3,7},{4,0},{5,1},{6,2},{7,3},{8,12},{9,13},{10,... | collective-permute-start | bytes 2064392 | tf_op jit(solution)/shard_map/ppermute | solution.py:705
  280.3 44.5 %copy-start.12 = (s32[48]{0:T(128)S(1)}, s32[48]{0:T(128)}, u32[]{:S(2)}) copy-start(s32[48]{0:T(128)} %and_select_fusion.pos_ref) | copy-start | bytes 580
  280.3 30.9 %collective-permute-start.24 = (bf16[16,8,2688]{2,1,0:T(8,128)(2,1)S(1)}, bf16[16,8,2688]{2,1,0:T(8,128)(2,1)S(1)}, u32[]{:S(2)}, u32[]{:S(2)}) collective-permute-start(bf16[16,8,2688]{2,1,0:T(8,128)(2,1)S(1)} %get-tuple-element.139), channel_id=1, source_target_pairs={{0,6},{1,7},{2,0},{3,1},{4,2},{5,3},{6,4},{7,5},{8,14},{9,15},{10,... | collective-permute-start | bytes 2064392 | tf_op jit(solution)/shard_map/ppermute | solution.py:705
  320.4 17.2 %all-to-all-start.5 = ((bf16[16,8,2688]{2,1,0:T(8,128)(2,1)}), bf16[16,8,2688]{2,1,0:T(8,128)(2,1)}, u32[]{:S(2)}, u32[]{:S(2)}) async-start(bf16[16,8,2688]{2,1,0:T(8,128)(2,1)} %fusion.2), calls=%async_computation.5 | async-start | bytes 1376256 | tf_op jit(solution)/shard_map/all_to_all | solution.py:708
  (30 other events, 452.2 us)

commit v5 on v4

--- a/solution.py
+++ b/solution.py
@@ -239,12 +239,10 @@
 
     for one in x_loads:
         one.wait()
-    loads[1].wait()
     for t in range(tiles):
 
         @pl.when(chunk * tiles + t >= live)
         def _(t=t):
-            up[t] = jnp.zeros(up.shape[1:], BF16)
             for c in range(blocks):
                 x[c, t] = jnp.zeros((cells, lanes), BF16)
 
@@ -319,6 +317,13 @@
 
     def put_back(c, value):
         wide[c] = value
+
+    loads[1].wait()
+    for t in range(tiles):
+
+        @pl.when(chunk * tiles + t >= live)
+        def _(t=t):
+            up[t] = jnp.zeros(up.shape[1:], BF16)
 
     loads[3].wait()
     product(up, w_out_t, put_back)
@@ -674,26 +679,31 @@
     gains = jnp.broadcast_to(gain.astype(F32).reshape(blocks, 1, LANES), (blocks, 8, LANES))
     weights = [w_in, w_out, w_in.T, w_out.T, se_down, se_up, se_down.T, se_up.T, taps, gains]
 
-    received = []
+    inner = []
     for h in range(CHUNKS):
         send = sends[h]
         if h > 0:
-            send, received[-1] = lax.optimization_barrier((send, received[-1]))
-        received.append(lax.all_to_all(send, "enc", split_axis=0, concat_axis=0, tiled=True))
+            send, _ = lax.optimization_barrier((send, received))
+        received = lax.all_to_all(send, "enc", split_axis=0, concat_axis=0, tiled=True)
         if h == 0:
-            received[0], *weights = lax.optimization_barrier((received[0], *weights))
+            received, *weights = lax.optimization_barrier((received, *weights))
+        parts = route([received], table, info, h, per, columns, groups, False, h > 0)
+        if h > 0:
+            inner[-1], parts = lax.optimization_barrier((inner[-1], parts))
+        inner.append(exchange(parts))
 
     carried = []
-    arrived, small = [], []
+    arrived, small, narrowed, backs = [], [], [], []
     for h in range(CHUNKS):
-        if h > 0:
-            received[h], carried = lax.optimization_barrier((received[h], carried))
-        parts = route([received[h]], table, info, h, per, columns, groups, False, h > 0)
-        parts = exchange(parts)
-        made = run_block(h, side, info, parts, token_grads, weights, carried, False)
+        made = run_block(h, side, info, inner[h], token_grads, weights, carried, h == 0)
         carried = list(made[:4])
         small.append(made[-3:])
-        back = route(exchange(made[4:-3]), table, info, h, per, columns, groups, True)
+        narrowed.append(exchange(made[4:-3]))
+    narrowed[0], carried = lax.optimization_barrier((narrowed[0], carried))
+    for h in range(CHUNKS):
+        back = route(narrowed[h], table, info, h, per, columns, groups, True)
+        if h == 0:
+            back, carried = lax.optimization_barrier((back, carried))
         arrived.append(lax.all_to_all(back, "enc", split_axis=0, concat_axis=0, tiled=True))
     visual, normed, scaled, hidden = carried
     tile_grads = unpack_and_spread(arrived, own, pos, local_tiles, grid)

time: 344 us -> 316 us (0.919)
  waiting for transfers between devices: 132 us -> 115 us
  local copies, waits for them, and re-layouts: 34.7 us -> 30 us
    ppermute x21 -> x14, waiting for transfers between devices: 57.5 us -> 17.2 us  [exchange(): lax.ppermute(parts[k], 'abs', partner_pairs(k, columns))]
    all_to_all x2, waiting for transfers between devices: 32.8 us -> 56.5 us  [local(): lax.all_to_all(send, 'enc', split_axis=0, concat_axis=0, tiled=True)]
    all_to_all x1 -> x2, starting transfers between devices: 4.52 us -> 10.1 us  [exchange(): lax.all_to_all(parts[0], 'abs', split_axis=0, concat_axis=0, tiled=True)]
    ppermute x21 -> x14, starting transfers between devices: 23.6 us -> 18.3 us  [exchange(): lax.ppermute(parts[k], 'abs', partner_pairs(k, columns))]
    all_to_all x2, starting transfers between devices: 13.2 us -> 9.25 us  [local(): lax.all_to_all(back, 'enc', split_axis=0, concat_axis=0, tiled=True)]
    unnamed x67 -> x51, local copies, waits for them, and re-layouts: 22.7 us -> 20.3 us
  transfers between devices with their start and end apart: 31 -> 25, of which waited for: 17 -> 15; matrix products, arithmetic and copies ran while one was open for 7% -> 6% of each run, Pallas kernels for 26% -> 28%
where the time goes in v5:
time: 316 us; the launch traced here: 314 us
  waiting for transfers between devices  115 us (36%)
  Pallas kernels  98.7 us (31%)
  starting transfers between devices  58 us (18%)
  local copies, waits for them, and re-layouts  30 us (9%)
  other arithmetic  11.9 us (4%)
    all_to_all x2, waiting for transfers between devices, local(): lax.all_to_all(send, 'enc', split_axis=0, concat_axis=0, tiled=True)  56.5 us
    pallas_call x2, Pallas kernels, run_block(): pl.pallas_call(functools.partial(block_kernel, chunk, side, columns, len(...  54.8 us
    ppermute x3, waiting for transfers between devices, local(): lax.ppermute(pair[k], 'abs', partner_pairs(2 * k, columns))  29.2 us
    unnamed x51, local copies, waits for them, and re-layouts  20.3 us
    ppermute x14, starting transfers between devices, exchange(): lax.ppermute(parts[k], 'abs', partner_pairs(k, columns))  18.3 us
    ppermute x14, waiting for transfers between devices, exchange(): lax.ppermute(parts[k], 'abs', partner_pairs(k, columns))  17.2 us
    pallas_call x1, Pallas kernels, weight_terms(): pl.pallas_call(functools.partial(weights_kernel, len(small), columns), gr...  15 us
    pallas_call x4, Pallas kernels, route(): pl.pallas_call(functools.partial(route_kernel, chunk, per, columns, back)...  12.7 us
  transfers between devices with their start and end apart: 25, of which 15 were waited for; matrix products, arithmetic and copies ran while one was open for 6% of the time, Pallas kernels for 28%

profile of v5, /device:TPU:0, one launch (start us, length us, event | category | flops | bytes accessed | tf_op | source)
XLA Modules:
  0.0 314.4 jit_solution(7344270090450452648)
XLA Ops:
  7.0 8.3 %pool_and_pack.1 = (bf16[16,5,144,128]{3,2,1,0:T(8,128)(2,1)}, bf16[16,5,144,128]{3,2,1,0:T(8,128)(2,1)}) custom-call(s32[48]{0:T(128)} %get-tuple-element.147.own_ref, s32[48]{0:T(128)} %and_select_fusion.pos_ref, bf16[48,24,24,128]{3,2,1,0:T(8,128)(2,1)} %tiles_ref.1), custom_call_target="tpu_custom_call" | custom-call | flops 3538944 | bytes 10616832 | tf_op jit(solution)/shard_map/pool_and_pack/pallas_call | solution.py:62
  15.4 7.1 %all-to-all-start = ((bf16[16,5,144,128]{3,2,1,0:T(8,128)(2,1)}), bf16[16,5,144,128]{3,2,1,0:T(8,128)(2,1)S(1)}, u32[]{:S(2)}, u32[]{:S(2)}) async-start(bf16[16,5,144,128]{3,2,1,0:T(8,128)(2,1)} %get-tuple-element.74), calls=%async_computation | async-start | bytes 5898240 | tf_op jit(solution)/shard_map/all_to_all | solution.py:687
  22.5 4.0 %copy.36 = bf16[1024,1024]{0,1:T(8,128)(2,1)} copy(bf16[1024,1024]{1,0:T(8,128)(2,1)} %rest_2_) | data formatting | bytes 4194304 | tf_op args[1]
  26.5 4.0 %copy.37 = bf16[1024,1024]{0,1:T(8,128)(2,1)} copy(bf16[1024,1024]{1,0:T(8,128)(2,1)} %rest_3_) | data formatting | bytes 4194304 | tf_op args[2]
  34.2 32.8 %all-to-all-done.rest_0_ = bf16[16,5,144,128]{3,2,1,0:T(8,128)(2,1)S(1)} async-done(((bf16[16,5,144,128]{3,2,1,0:T(8,128)(2,1)}), bf16[16,5,144,128]{3,2,1,0:T(8,128)(2,1)S(1)}, u32[]{:S(2)}, u32[]{:S(2)}) %all-to-all-start) | async-done | bytes 2949152 | tf_op jit(solution)/shard_map/all_to_all | solution.py:687
  69.3 4.2 %all-to-all-start.1 = ((bf16[16,5,144,128]{3,2,1,0:T(8,128)(2,1)}), bf16[16,5,144,128]{3,2,1,0:T(8,128)(2,1)S(1)}, u32[]{:S(2)}, u32[]{:S(2)}) async-start(bf16[16,5,144,128]{3,2,1,0:T(8,128)(2,1)} %get-tuple-element.85), calls=%async_computation.1 | async-start | bytes 5898240 | tf_op jit(solution)/shard_map/all_to_all | solution.py:687
  76.1 2.8 route_in.2
  90.8 23.7 %all-to-all-done.1.rest_0_ = bf16[16,5,144,128]{3,2,1,0:T(8,128)(2,1)S(1)} async-done(((bf16[16,5,144,128]{3,2,1,0:T(8,128)(2,1)}), bf16[16,5,144,128]{3,2,1,0:T(8,128)(2,1)S(1)}, u32[]{:S(2)}, u32[]{:S(2)}) %all-to-all-start.1) | async-done | bytes 2949152 | tf_op jit(solution)/shard_map/all_to_all | solution.py:687
  114.5 3.3 %route_in.3 = bf16[8,5,144,128]{3,2,1,0:T(8,128)(2,1)S(1)} custom-call(s32[80]{0:T(128)S(1)} %select_reduce_fusion.7.table_ref, s32[3]{0:T(128)S(1)} %pad_add_fusion.info_ref, bf16[16,5,144,128]{3,2,1,0:T(8,128)(2,1)S(1)} %all-to-all-done.1.rest_0_), custom_call_target="tpu_custom_call" | custom-call | bytes 5898240 | tf_op jit(solution)/shard_map/route_in/pallas_call | solution.py:139
  119.1 5.3 %all-to-all-start.3 = ((bf16[8,5,144,128]{3,2,1,0:T(8,128)(2,1)}), bf16[8,5,144,128]{3,2,1,0:T(8,128)(2,1)S(1)}, u32[]{:S(2)}, u32[]{:S(2)}) async-start(bf16[8,5,144,128]{3,2,1,0:T(8,128)(2,1)} %copy-done.4), calls=%async_computation.3 | async-start | bytes 2949120 | tf_op jit(solution)/shard_map/all_to_all | solution.py:93
  124.4 27.4 %block_0.1 = (bf16[10,144,1024]{2,1,0:T(8,128)(2,1)}, bf16[10,144,1024]{2,1,0:T(8,128)(2,1)}, bf16[10,144,1024]{2,1,0:T(8,128)(2,1)}, bf16[10,144,1024]{2,1,0:T(...) custom-call(s32[3]{0:T(128)} %copy-done.6, ...), custom_call_target="tpu_custom_call" | custom-call | flops 6039797760 | bytes 20185088 | tf_op jit(solution)/shard_map/block_0/pallas_call | solution.py:437
  151.8 4.8 %all-to-all-start.2 = ((bf16[8,5,144,128]{3,2,1,0:T(8,128)(2,1)}), bf16[8,5,144,128]{3,2,1,0:T(8,128)(2,1)S(1)}, u32[]{:S(2)}, u32[]{:S(2)}) async-start(bf16[8,5,144,128]{3,2,1,0:T(8,128)(2,1)} %get-tuple-element.104), calls=%async_computation.2 | async-start | bytes 2949120 | tf_op jit(solution)/shard_map/all_to_all | solution.py:93
  159.2 27.4 %block_1.1 = (bf16[10,144,1024]{2,1,0:T(8,128)(2,1)}, bf16[10,144,1024]{2,1,0:T(8,128)(2,1)}, bf16[10,144,1024]{2,1,0:T(8,128)(2,1)}, bf16[10,144,1024]{2,1,0:T(...) custom-call(s32[3]{0:T(128)} %copy-done.6, ...), custom_call_target="tpu_custom_call", output_to_operand_aliasing={{0}: (13, {}), {1}: (14, {}), {2}: (15, {}), {3}: (16, {})} | custom-call | flops 6039797760 | bytes 20185088 | tf_op jit(solution)/shard_map/block_1/pallas_call | solution.py:437
  186.7 3.3 %route_back.2 = bf16[16,5,144,128]{3,2,1,0:T(8,128)(2,1)S(1)} custom-call(s32[80]{0:T(128)S(1)} %select_reduce_fusion.7.table_ref, s32[3]{0:T(128)S(1)} %copy-done.7, bf16[8,5,144,128]{3,2,1,0:T(8,128)(2,1)S(1)} %all-to-all-done.2.rest_0_), custom_call_target="tpu_custom_call" | custom-call | bytes 5898240 | tf_op jit(solution)/shard_map/route_back/pallas_call | solution.py:139
  192.6 3.7 %all-to-all-start.4 = ((bf16[16,5,144,128]{3,2,1,0:T(8,128)(2,1)}), bf16[16,5,144,128]{3,2,1,0:T(8,128)(2,1)S(1)}, u32[]{:S(2)}, u32[]{:S(2)}) async-start(bf16[16,5,144,128]{3,2,1,0:T(8,128)(2,1)} %copy-done), calls=%async_computation.4 | async-start | bytes 5898240 | tf_op jit(solution)/shard_map/all_to_all | solution.py:707
  196.4 15.0 %weight_terms.1 = (bf16[4,16,8,2688]{3,2,1,0:T(8,128)(2,1)}, bf16[4,16,8,2688]{3,2,1,0:T(8,128)(2,1)}) custom-call(s32[3]{0:T(128)} %copy-done.6, bf16[10,144,1024]{2,1,0:T(8,128)(2,1)} %get-tuple-element.129.normed, bf16[10,144,1024]{2,1,0:T(8,128)(2,1)} %get-tuple-element.130.scaled, bf16[10,144,1024]{2,1,0:T(8,128)(2,1)} %get-tuple-element.131.hidden, ...), custom_call_target="tpu_custom_call" | custom-call | flops 6039797760 | bytes 11796480 | tf_op jit(solution)/shard_map/weight_terms/pallas_call | solution.py:555
  212.0 3.2 %collective-permute-start.10 = (bf16[5,144,128]{2,1,0:T(8,128)(2,1)}, bf16[5,144,128]{2,1,0:T(8,128)(2,1)S(1)}, u32[]{:S(2)}, u32[]{:S(2)}) collective-permute-start(bf16[5,144,128]{2,1,0:T(8,128)(2,1)} %get-tuple-element.125), channel_id=1, source_target_pairs={{0,4},{1,5},{2,6},{3,7},{4,0},{5,1},{6,2},{7,3},{8,12},{9,13},{10,... | collective-permute-start | bytes 552968 | tf_op jit(solution)/shard_map/ppermute | solution.py:94
  215.2 2.9 collective-permute-start.12
  221.2 2.7 collective-permute-done.11.rest_5_
  225.8 3.6 %collective-permute-done.12.rest_6_ = bf16[5,144,128]{2,1,0:T(8,128)(2,1)S(1)} collective-permute-done((bf16[5,144,128]{2,1,0:T(8,128)(2,1)}, bf16[5,144,128]{2,1,0:T(8,128)(2,1)S(1)}, u32[]{:S(2)}, u32[]{:S(2)}) %collective-permute-start.12) | collective-permute-done | bytes 184352 | tf_op jit(solution)/shard_map/ppermute | solution.py:94
  232.3 4.6 %collective-permute-done.9.rest_3_ = bf16[5,144,128]{2,1,0:T(8,128)(2,1)S(1)} collective-permute-done((bf16[5,144,128]{2,1,0:T(8,128)(2,1)S(1)}, bf16[5,144,128]{2,1,0:T(8,128)(2,1)S(1)}, u32[]{:S(2)}, u32[]{:S(2)}) %collective-permute-start.9) | collective-permute-done | bytes 184352 | tf_op jit(solution)/shard_map/ppermute | solution.py:94
  237.0 3.3 %route_back.3 = bf16[16,5,144,128]{3,2,1,0:T(8,128)(2,1)S(1)} custom-call(s32[80]{0:T(128)S(1)} %select_reduce_fusion.7.table_ref, s32[3]{0:T(128)S(1)} %copy-done.8, bf16[5,144,128]{2,1,0:T(8,128)(2,1)S(1)} %copy-done.5, bf16[5,144,128]{2,1,0:T(8,128)(2,1)S(1)} %collective-permute-done.7.rest_1_, bf16[5,144,128]{2,1,0:T(8,128)(2,1)S(1)} %collective-permute-done.8.rest_2_, ...), custom_call_target="tpu_custom_call" | custom-call | bytes 5898240 | tf_op jit(solution)/shard_map/route_back/pallas_call | solution.py:139
  243.6 5.5 %all-to-all-start.5 = ((bf16[16,5,144,128]{3,2,1,0:T(8,128)(2,1)}), bf16[16,5,144,128]{3,2,1,0:T(8,128)(2,1)}, u32[]{:S(2)}, u32[]{:S(2)}) async-start(bf16[16,5,144,128]{3,2,1,0:T(8,128)(2,1)} %copy-done.1), calls=%async_computation.5 | async-start | bytes 5898240 | tf_op jit(solution)/shard_map/all_to_all | solution.py:707
  249.1 2.6 fusion.4
  252.0 2.5 collective-permute-start.16
  255.9 14.8 %collective-permute-done.15 = bf16[16,8,2688]{2,1,0:T(8,128)(2,1)S(1)} collective-permute-done((bf16[16,8,2688]{2,1,0:T(8,128)(2,1)S(1)}, bf16[16,8,2688]{2,1,0:T(8,128)(2,1)S(1)}, u32[]{:S(2)}, u32[]{:S(2)}) %collective-permute-start.15) | collective-permute-done | bytes 688160 | tf_op jit(solution)/shard_map/ppermute | solution.py:715
  270.7 13.9 %collective-permute-done.16 = bf16[16,8,2688]{2,1,0:T(8,128)(2,1)S(1)} collective-permute-done((bf16[16,8,2688]{2,1,0:T(8,128)(2,1)S(1)}, bf16[16,8,2688]{2,1,0:T(8,128)(2,1)S(1)}, u32[]{:S(2)}, u32[]{:S(2)}) %collective-permute-start.16) | collective-permute-done | bytes 688160 | tf_op jit(solution)/shard_map/ppermute | solution.py:715
  285.2 2.7 fusion.2
  287.8 5.6 %all-to-all-done.5.rest_1_ = bf16[16,5,144,128]{3,2,1,0:T(8,128)(2,1)} async-done(((bf16[16,5,144,128]{3,2,1,0:T(8,128)(2,1)}), bf16[16,5,144,128]{3,2,1,0:T(8,128)(2,1)}, u32[]{:S(2)}, u32[]{:S(2)}) %all-to-all-start.5) | async-done | bytes 2949152 | tf_op jit(solution)/shard_map/all_to_all | solution.py:707
  293.4 4.3 %all-to-all-start.6 = ((bf16[16,8,2688]{2,1,0:T(8,128)(2,1)}), bf16[16,8,2688]{2,1,0:T(8,128)(2,1)}, u32[]{:S(2)}, u32[]{:S(2)}) async-start(bf16[16,8,2688]{2,1,0:T(8,128)(2,1)} %fusion.2), calls=%async_computation.6 | async-start | bytes 1376256 | tf_op jit(solution)/shard_map/all_to_all | solution.py:718
  297.7 7.9 %unpack_and_spread.1 = bf16[48,24,24,128]{3,2,1,0:T(8,128)(2,1)} custom-call(s32[48]{0:T(128)S(1)} %copy-done.9, s32[48]{0:T(128)S(1)} %copy-done.10, bf16[16,5,144,128]{3,2,1,0:T(8,128)(2,1)S(1)} %all-to-all-done.4.rest_0_, bf16[16,5,144,128]{3,2,1,0:T(8,128)(2,1)} %all-to-all-done.5.rest_1_), custom_call_target="tpu_custom_call" | custom-call | bytes 8847360 | tf_op jit(solution)/shard_map/unpack_and_spread/pallas_call | solution.py:595
  305.6 4.4 %all-to-all-done.6 = bf16[16,8,2688]{2,1,0:T(8,128)(2,1)} async-done(((bf16[16,8,2688]{2,1,0:T(8,128)(2,1)}), bf16[16,8,2688]{2,1,0:T(8,128)(2,1)}, u32[]{:S(2)}, u32[]{:S(2)}) %all-to-all-start.6) | async-done | bytes 688160 | tf_op jit(solution)/shard_map/all_to_all | solution.py:718
  (117 shorter events, 51.7 us)
Async XLA Ops:
  15.4 51.6 %all-to-all-start = ((bf16[16,5,144,128]{3,2,1,0:T(8,128)(2,1)}), bf16[16,5,144,128]{3,2,1,0:T(8,128)(2,1)S(1)}, u32[]{:S(2)}, u32[]{:S(2)}) async-start(bf16[16,5,144,128]{3,2,1,0:T(8,128)(2,1)} %get-tuple-element.74), calls=%async_computation | async-start | bytes 5898240 | tf_op jit(solution)/shard_map/all_to_all | solution.py:687
  69.3 45.3 %all-to-all-start.1 = ((bf16[16,5,144,128]{3,2,1,0:T(8,128)(2,1)}), bf16[16,5,144,128]{3,2,1,0:T(8,128)(2,1)S(1)}, u32[]{:S(2)}, u32[]{:S(2)}) async-start(bf16[16,5,144,128]{3,2,1,0:T(8,128)(2,1)} %get-tuple-element.85), calls=%async_computation.1 | async-start | bytes 5898240 | tf_op jit(solution)/shard_map/all_to_all | solution.py:687
  74.2 43.6 %copy-start.6 = (s32[3]{0:T(128)}, s32[3]{0:T(128)S(1)}, u32[]{:S(2)}) copy-start(s32[3]{0:T(128)S(1)} %pad_add_fusion.info_ref) | copy-start | bytes 40
  79.6 6.8 %collective-permute-start = (bf16[5,144,128]{2,1,0:T(8,128)(2,1)S(1)}, bf16[5,144,128]{2,1,0:T(8,128)(2,1)S(1)}, u32[]{:S(2)}, u32[]{:S(2)}) collective-permute-start(bf16[5,144,128]{2,1,0:T(8,128)(2,1)S(1)} %get-tuple-element.77), channel_id=1, source_target_pairs={{0,1},{1,0},{2,3},{3,2},{4,5},{5,4},{6,7},{7,6},{8,9},{9,8},{10,11... | collective-permute-start | bytes 552968 | tf_op jit(solution)/shard_map/ppermute | solution.py:94
  79.6 9.5 %collective-permute-start.1 = (bf16[5,144,128]{2,1,0:T(8,128)(2,1)S(1)}, bf16[5,144,128]{2,1,0:T(8,128)(2,1)S(1)}, u32[]{:S(2)}, u32[]{:S(2)}) collective-permute-start(bf16[5,144,128]{2,1,0:T(8,128)(2,1)S(1)} %get-tuple-element.78), channel_id=1, source_target_pairs={{0,2},{1,3},{2,4},{3,5},{4,6},{5,7},{6,0},{7,1},{8,10},{9,11},{10,... | collective-permute-start | bytes 552968 | tf_op jit(solution)/shard_map/ppermute | solution.py:94
  81.5 37.5 %collective-permute-start.2 = (bf16[5,144,128]{2,1,0:T(8,128)(2,1)}, bf16[5,144,128]{2,1,0:T(8,128)(2,1)}, u32[]{:S(2)}, u32[]{:S(2)}) collective-permute-start(bf16[5,144,128]{2,1,0:T(8,128)(2,1)} %get-tuple-element.79), channel_id=1, source_target_pairs={{0,3},{1,2},{2,5},{3,4},{4,7},{5,6},{6,1},{7,0},{8,11},{9,10},{10,... | collective-permute-start | bytes 552968 | tf_op jit(solution)/shard_map/ppermute | solution.py:94
  83.3 35.7 %collective-permute-start.3 = (bf16[5,144,128]{2,1,0:T(8,128)(2,1)}, bf16[5,144,128]{2,1,0:T(8,128)(2,1)}, u32[]{:S(2)}, u32[]{:S(2)}) collective-permute-start(bf16[5,144,128]{2,1,0:T(8,128)(2,1)} %get-tuple-element.80), channel_id=1, source_target_pairs={{0,4},{1,5},{2,6},{3,7},{4,0},{5,1},{6,2},{7,3},{8,12},{9,13},{10,... | collective-permute-start | bytes 552968 | tf_op jit(solution)/shard_map/ppermute | solution.py:94
  85.3 33.8 %collective-permute-start.4 = (bf16[5,144,128]{2,1,0:T(8,128)(2,1)S(1)}, bf16[5,144,128]{2,1,0:T(8,128)(2,1)}, u32[]{:S(2)}, u32[]{:S(2)}) collective-permute-start(bf16[5,144,128]{2,1,0:T(8,128)(2,1)S(1)} %get-tuple-element.81), channel_id=1, source_target_pairs={{0,5},{1,4},{2,7},{3,6},{4,1},{5,0},{6,3},{7,2},{8,13},{9,12},{10,... | collective-permute-start | bytes 552968 | tf_op jit(solution)/shard_map/ppermute | solution.py:94
  86.4 32.6 %collective-permute-start.5 = (bf16[5,144,128]{2,1,0:T(8,128)(2,1)S(1)}, bf16[5,144,128]{2,1,0:T(8,128)(2,1)}, u32[]{:S(2)}, u32[]{:S(2)}) collective-permute-start(bf16[5,144,128]{2,1,0:T(8,128)(2,1)S(1)} %get-tuple-element.82), channel_id=1, source_target_pairs={{0,6},{1,7},{2,0},{3,1},{4,2},{5,3},{6,4},{7,5},{8,14},{9,15},{10,... | collective-permute-start | bytes 552968 | tf_op jit(solution)/shard_map/ppermute | solution.py:94
  89.8 29.2 %collective-permute-start.6 = (bf16[5,144,128]{2,1,0:T(8,128)(2,1)S(1)}, bf16[5,144,128]{2,1,0:T(8,128)(2,1)}, u32[]{:S(2)}, u32[]{:S(2)}) collective-permute-start(bf16[5,144,128]{2,1,0:T(8,128)(2,1)S(1)} %get-tuple-element.83), channel_id=1, source_target_pairs={{0,7},{1,6},{2,1},{3,0},{4,3},{5,2},{6,5},{7,4},{8,15},{9,14},{10,... | collective-permute-start | bytes 552968 | tf_op jit(solution)/shard_map/ppermute | solution.py:94
  119.1 32.7 %all-to-all-start.3 = ((bf16[8,5,144,128]{3,2,1,0:T(8,128)(2,1)}), bf16[8,5,144,128]{3,2,1,0:T(8,128)(2,1)S(1)}, u32[]{:S(2)}, u32[]{:S(2)}) async-start(bf16[8,5,144,128]{3,2,1,0:T(8,128)(2,1)} %copy-done.4), calls=%async_computation.3 | async-start | bytes 2949120 | tf_op jit(solution)/shard_map/all_to_all | solution.py:93
  151.8 34.8 %all-to-all-start.2 = ((bf16[8,5,144,128]{3,2,1,0:T(8,128)(2,1)}), bf16[8,5,144,128]{3,2,1,0:T(8,128)(2,1)S(1)}, u32[]{:S(2)}, u32[]{:S(2)}) async-start(bf16[8,5,144,128]{3,2,1,0:T(8,128)(2,1)} %get-tuple-element.104), calls=%async_computation.2 | async-start | bytes 2949120 | tf_op jit(solution)/shard_map/all_to_all | solution.py:93
  192.6 50.9 %all-to-all-start.4 = ((bf16[16,5,144,128]{3,2,1,0:T(8,128)(2,1)}), bf16[16,5,144,128]{3,2,1,0:T(8,128)(2,1)S(1)}, u32[]{:S(2)}, u32[]{:S(2)}) async-start(bf16[16,5,144,128]{3,2,1,0:T(8,128)(2,1)} %copy-done), calls=%async_computation.4 | async-start | bytes 5898240 | tf_op jit(solution)/shard_map/all_to_all | solution.py:707
  196.4 27.5 %copy-start.19 = (bf16[5,144,128]{2,1,0:T(8,128)(2,1)S(1)}, bf16[5,144,128]{2,1,0:T(8,128)(2,1)}, u32[]{:S(2)}) copy-start(bf16[5,144,128]{2,1,0:T(8,128)(2,1)} %get-tuple-element.123) | copy-start | bytes 552964
  196.4 32.9 %copy-start.18 = (bf16[5,144,128]{2,1,0:T(8,128)(2,1)S(1)}, bf16[5,144,128]{2,1,0:T(8,128)(2,1)}, u32[]{:S(2)}) copy-start(bf16[5,144,128]{2,1,0:T(8,128)(2,1)} %get-tuple-element.124) | copy-start | bytes 552964
  196.4 40.5 %copy-start.5 = (bf16[5,144,128]{2,1,0:T(8,128)(2,1)S(1)}, bf16[5,144,128]{2,1,0:T(8,128)(2,1)}, u32[]{:S(2)}) copy-start(bf16[5,144,128]{2,1,0:T(8,128)(2,1)} %get-tuple-element.121.rest_0_) | copy-start | bytes 552964
  196.4 40.5 %copy-start.8 = (s32[3]{0:T(128)S(1)}, s32[3]{0:T(128)}, u32[]{:S(2)}) copy-start(s32[3]{0:T(128)} %copy-done.6) | copy-start | bytes 40
  211.5 37.6 %collective-permute-start.14 = (bf16[4,16,8,2688]{3,2,1,0:T(8,128)(2,1)}, bf16[4,16,8,2688]{3,2,1,0:T(8,128)(2,1)}, u32[]{:S(2)}, u32[]{:S(2)}) collective-permute-start(bf16[4,16,8,2688]{3,2,1,0:T(8,128)(2,1)} %get-tuple-element.139), channel_id=1, source_target_pairs={{0,1},{1,0},{2,3},{3,2},{4,5},{5,4},{6,7},{7,6},{8,9},{9,8},{10,11... | collective-permute-start | bytes 8257544 | tf_op jit(solution)/shard_map/ppermute | solution.py:712
  212.0 9.2 %collective-permute-start.10 = (bf16[5,144,128]{2,1,0:T(8,128)(2,1)}, bf16[5,144,128]{2,1,0:T(8,128)(2,1)S(1)}, u32[]{:S(2)}, u32[]{:S(2)}) collective-permute-start(bf16[5,144,128]{2,1,0:T(8,128)(2,1)} %get-tuple-element.125), channel_id=1, source_target_pairs={{0,4},{1,5},{2,6},{3,7},{4,0},{5,1},{6,2},{7,3},{8,12},{9,13},{10,... | collective-permute-start | bytes 552968 | tf_op jit(solution)/shard_map/ppermute | solution.py:94
  215.2 8.7 %collective-permute-start.11 = (bf16[5,144,128]{2,1,0:T(8,128)(2,1)}, bf16[5,144,128]{2,1,0:T(8,128)(2,1)S(1)}, u32[]{:S(2)}, u32[]{:S(2)}) collective-permute-start(bf16[5,144,128]{2,1,0:T(8,128)(2,1)} %get-tuple-element.126), channel_id=1, source_target_pairs={{0,5},{1,4},{2,7},{3,6},{4,1},{5,0},{6,3},{7,2},{8,13},{9,12},{10,... | collective-permute-start | bytes 552968 | tf_op jit(solution)/shard_map/ppermute | solution.py:94
  215.2 14.1 %collective-permute-start.12 = (bf16[5,144,128]{2,1,0:T(8,128)(2,1)}, bf16[5,144,128]{2,1,0:T(8,128)(2,1)S(1)}, u32[]{:S(2)}, u32[]{:S(2)}) collective-permute-start(bf16[5,144,128]{2,1,0:T(8,128)(2,1)} %get-tuple-element.127), channel_id=1, source_target_pairs={{0,6},{1,7},{2,0},{3,1},{4,2},{5,3},{6,4},{7,5},{8,14},{9,15},{10,... | collective-permute-start | bytes 552968 | tf_op jit(solution)/shard_map/ppermute | solution.py:94
  218.1 14.1 %collective-permute-start.13 = (bf16[5,144,128]{2,1,0:T(8,128)(2,1)}, bf16[5,144,128]{2,1,0:T(8,128)(2,1)S(1)}, u32[]{:S(2)}, u32[]{:S(2)}) collective-permute-start(bf16[5,144,128]{2,1,0:T(8,128)(2,1)} %get-tuple-element.128), channel_id=1, source_target_pairs={{0,7},{1,6},{2,1},{3,0},{4,3},{5,2},{6,5},{7,4},{8,15},{9,14},{10,... | collective-permute-start | bytes 552968 | tf_op jit(solution)/shard_map/ppermute | solution.py:94
  221.2 11.0 %collective-permute-start.7 = (bf16[5,144,128]{2,1,0:T(8,128)(2,1)S(1)}, bf16[5,144,128]{2,1,0:T(8,128)(2,1)S(1)}, u32[]{:S(2)}, u32[]{:S(2)}) collective-permute-start(bf16[5,144,128]{2,1,0:T(8,128)(2,1)S(1)} %copy-done.20), channel_id=1, source_target_pairs={{0,1},{1,0},{2,3},{3,2},{4,5},{5,4},{6,7},{7,6},{8,9},{9,8},{10,11... | collective-permute-start | bytes 552968 | tf_op jit(solution)/shard_map/ppermute | solution.py:94
  223.9 8.4 %collective-permute-start.8 = (bf16[5,144,128]{2,1,0:T(8,128)(2,1)S(1)}, bf16[5,144,128]{2,1,0:T(8,128)(2,1)S(1)}, u32[]{:S(2)}, u32[]{:S(2)}) collective-permute-start(bf16[5,144,128]{2,1,0:T(8,128)(2,1)S(1)} %copy-done.19), channel_id=1, source_target_pairs={{0,2},{1,3},{2,4},{3,5},{4,6},{5,7},{6,0},{7,1},{8,10},{9,11},{10,... | collective-permute-start | bytes 552968 | tf_op jit(solution)/shard_map/ppermute | solution.py:94
  229.4 7.6 %collective-permute-start.9 = (bf16[5,144,128]{2,1,0:T(8,128)(2,1)S(1)}, bf16[5,144,128]{2,1,0:T(8,128)(2,1)S(1)}, u32[]{:S(2)}, u32[]{:S(2)}) collective-permute-start(bf16[5,144,128]{2,1,0:T(8,128)(2,1)S(1)} %copy-done.18), channel_id=1, source_target_pairs={{0,3},{1,2},{2,5},{3,4},{4,7},{5,6},{6,1},{7,0},{8,11},{9,10},{10,... | collective-permute-start | bytes 552968 | tf_op jit(solution)/shard_map/ppermute | solution.py:94
  243.6 49.8 %all-to-all-start.5 = ((bf16[16,5,144,128]{3,2,1,0:T(8,128)(2,1)}), bf16[16,5,144,128]{3,2,1,0:T(8,128)(2,1)}, u32[]{:S(2)}, u32[]{:S(2)}) async-start(bf16[16,5,144,128]{3,2,1,0:T(8,128)(2,1)} %copy-done.1), calls=%async_computation.5 | async-start | bytes 5898240 | tf_op jit(solution)/shard_map/all_to_all | solution.py:707
  251.7 19.0 %collective-permute-start.15 = (bf16[16,8,2688]{2,1,0:T(8,128)(2,1)S(1)}, bf16[16,8,2688]{2,1,0:T(8,128)(2,1)S(1)}, u32[]{:S(2)}, u32[]{:S(2)}) collective-permute-start(bf16[16,8,2688]{2,1,0:T(8,128)(2,1)S(1)} %get-tuple-element.150), channel_id=1, source_target_pairs={{0,2},{1,3},{2,4},{3,5},{4,6},{5,7},{6,0},{7,1},{8,10},{9,11},{10,... | collective-permute-start | bytes 2064392 | tf_op jit(solution)/shard_map/ppermute | solution.py:715
  252.0 32.6 %collective-permute-start.16 = (bf16[16,8,2688]{2,1,0:T(8,128)(2,1)S(1)}, bf16[16,8,2688]{2,1,0:T(8,128)(2,1)S(1)}, u32[]{:S(2)}, u32[]{:S(2)}) collective-permute-start(bf16[16,8,2688]{2,1,0:T(8,128)(2,1)S(1)} %get-tuple-element.152), channel_id=1, source_target_pairs={{0,4},{1,5},{2,6},{3,7},{4,0},{5,1},{6,2},{7,3},{8,12},{9,13},{10,... | collective-permute-start | bytes 2064392 | tf_op jit(solution)/shard_map/ppermute | solution.py:715
  254.6 43.1 %copy-start.9 = (s32[48]{0:T(128)S(1)}, s32[48]{0:T(128)}, u32[]{:S(2)}) copy-start(s32[48]{0:T(128)} %get-tuple-element.147.own_ref) | copy-start | bytes 580
  254.6 43.1 %copy-start.10 = (s32[48]{0:T(128)S(1)}, s32[48]{0:T(128)}, u32[]{:S(2)}) copy-start(s32[48]{0:T(128)} %and_select_fusion.pos_ref) | copy-start | bytes 580
  254.6 30.6 %collective-permute-start.17 = (bf16[16,8,2688]{2,1,0:T(8,128)(2,1)S(1)}, bf16[16,8,2688]{2,1,0:T(8,128)(2,1)S(1)}, u32[]{:S(2)}, u32[]{:S(2)}) collective-permute-start(bf16[16,8,2688]{2,1,0:T(8,128)(2,1)S(1)} %get-tuple-element.151), channel_id=1, source_target_pairs={{0,6},{1,7},{2,0},{3,1},{4,2},{5,3},{6,4},{7,5},{8,14},{9,15},{10,... | collective-permute-start | bytes 2064392 | tf_op jit(solution)/shard_map/ppermute | solution.py:715
  293.4 16.6 %all-to-all-start.6 = ((bf16[16,8,2688]{2,1,0:T(8,128)(2,1)}), bf16[16,8,2688]{2,1,0:T(8,128)(2,1)}, u32[]{:S(2)}, u32[]{:S(2)}) async-start(bf16[16,8,2688]{2,1,0:T(8,128)(2,1)} %fusion.2), calls=%async_computation.6 | async-start | bytes 1376256 | tf_op jit(solution)/shard_map/all_to_all | solution.py:718
  (16 other events, 92.2 us)

commit v6 on v5

--- a/solution.py
+++ b/solution.py
@@ -56,7 +56,7 @@
 def pool_and_pack(tiles, own, pos, groups, slots):
     count, grid, _, channels = tiles.shape
     cells = grid * grid // 4
-    per = 4
+    per = 8
     steps = count // per
     made = jax.ShapeDtypeStruct((groups, slots, cells, channels), BF16)
     return pl.pallas_call(
@@ -608,26 +608,19 @@
     )(own, pos, *arrived)
 
 
-def before(table):
-    groups = table.shape[1]
-    index = jnp.arange(groups, dtype=jnp.int32)
-    lower = index[None, :] < index[:, None]
-    return jnp.sum(jnp.where(lower[None], table[:, None, :], 0), axis=2, dtype=jnp.int32)
-
-
 def routing(counts, owners, ranks, group_id, local_tiles, capacity):
     groups = counts.shape[0]
-    start = before(counts)
     flat_counts, flat_owners, flat_ranks = counts.reshape(-1), owners.reshape(-1), ranks.reshape(-1)
-    ahead = (flat_owners[:, None] == flat_owners[None, :]) & (flat_ranks[None, :] < flat_ranks[:, None])
-    offset = jnp.sum(jnp.where(ahead, flat_counts[None, :], 0), axis=1, dtype=jnp.int32).reshape(groups, groups)
     sources = jnp.arange(groups, dtype=jnp.int32)
     mine = (sources == group_id)[:, None]
 
     def row(table):
         return jnp.sum(jnp.where(mine, table, 0), axis=0, dtype=jnp.int32)
 
-    owner_row, start_row, offset_row = row(owners), row(start), row(offset)
+    owner_row, rank_row, count_row = row(owners), row(ranks), row(counts)
+    start_row = jnp.sum(jnp.where(sources[None, :] < sources[:, None], count_row[None, :], 0), axis=1, dtype=jnp.int32)
+    ahead = (owner_row[:, None] == flat_owners[None, :]) & (flat_ranks[None, :] < rank_row[:, None])
+    offset_row = jnp.sum(jnp.where(ahead, flat_counts[None, :], 0), axis=1, dtype=jnp.int32)
     ids = jnp.arange(local_tiles, dtype=jnp.int32)
     member = jnp.sum((start_row[None, :] <= ids[:, None]).astype(jnp.int32), axis=1, dtype=jnp.int32) - 1
     which = member[:, None] == sources[None, :]
@@ -635,7 +628,9 @@
     slot = jnp.sum(jnp.where(which, (offset_row - start_row)[None, :], 0), axis=1, dtype=jnp.int32) + ids
     arriving = owners == group_id
     recv_count = jnp.sum(jnp.where(arriving, counts, 0), axis=1, dtype=jnp.int32)
-    recv_offset = jnp.sum(jnp.where(arriving, offset, 0), axis=1, dtype=jnp.int32)
+    recv_rank = jnp.sum(jnp.where(arriving, ranks, 0), axis=1, dtype=jnp.int32)
+    earlier = recv_rank[None, :] < recv_rank[:, None]
+    recv_offset = jnp.sum(jnp.where(earlier, recv_count[None, :], 0), axis=1, dtype=jnp.int32)
     positions = jnp.arange(capacity, dtype=jnp.int32)
     inside = (positions[:, None] >= recv_offset[None, :]) & (
         positions[:, None] < (recv_offset + recv_count)[None, :]

time: 316 us -> 312 us (0.987)
  Pallas kernels: 98.7 us -> 90.5 us
    pallas_call x4, Pallas kernels: 12.7 us -> 6.94 us  [route(): pl.pallas_call(functools.partial(route_kernel, chunk, per, columns, back)...]
  transfers between devices with their start and end apart: 25 -> 25, of which waited for: 15 -> 15; matrix products, arithmetic and copies ran while one was open for 6% -> 7% of each run, Pallas kernels for 28% -> 27%
where the time goes in v6:
time: 312 us; the launch traced here: 310 us
  waiting for transfers between devices  117 us (38%)
  Pallas kernels  90.5 us (29%)
  starting transfers between devices  60.9 us (20%)
  local copies, waits for them, and re-layouts  30 us (10%)
  other arithmetic  11.1 us (4%)
    all_to_all x2, waiting for transfers between devices, local(): lax.all_to_all(send, 'enc', split_axis=0, concat_axis=0, tiled=True)  57.5 us
    pallas_call x2, Pallas kernels, run_block(): pl.pallas_call(functools.partial(block_kernel, chunk, side, columns, len(...  54.8 us
    ppermute x3, waiting for transfers between devices, local(): lax.ppermute(pair[k], 'abs', partner_pairs(2 * k, columns))  29.4 us
    unnamed x51, local copies, waits for them, and re-layouts  20.3 us
    ppermute x14, starting transfers between devices, exchange(): lax.ppermute(parts[k], 'abs', partner_pairs(k, columns))  18.3 us
    ppermute x14, waiting for transfers between devices, exchange(): lax.ppermute(parts[k], 'abs', partner_pairs(k, columns))  17.2 us
    pallas_call x1, Pallas kernels, weight_terms(): pl.pallas_call(functools.partial(weights_kernel, len(small), columns), gr...  15 us
    all_to_all x2, starting transfers between devices, local(): lax.all_to_all(back, 'enc', split_axis=0, concat_axis=0, tiled=True)  12.2 us
  transfers between devices with their start and end apart: 25, of which 15 were waited for; matrix products, arithmetic and copies ran while one was open for 7% of the time, Pallas kernels for 27%

profile of v6, /device:TPU:0, one launch (start us, length us, event | category | flops | bytes accessed | tf_op | source)
XLA Modules:
  0.0 310.3 jit_solution(119726188543940065)
XLA Ops:
  6.0 5.8 %pool_and_pack.1 = (bf16[16,5,144,128]{3,2,1,0:T(8,128)(2,1)}, bf16[16,5,144,128]{3,2,1,0:T(8,128)(2,1)}) custom-call(s32[48]{0:T(128)} %get-tuple-element.149.own_ref, s32[48]{0:T(128)} %and_select_fusion.pos_ref, bf16[48,24,24,128]{3,2,1,0:T(8,128)(2,1)} %tiles_ref.1), custom_call_target="tpu_custom_call" | custom-call | flops 3538944 | bytes 10616832 | tf_op jit(solution)/shard_map/pool_and_pack/pallas_call | solution.py:62
  11.8 7.1 %all-to-all-start = ((bf16[16,5,144,128]{3,2,1,0:T(8,128)(2,1)}), bf16[16,5,144,128]{3,2,1,0:T(8,128)(2,1)S(1)}, u32[]{:S(2)}, u32[]{:S(2)}) async-start(bf16[16,5,144,128]{3,2,1,0:T(8,128)(2,1)} %get-tuple-element.74), calls=%async_computation | async-start | bytes 5898240 | tf_op jit(solution)/shard_map/all_to_all | solution.py:682
  18.9 4.0 %copy.36 = bf16[1024,1024]{0,1:T(8,128)(2,1)} copy(bf16[1024,1024]{1,0:T(8,128)(2,1)} %rest_2_) | data formatting | bytes 4194304 | tf_op args[1]
  22.9 4.0 %copy.37 = bf16[1024,1024]{0,1:T(8,128)(2,1)} copy(bf16[1024,1024]{1,0:T(8,128)(2,1)} %rest_3_) | data formatting | bytes 4194304 | tf_op args[2]
  27.9 2.0 copy.39
  30.6 32.8 %all-to-all-done.rest_0_ = bf16[16,5,144,128]{3,2,1,0:T(8,128)(2,1)S(1)} async-done(((bf16[16,5,144,128]{3,2,1,0:T(8,128)(2,1)}), bf16[16,5,144,128]{3,2,1,0:T(8,128)(2,1)S(1)}, u32[]{:S(2)}, u32[]{:S(2)}) %all-to-all-start) | async-done | bytes 2949152 | tf_op jit(solution)/shard_map/all_to_all | solution.py:682
  65.7 4.2 %all-to-all-start.1 = ((bf16[16,5,144,128]{3,2,1,0:T(8,128)(2,1)}), bf16[16,5,144,128]{3,2,1,0:T(8,128)(2,1)S(1)}, u32[]{:S(2)}, u32[]{:S(2)}) async-start(bf16[16,5,144,128]{3,2,1,0:T(8,128)(2,1)} %get-tuple-element.85), calls=%async_computation.1 | async-start | bytes 5898240 | tf_op jit(solution)/shard_map/all_to_all | solution.py:682
  86.3 24.7 %all-to-all-done.1.rest_0_ = bf16[16,5,144,128]{3,2,1,0:T(8,128)(2,1)S(1)} async-done(((bf16[16,5,144,128]{3,2,1,0:T(8,128)(2,1)}), bf16[16,5,144,128]{3,2,1,0:T(8,128)(2,1)S(1)}, u32[]{:S(2)}, u32[]{:S(2)}) %all-to-all-start.1) | async-done | bytes 2949152 | tf_op jit(solution)/shard_map/all_to_all | solution.py:682
  113.8 5.3 %all-to-all-start.3 = ((bf16[8,5,144,128]{3,2,1,0:T(8,128)(2,1)}), bf16[8,5,144,128]{3,2,1,0:T(8,128)(2,1)S(1)}, u32[]{:S(2)}, u32[]{:S(2)}) async-start(bf16[8,5,144,128]{3,2,1,0:T(8,128)(2,1)} %copy-done.4), calls=%async_computation.3 | async-start | bytes 2949120 | tf_op jit(solution)/shard_map/all_to_all | solution.py:93
  119.2 27.4 %block_0.1 = (bf16[10,144,1024]{2,1,0:T(8,128)(2,1)}, bf16[10,144,1024]{2,1,0:T(8,128)(2,1)}, bf16[10,144,1024]{2,1,0:T(8,128)(2,1)}, bf16[10,144,1024]{2,1,0:T(...) custom-call(s32[3]{0:T(128)} %copy-done.6, ...), custom_call_target="tpu_custom_call" | custom-call | flops 6039797760 | bytes 20185088 | tf_op jit(solution)/shard_map/block_0/pallas_call | solution.py:437
  146.6 5.1 %all-to-all-start.2 = ((bf16[8,5,144,128]{3,2,1,0:T(8,128)(2,1)}), bf16[8,5,144,128]{3,2,1,0:T(8,128)(2,1)S(1)}, u32[]{:S(2)}, u32[]{:S(2)}) async-start(bf16[8,5,144,128]{3,2,1,0:T(8,128)(2,1)} %get-tuple-element.104), calls=%async_computation.2 | async-start | bytes 2949120 | tf_op jit(solution)/shard_map/all_to_all | solution.py:93
  154.3 27.5 %block_1.1 = (bf16[10,144,1024]{2,1,0:T(8,128)(2,1)}, bf16[10,144,1024]{2,1,0:T(8,128)(2,1)}, bf16[10,144,1024]{2,1,0:T(8,128)(2,1)}, bf16[10,144,1024]{2,1,0:T(...) custom-call(s32[3]{0:T(128)} %copy-done.6, ...), custom_call_target="tpu_custom_call", output_to_operand_aliasing={{0}: (13, {}), {1}: (14, {}), {2}: (15, {}), {3}: (16, {})} | custom-call | flops 6039797760 | bytes 20185088 | tf_op jit(solution)/shard_map/block_1/pallas_call | solution.py:437
  186.3 6.2 %all-to-all-start.4 = ((bf16[16,5,144,128]{3,2,1,0:T(8,128)(2,1)}), bf16[16,5,144,128]{3,2,1,0:T(8,128)(2,1)S(1)}, u32[]{:S(2)}, u32[]{:S(2)}) async-start(bf16[16,5,144,128]{3,2,1,0:T(8,128)(2,1)} %copy-done), calls=%async_computation.4 | async-start | bytes 5898240 | tf_op jit(solution)/shard_map/all_to_all | solution.py:702
  192.5 15.0 %weight_terms.1 = (bf16[4,16,8,2688]{3,2,1,0:T(8,128)(2,1)}, bf16[4,16,8,2688]{3,2,1,0:T(8,128)(2,1)}) custom-call(s32[3]{0:T(128)} %copy-done.6, bf16[10,144,1024]{2,1,0:T(8,128)(2,1)} %get-tuple-element.129.normed, bf16[10,144,1024]{2,1,0:T(8,128)(2,1)} %get-tuple-element.130.scaled, bf16[10,144,1024]{2,1,0:T(8,128)(2,1)} %get-tuple-element.131.hidden, ...), custom_call_target="tpu_custom_call" | custom-call | flops 6039797760 | bytes 11796480 | tf_op jit(solution)/shard_map/weight_terms/pallas_call | solution.py:555
  207.9 3.4 %collective-permute-start.10 = (bf16[5,144,128]{2,1,0:T(8,128)(2,1)}, bf16[5,144,128]{2,1,0:T(8,128)(2,1)S(1)}, u32[]{:S(2)}, u32[]{:S(2)}) collective-permute-start(bf16[5,144,128]{2,1,0:T(8,128)(2,1)} %get-tuple-element.125), channel_id=1, source_target_pairs={{0,4},{1,5},{2,6},{3,7},{4,0},{5,1},{6,2},{7,3},{8,12},{9,13},{10,... | collective-permute-start | bytes 552968 | tf_op jit(solution)/shard_map/ppermute | solution.py:94
  211.3 3.0 collective-permute-start.12
  214.8 2.2 collective-permute-done.10.rest_4_
  217.0 3.3 %collective-permute-done.11.rest_5_ = bf16[5,144,128]{2,1,0:T(8,128)(2,1)S(1)} collective-permute-done((bf16[5,144,128]{2,1,0:T(8,128)(2,1)}, bf16[5,144,128]{2,1,0:T(8,128)(2,1)S(1)}, u32[]{:S(2)}, u32[]{:S(2)}) %collective-permute-start.11) | collective-permute-done | bytes 184352 | tf_op jit(solution)/shard_map/ppermute | solution.py:94
  222.0 3.4 %collective-permute-done.12.rest_6_ = bf16[5,144,128]{2,1,0:T(8,128)(2,1)S(1)} collective-permute-done((bf16[5,144,128]{2,1,0:T(8,128)(2,1)}, bf16[5,144,128]{2,1,0:T(8,128)(2,1)S(1)}, u32[]{:S(2)}, u32[]{:S(2)}) %collective-permute-start.12) | collective-permute-done | bytes 184352 | tf_op jit(solution)/shard_map/ppermute | solution.py:94
  226.0 2.4 collective-permute-done.13.rest_7_
  229.0 4.1 %collective-permute-done.9.rest_3_ = bf16[5,144,128]{2,1,0:T(8,128)(2,1)S(1)} collective-permute-done((bf16[5,144,128]{2,1,0:T(8,128)(2,1)S(1)}, bf16[5,144,128]{2,1,0:T(8,128)(2,1)S(1)}, u32[]{:S(2)}, u32[]{:S(2)}) %collective-permute-start.9) | collective-permute-done | bytes 184352 | tf_op jit(solution)/shard_map/ppermute | solution.py:94
  236.4 2.6 all-to-all-done.4.rest_0_
  239.0 6.0 %all-to-all-start.5 = ((bf16[16,5,144,128]{3,2,1,0:T(8,128)(2,1)}), bf16[16,5,144,128]{3,2,1,0:T(8,128)(2,1)}, u32[]{:S(2)}, u32[]{:S(2)}) async-start(bf16[16,5,144,128]{3,2,1,0:T(8,128)(2,1)} %copy-done.1), calls=%async_computation.5 | async-start | bytes 5898240 | tf_op jit(solution)/shard_map/all_to_all | solution.py:702
  245.0 2.6 fusion.4
  247.9 2.7 collective-permute-start.16
  251.7 14.9 %collective-permute-done.15 = bf16[16,8,2688]{2,1,0:T(8,128)(2,1)S(1)} collective-permute-done((bf16[16,8,2688]{2,1,0:T(8,128)(2,1)S(1)}, bf16[16,8,2688]{2,1,0:T(8,128)(2,1)S(1)}, u32[]{:S(2)}, u32[]{:S(2)}) %collective-permute-start.15) | collective-permute-done | bytes 688160 | tf_op jit(solution)/shard_map/ppermute | solution.py:710
  266.5 14.1 %collective-permute-done.16 = bf16[16,8,2688]{2,1,0:T(8,128)(2,1)S(1)} collective-permute-done((bf16[16,8,2688]{2,1,0:T(8,128)(2,1)S(1)}, bf16[16,8,2688]{2,1,0:T(8,128)(2,1)S(1)}, u32[]{:S(2)}, u32[]{:S(2)}) %collective-permute-start.16) | collective-permute-done | bytes 688160 | tf_op jit(solution)/shard_map/ppermute | solution.py:710
  281.1 2.7 fusion.2
  283.7 5.6 %all-to-all-done.5.rest_1_ = bf16[16,5,144,128]{3,2,1,0:T(8,128)(2,1)} async-done(((bf16[16,5,144,128]{3,2,1,0:T(8,128)(2,1)}), bf16[16,5,144,128]{3,2,1,0:T(8,128)(2,1)}, u32[]{:S(2)}, u32[]{:S(2)}) %all-to-all-start.5) | async-done | bytes 2949152 | tf_op jit(solution)/shard_map/all_to_all | solution.py:702
  289.3 4.3 %all-to-all-start.6 = ((bf16[16,8,2688]{2,1,0:T(8,128)(2,1)}), bf16[16,8,2688]{2,1,0:T(8,128)(2,1)}, u32[]{:S(2)}, u32[]{:S(2)}) async-start(bf16[16,8,2688]{2,1,0:T(8,128)(2,1)} %fusion.2), calls=%async_computation.6 | async-start | bytes 1376256 | tf_op jit(solution)/shard_map/all_to_all | solution.py:713
  293.6 7.9 %unpack_and_spread.1 = bf16[48,24,24,128]{3,2,1,0:T(8,128)(2,1)} custom-call(s32[48]{0:T(128)S(1)} %copy-done.9, s32[48]{0:T(128)S(1)} %copy-done.10, bf16[16,5,144,128]{3,2,1,0:T(8,128)(2,1)S(1)} %all-to-all-done.4.rest_0_, bf16[16,5,144,128]{3,2,1,0:T(8,128)(2,1)} %all-to-all-done.5.rest_1_), custom_call_target="tpu_custom_call" | custom-call | bytes 8847360 | tf_op jit(solution)/shard_map/unpack_and_spread/pallas_call | solution.py:595
  301.5 4.4 %all-to-all-done.6 = bf16[16,8,2688]{2,1,0:T(8,128)(2,1)} async-done(((bf16[16,8,2688]{2,1,0:T(8,128)(2,1)}), bf16[16,8,2688]{2,1,0:T(8,128)(2,1)}, u32[]{:S(2)}, u32[]{:S(2)}) %all-to-all-start.6) | async-done | bytes 688160 | tf_op jit(solution)/shard_map/all_to_all | solution.py:713
  (116 shorter events, 48.8 us)
Async XLA Ops:
  11.8 51.6 %all-to-all-start = ((bf16[16,5,144,128]{3,2,1,0:T(8,128)(2,1)}), bf16[16,5,144,128]{3,2,1,0:T(8,128)(2,1)S(1)}, u32[]{:S(2)}, u32[]{:S(2)}) async-start(bf16[16,5,144,128]{3,2,1,0:T(8,128)(2,1)} %get-tuple-element.74), calls=%async_computation | async-start | bytes 5898240 | tf_op jit(solution)/shard_map/all_to_all | solution.py:682
  65.7 45.3 %all-to-all-start.1 = ((bf16[16,5,144,128]{3,2,1,0:T(8,128)(2,1)}), bf16[16,5,144,128]{3,2,1,0:T(8,128)(2,1)S(1)}, u32[]{:S(2)}, u32[]{:S(2)}) async-start(bf16[16,5,144,128]{3,2,1,0:T(8,128)(2,1)} %get-tuple-element.85), calls=%async_computation.1 | async-start | bytes 5898240 | tf_op jit(solution)/shard_map/all_to_all | solution.py:682
  70.8 41.8 %copy-start.6 = (s32[3]{0:T(128)}, s32[3]{0:T(128)S(1)}, u32[]{:S(2)}) copy-start(s32[3]{0:T(128)S(1)} %pad_add_fusion.info_ref) | copy-start | bytes 40
  75.2 6.6 %collective-permute-start = (bf16[5,144,128]{2,1,0:T(8,128)(2,1)S(1)}, bf16[5,144,128]{2,1,0:T(8,128)(2,1)S(1)}, u32[]{:S(2)}, u32[]{:S(2)}) collective-permute-start(bf16[5,144,128]{2,1,0:T(8,128)(2,1)S(1)} %get-tuple-element.77), channel_id=1, source_target_pairs={{0,1},{1,0},{2,3},{3,2},{4,5},{5,4},{6,7},{7,6},{8,9},{9,8},{10,11... | collective-permute-start | bytes 552968 | tf_op jit(solution)/shard_map/ppermute | solution.py:94
  75.3 9.4 %collective-permute-start.1 = (bf16[5,144,128]{2,1,0:T(8,128)(2,1)S(1)}, bf16[5,144,128]{2,1,0:T(8,128)(2,1)S(1)}, u32[]{:S(2)}, u32[]{:S(2)}) collective-permute-start(bf16[5,144,128]{2,1,0:T(8,128)(2,1)S(1)} %get-tuple-element.78), channel_id=1, source_target_pairs={{0,2},{1,3},{2,4},{3,5},{4,6},{5,7},{6,0},{7,1},{8,10},{9,11},{10,... | collective-permute-start | bytes 552968 | tf_op jit(solution)/shard_map/ppermute | solution.py:94
  77.2 36.6 %collective-permute-start.2 = (bf16[5,144,128]{2,1,0:T(8,128)(2,1)}, bf16[5,144,128]{2,1,0:T(8,128)(2,1)}, u32[]{:S(2)}, u32[]{:S(2)}) collective-permute-start(bf16[5,144,128]{2,1,0:T(8,128)(2,1)} %get-tuple-element.79), channel_id=1, source_target_pairs={{0,3},{1,2},{2,5},{3,4},{4,7},{5,6},{6,1},{7,0},{8,11},{9,10},{10,... | collective-permute-start | bytes 552968 | tf_op jit(solution)/shard_map/ppermute | solution.py:94
  78.7 35.1 %collective-permute-start.3 = (bf16[5,144,128]{2,1,0:T(8,128)(2,1)}, bf16[5,144,128]{2,1,0:T(8,128)(2,1)}, u32[]{:S(2)}, u32[]{:S(2)}) collective-permute-start(bf16[5,144,128]{2,1,0:T(8,128)(2,1)} %get-tuple-element.80), channel_id=1, source_target_pairs={{0,4},{1,5},{2,6},{3,7},{4,0},{5,1},{6,2},{7,3},{8,12},{9,13},{10,... | collective-permute-start | bytes 552968 | tf_op jit(solution)/shard_map/ppermute | solution.py:94
  80.7 33.1 %collective-permute-start.4 = (bf16[5,144,128]{2,1,0:T(8,128)(2,1)S(1)}, bf16[5,144,128]{2,1,0:T(8,128)(2,1)}, u32[]{:S(2)}, u32[]{:S(2)}) collective-permute-start(bf16[5,144,128]{2,1,0:T(8,128)(2,1)S(1)} %get-tuple-element.81), channel_id=1, source_target_pairs={{0,5},{1,4},{2,7},{3,6},{4,1},{5,0},{6,3},{7,2},{8,13},{9,12},{10,... | collective-permute-start | bytes 552968 | tf_op jit(solution)/shard_map/ppermute | solution.py:94
  81.8 32.0 %collective-permute-start.5 = (bf16[5,144,128]{2,1,0:T(8,128)(2,1)S(1)}, bf16[5,144,128]{2,1,0:T(8,128)(2,1)}, u32[]{:S(2)}, u32[]{:S(2)}) collective-permute-start(bf16[5,144,128]{2,1,0:T(8,128)(2,1)S(1)} %get-tuple-element.82), channel_id=1, source_target_pairs={{0,6},{1,7},{2,0},{3,1},{4,2},{5,3},{6,4},{7,5},{8,14},{9,15},{10,... | collective-permute-start | bytes 552968 | tf_op jit(solution)/shard_map/ppermute | solution.py:94
  85.3 28.5 %collective-permute-start.6 = (bf16[5,144,128]{2,1,0:T(8,128)(2,1)S(1)}, bf16[5,144,128]{2,1,0:T(8,128)(2,1)}, u32[]{:S(2)}, u32[]{:S(2)}) collective-permute-start(bf16[5,144,128]{2,1,0:T(8,128)(2,1)S(1)} %get-tuple-element.83), channel_id=1, source_target_pairs={{0,7},{1,6},{2,1},{3,0},{4,3},{5,2},{6,5},{7,4},{8,15},{9,14},{10,... | collective-permute-start | bytes 552968 | tf_op jit(solution)/shard_map/ppermute | solution.py:94
  113.8 32.7 %all-to-all-start.3 = ((bf16[8,5,144,128]{3,2,1,0:T(8,128)(2,1)}), bf16[8,5,144,128]{3,2,1,0:T(8,128)(2,1)S(1)}, u32[]{:S(2)}, u32[]{:S(2)}) async-start(bf16[8,5,144,128]{3,2,1,0:T(8,128)(2,1)} %copy-done.4), calls=%async_computation.3 | async-start | bytes 2949120 | tf_op jit(solution)/shard_map/all_to_all | solution.py:93
  146.6 35.2 %all-to-all-start.2 = ((bf16[8,5,144,128]{3,2,1,0:T(8,128)(2,1)}), bf16[8,5,144,128]{3,2,1,0:T(8,128)(2,1)S(1)}, u32[]{:S(2)}, u32[]{:S(2)}) async-start(bf16[8,5,144,128]{3,2,1,0:T(8,128)(2,1)} %get-tuple-element.104), calls=%async_computation.2 | async-start | bytes 2949120 | tf_op jit(solution)/shard_map/all_to_all | solution.py:93
  186.3 52.6 %all-to-all-start.4 = ((bf16[16,5,144,128]{3,2,1,0:T(8,128)(2,1)}), bf16[16,5,144,128]{3,2,1,0:T(8,128)(2,1)S(1)}, u32[]{:S(2)}, u32[]{:S(2)}) async-start(bf16[16,5,144,128]{3,2,1,0:T(8,128)(2,1)} %copy-done), calls=%async_computation.4 | async-start | bytes 5898240 | tf_op jit(solution)/shard_map/all_to_all | solution.py:702
  192.5 27.8 %copy-start.19 = (bf16[5,144,128]{2,1,0:T(8,128)(2,1)S(1)}, bf16[5,144,128]{2,1,0:T(8,128)(2,1)}, u32[]{:S(2)}) copy-start(bf16[5,144,128]{2,1,0:T(8,128)(2,1)} %get-tuple-element.123) | copy-start | bytes 552964
  192.5 32.9 %copy-start.18 = (bf16[5,144,128]{2,1,0:T(8,128)(2,1)S(1)}, bf16[5,144,128]{2,1,0:T(8,128)(2,1)}, u32[]{:S(2)}) copy-start(bf16[5,144,128]{2,1,0:T(8,128)(2,1)} %get-tuple-element.124) | copy-start | bytes 552964
  192.5 40.6 %copy-start.5 = (bf16[5,144,128]{2,1,0:T(8,128)(2,1)S(1)}, bf16[5,144,128]{2,1,0:T(8,128)(2,1)}, u32[]{:S(2)}) copy-start(bf16[5,144,128]{2,1,0:T(8,128)(2,1)} %get-tuple-element.121.rest_0_) | copy-start | bytes 552964
  192.5 40.6 %copy-start.8 = (s32[3]{0:T(128)S(1)}, s32[3]{0:T(128)}, u32[]{:S(2)}) copy-start(s32[3]{0:T(128)} %copy-done.6) | copy-start | bytes 40
  207.6 37.4 %collective-permute-start.14 = (bf16[4,16,8,2688]{3,2,1,0:T(8,128)(2,1)}, bf16[4,16,8,2688]{3,2,1,0:T(8,128)(2,1)}, u32[]{:S(2)}, u32[]{:S(2)}) collective-permute-start(bf16[4,16,8,2688]{3,2,1,0:T(8,128)(2,1)} %get-tuple-element.139), channel_id=1, source_target_pairs={{0,1},{1,0},{2,3},{3,2},{4,5},{5,4},{6,7},{7,6},{8,9},{9,8},{10,11... | collective-permute-start | bytes 8257544 | tf_op jit(solution)/shard_map/ppermute | solution.py:707
  207.9 9.1 %collective-permute-start.10 = (bf16[5,144,128]{2,1,0:T(8,128)(2,1)}, bf16[5,144,128]{2,1,0:T(8,128)(2,1)S(1)}, u32[]{:S(2)}, u32[]{:S(2)}) collective-permute-start(bf16[5,144,128]{2,1,0:T(8,128)(2,1)} %get-tuple-element.125), channel_id=1, source_target_pairs={{0,4},{1,5},{2,6},{3,7},{4,0},{5,1},{6,2},{7,3},{8,12},{9,13},{10,... | collective-permute-start | bytes 552968 | tf_op jit(solution)/shard_map/ppermute | solution.py:94
  211.3 9.1 %collective-permute-start.11 = (bf16[5,144,128]{2,1,0:T(8,128)(2,1)}, bf16[5,144,128]{2,1,0:T(8,128)(2,1)S(1)}, u32[]{:S(2)}, u32[]{:S(2)}) collective-permute-start(bf16[5,144,128]{2,1,0:T(8,128)(2,1)} %get-tuple-element.126), channel_id=1, source_target_pairs={{0,5},{1,4},{2,7},{3,6},{4,1},{5,0},{6,3},{7,2},{8,13},{9,12},{10,... | collective-permute-start | bytes 552968 | tf_op jit(solution)/shard_map/ppermute | solution.py:94
  211.3 14.1 %collective-permute-start.12 = (bf16[5,144,128]{2,1,0:T(8,128)(2,1)}, bf16[5,144,128]{2,1,0:T(8,128)(2,1)S(1)}, u32[]{:S(2)}, u32[]{:S(2)}) collective-permute-start(bf16[5,144,128]{2,1,0:T(8,128)(2,1)} %get-tuple-element.127), channel_id=1, source_target_pairs={{0,6},{1,7},{2,0},{3,1},{4,2},{5,3},{6,4},{7,5},{8,14},{9,15},{10,... | collective-permute-start | bytes 552968 | tf_op jit(solution)/shard_map/ppermute | solution.py:94
  214.3 14.1 %collective-permute-start.13 = (bf16[5,144,128]{2,1,0:T(8,128)(2,1)}, bf16[5,144,128]{2,1,0:T(8,128)(2,1)S(1)}, u32[]{:S(2)}, u32[]{:S(2)}) collective-permute-start(bf16[5,144,128]{2,1,0:T(8,128)(2,1)} %get-tuple-element.128), channel_id=1, source_target_pairs={{0,7},{1,6},{2,1},{3,0},{4,3},{5,2},{6,5},{7,4},{8,15},{9,14},{10,... | collective-permute-start | bytes 552968 | tf_op jit(solution)/shard_map/ppermute | solution.py:94
  217.0 11.4 %collective-permute-start.7 = (bf16[5,144,128]{2,1,0:T(8,128)(2,1)S(1)}, bf16[5,144,128]{2,1,0:T(8,128)(2,1)S(1)}, u32[]{:S(2)}, u32[]{:S(2)}) collective-permute-start(bf16[5,144,128]{2,1,0:T(8,128)(2,1)S(1)} %copy-done.20), channel_id=1, source_target_pairs={{0,1},{1,0},{2,3},{3,2},{4,5},{5,4},{6,7},{7,6},{8,9},{9,8},{10,11... | collective-permute-start | bytes 552968 | tf_op jit(solution)/shard_map/ppermute | solution.py:94
  220.3 8.7 %collective-permute-start.8 = (bf16[5,144,128]{2,1,0:T(8,128)(2,1)S(1)}, bf16[5,144,128]{2,1,0:T(8,128)(2,1)S(1)}, u32[]{:S(2)}, u32[]{:S(2)}) collective-permute-start(bf16[5,144,128]{2,1,0:T(8,128)(2,1)S(1)} %copy-done.19), channel_id=1, source_target_pairs={{0,2},{1,3},{2,4},{3,5},{4,6},{5,7},{6,0},{7,1},{8,10},{9,11},{10,... | collective-permute-start | bytes 552968 | tf_op jit(solution)/shard_map/ppermute | solution.py:94
  225.4 7.7 %collective-permute-start.9 = (bf16[5,144,128]{2,1,0:T(8,128)(2,1)S(1)}, bf16[5,144,128]{2,1,0:T(8,128)(2,1)S(1)}, u32[]{:S(2)}, u32[]{:S(2)}) collective-permute-start(bf16[5,144,128]{2,1,0:T(8,128)(2,1)S(1)} %copy-done.18), channel_id=1, source_target_pairs={{0,3},{1,2},{2,5},{3,4},{4,7},{5,6},{6,1},{7,0},{8,11},{9,10},{10,... | collective-permute-start | bytes 552968 | tf_op jit(solution)/shard_map/ppermute | solution.py:94
  239.0 50.3 %all-to-all-start.5 = ((bf16[16,5,144,128]{3,2,1,0:T(8,128)(2,1)}), bf16[16,5,144,128]{3,2,1,0:T(8,128)(2,1)}, u32[]{:S(2)}, u32[]{:S(2)}) async-start(bf16[16,5,144,128]{3,2,1,0:T(8,128)(2,1)} %copy-done.1), calls=%async_computation.5 | async-start | bytes 5898240 | tf_op jit(solution)/shard_map/all_to_all | solution.py:702
  247.6 18.9 %collective-permute-start.15 = (bf16[16,8,2688]{2,1,0:T(8,128)(2,1)S(1)}, bf16[16,8,2688]{2,1,0:T(8,128)(2,1)S(1)}, u32[]{:S(2)}, u32[]{:S(2)}) collective-permute-start(bf16[16,8,2688]{2,1,0:T(8,128)(2,1)S(1)} %get-tuple-element.150), channel_id=1, source_target_pairs={{0,2},{1,3},{2,4},{3,5},{4,6},{5,7},{6,0},{7,1},{8,10},{9,11},{10,... | collective-permute-start | bytes 2064392 | tf_op jit(solution)/shard_map/ppermute | solution.py:710
  247.9 32.7 %collective-permute-start.16 = (bf16[16,8,2688]{2,1,0:T(8,128)(2,1)S(1)}, bf16[16,8,2688]{2,1,0:T(8,128)(2,1)S(1)}, u32[]{:S(2)}, u32[]{:S(2)}) collective-permute-start(bf16[16,8,2688]{2,1,0:T(8,128)(2,1)S(1)} %get-tuple-element.152), channel_id=1, source_target_pairs={{0,4},{1,5},{2,6},{3,7},{4,0},{5,1},{6,2},{7,3},{8,12},{9,13},{10,... | collective-permute-start | bytes 2064392 | tf_op jit(solution)/shard_map/ppermute | solution.py:710
  250.6 43.0 %copy-start.9 = (s32[48]{0:T(128)S(1)}, s32[48]{0:T(128)}, u32[]{:S(2)}) copy-start(s32[48]{0:T(128)} %get-tuple-element.149.own_ref) | copy-start | bytes 580
  250.6 43.0 %copy-start.10 = (s32[48]{0:T(128)S(1)}, s32[48]{0:T(128)}, u32[]{:S(2)}) copy-start(s32[48]{0:T(128)} %and_select_fusion.pos_ref) | copy-start | bytes 580
  250.6 30.4 %collective-permute-start.17 = (bf16[16,8,2688]{2,1,0:T(8,128)(2,1)S(1)}, bf16[16,8,2688]{2,1,0:T(8,128)(2,1)S(1)}, u32[]{:S(2)}, u32[]{:S(2)}) collective-permute-start(bf16[16,8,2688]{2,1,0:T(8,128)(2,1)S(1)} %get-tuple-element.151), channel_id=1, source_target_pairs={{0,6},{1,7},{2,0},{3,1},{4,2},{5,3},{6,4},{7,5},{8,14},{9,15},{10,... | collective-permute-start | bytes 2064392 | tf_op jit(solution)/shard_map/ppermute | solution.py:710
  289.3 16.6 %all-to-all-start.6 = ((bf16[16,8,2688]{2,1,0:T(8,128)(2,1)}), bf16[16,8,2688]{2,1,0:T(8,128)(2,1)}, u32[]{:S(2)}, u32[]{:S(2)}) async-start(bf16[16,8,2688]{2,1,0:T(8,128)(2,1)} %fusion.2), calls=%async_computation.6 | async-start | bytes 1376256 | tf_op jit(solution)/shard_map/all_to_all | solution.py:713
  (16 other events, 91.3 us)

commit v7 on v6

--- a/solution.py
+++ b/solution.py
@@ -56,7 +56,7 @@
 def pool_and_pack(tiles, own, pos, groups, slots):
     count, grid, _, channels = tiles.shape
     cells = grid * grid // 4
-    per = 8
+    per = 16
     steps = count // per
     made = jax.ShapeDtypeStruct((groups, slots, cells, channels), BF16)
     return pl.pallas_call(
@@ -142,7 +142,7 @@
         out_specs=ANY if back else [ANY] * len(parts),
         out_shape=whole if back else parts,
         scratch_shapes=[pltpu.SemaphoreType.DMA],
-        compiler_params=pltpu.CompilerParams(vmem_limit_bytes=16 * 1024 * 1024),
+        compiler_params=pltpu.CompilerParams(vmem_limit_bytes=52 * 1024 * 1024),
         cost_estimate=pl.CostEstimate(
             flops=0, bytes_accessed=8 * columns * slots * cells * channels, transcendentals=0
         ),

time: 312 us -> 308 us (0.987)
  local copies, waits for them, and re-layouts: 30 us -> 23.2 us
  Pallas kernels: 90.5 us -> 93.9 us
    unnamed x51 -> x53, local copies, waits for them, and re-layouts: 20.3 us -> 13.5 us
    pallas_call x4, Pallas kernels: 6.94 us -> 11 us  [route(): pl.pallas_call(functools.partial(route_kernel, chunk, per, columns, back)...]
    all_to_all x2, starting transfers between devices: 12.2 us -> 8.2 us  [local(): lax.all_to_all(back, 'enc', split_axis=0, concat_axis=0, tiled=True)]
  transfers between devices with their start and end apart: 25 -> 25, of which waited for: 15 -> 15; matrix products, arithmetic and copies ran while one was open for 7% -> 7% of each run, Pallas kernels for 27% -> 28%
where the time goes in v7:
time: 308 us; the launch traced here: 307 us
  waiting for transfers between devices  119 us (39%)
  Pallas kernels  93.9 us (30%)
  starting transfers between devices  58.3 us (19%)
  local copies, waits for them, and re-layouts  23.2 us (8%)
  other arithmetic  11.1 us (4%)
    all_to_all x2, waiting for transfers between devices, local(): lax.all_to_all(send, 'enc', split_axis=0, concat_axis=0, tiled=True)  57.9 us
    pallas_call x2, Pallas kernels, run_block(): pl.pallas_call(functools.partial(block_kernel, chunk, side, columns, len(...  54.9 us
    ppermute x3, waiting for transfers between devices, local(): lax.ppermute(pair[k], 'abs', partner_pairs(2 * k, columns))  28.5 us
    ppermute x14, starting transfers between devices, exchange(): lax.ppermute(parts[k], 'abs', partner_pairs(k, columns))  18.2 us
    ppermute x14, waiting for transfers between devices, exchange(): lax.ppermute(parts[k], 'abs', partner_pairs(k, columns))  17.2 us
    pallas_call x1, Pallas kernels, weight_terms(): pl.pallas_call(functools.partial(weights_kernel, len(small), columns), gr...  15 us
    unnamed x53, local copies, waits for them, and re-layouts  13.5 us
    all_to_all x2, starting transfers between devices, local(): lax.all_to_all(send, 'enc', split_axis=0, concat_axis=0, tiled=True)  11.6 us
  transfers between devices with their start and end apart: 25, of which 15 were waited for; matrix products, arithmetic and copies ran while one was open for 7% of the time, Pallas kernels for 28%

profile of v7, /device:TPU:0, one launch (start us, length us, event | category | flops | bytes accessed | tf_op | source)
XLA Modules:
  0.0 306.7 jit_solution(2090171162815712007)
XLA Ops:
  6.0 5.1 %pool_and_pack.1 = (bf16[16,5,144,128]{3,2,1,0:T(8,128)(2,1)}, bf16[16,5,144,128]{3,2,1,0:T(8,128)(2,1)}) custom-call(s32[48]{0:T(128)} %get-tuple-element.149.own_ref, s32[48]{0:T(128)} %and_select_fusion.pos_ref, bf16[48,24,24,128]{3,2,1,0:T(8,128)(2,1)} %tiles_ref.1), custom_call_target="tpu_custom_call" | custom-call | flops 3538944 | bytes 10616832 | tf_op jit(solution)/shard_map/pool_and_pack/pallas_call | solution.py:62
  11.1 7.1 %all-to-all-start = ((bf16[16,5,144,128]{3,2,1,0:T(8,128)(2,1)}), bf16[16,5,144,128]{3,2,1,0:T(8,128)(2,1)S(1)}, u32[]{:S(2)}, u32[]{:S(2)}) async-start(bf16[16,5,144,128]{3,2,1,0:T(8,128)(2,1)} %get-tuple-element.74), calls=%async_computation | async-start | bytes 5898240 | tf_op jit(solution)/shard_map/all_to_all | solution.py:682
  18.3 4.0 %copy.36 = bf16[1024,1024]{0,1:T(8,128)(2,1)} copy(bf16[1024,1024]{1,0:T(8,128)(2,1)} %rest_2_) | data formatting | bytes 4194304 | tf_op args[1]
  22.2 4.0 %copy.37 = bf16[1024,1024]{0,1:T(8,128)(2,1)} copy(bf16[1024,1024]{1,0:T(8,128)(2,1)} %rest_3_) | data formatting | bytes 4194304 | tf_op args[2]
  29.9 32.8 %all-to-all-done.rest_0_ = bf16[16,5,144,128]{3,2,1,0:T(8,128)(2,1)S(1)} async-done(((bf16[16,5,144,128]{3,2,1,0:T(8,128)(2,1)}), bf16[16,5,144,128]{3,2,1,0:T(8,128)(2,1)S(1)}, u32[]{:S(2)}, u32[]{:S(2)}) %all-to-all-start) | async-done | bytes 2949152 | tf_op jit(solution)/shard_map/all_to_all | solution.py:682
  64.4 4.5 %all-to-all-start.1 = ((bf16[16,5,144,128]{3,2,1,0:T(8,128)(2,1)}), bf16[16,5,144,128]{3,2,1,0:T(8,128)(2,1)}, u32[]{:S(2)}, u32[]{:S(2)}) async-start(bf16[16,5,144,128]{3,2,1,0:T(8,128)(2,1)} %get-tuple-element.85), calls=%async_computation.1 | async-start | bytes 5898240 | tf_op jit(solution)/shard_map/all_to_all | solution.py:682
  69.9 4.6 %route_in.2 = (bf16[5,144,128]{2,1,0:T(8,128)(2,1)S(1)}, bf16[5,144,128]{2,1,0:T(8,128)(2,1)S(1)}, bf16[5,144,128]{2,1,0:T(8,128)(2,1)S(1)}, bf16[5,144,128]{2,1...) custom-call(s32[80]{0:T(128)S(1)} %select_reduce_fusion.7.table_ref,, ...), custom_call_target="tpu_custom_call" | custom-call | bytes 5898240 | tf_op jit(solution)/shard_map/route_in/pallas_call | solution.py:139
  85.7 25.1 %all-to-all-done.1.rest_0_ = bf16[16,5,144,128]{3,2,1,0:T(8,128)(2,1)} async-done(((bf16[16,5,144,128]{3,2,1,0:T(8,128)(2,1)}), bf16[16,5,144,128]{3,2,1,0:T(8,128)(2,1)}, u32[]{:S(2)}, u32[]{:S(2)}) %all-to-all-start.1) | async-done | bytes 2949152 | tf_op jit(solution)/shard_map/all_to_all | solution.py:682
  110.7 3.1 %route_in.3 = bf16[8,5,144,128]{3,2,1,0:T(8,128)(2,1)} custom-call(s32[80]{0:T(128)S(1)} %select_reduce_fusion.7.table_ref, s32[3]{0:T(128)S(1)} %pad_add_fusion.info_ref, bf16[16,5,144,128]{3,2,1,0:T(8,128)(2,1)} %all-to-all-done.1.rest_0_), custom_call_target="tpu_custom_call" | custom-call | bytes 5898240 | tf_op jit(solution)/shard_map/route_in/pallas_call | solution.py:139
  114.7 5.3 %all-to-all-start.3 = ((bf16[8,5,144,128]{3,2,1,0:T(8,128)(2,1)}), bf16[8,5,144,128]{3,2,1,0:T(8,128)(2,1)S(1)}, u32[]{:S(2)}, u32[]{:S(2)}) async-start(bf16[8,5,144,128]{3,2,1,0:T(8,128)(2,1)} %route_in.3), calls=%async_computation.3 | async-start | bytes 2949120 | tf_op jit(solution)/shard_map/all_to_all | solution.py:93
  120.1 27.4 %block_0.1 = (bf16[10,144,1024]{2,1,0:T(8,128)(2,1)}, bf16[10,144,1024]{2,1,0:T(8,128)(2,1)}, bf16[10,144,1024]{2,1,0:T(8,128)(2,1)}, bf16[10,144,1024]{2,1,0:T(...) custom-call(s32[3]{0:T(128)} %copy-done.1, ...), custom_call_target="tpu_custom_call" | custom-call | flops 6039797760 | bytes 20185088 | tf_op jit(solution)/shard_map/block_0/pallas_call | solution.py:437
  147.5 4.8 %all-to-all-start.2 = ((bf16[8,5,144,128]{3,2,1,0:T(8,128)(2,1)}), bf16[8,5,144,128]{3,2,1,0:T(8,128)(2,1)S(1)}, u32[]{:S(2)}, u32[]{:S(2)}) async-start(bf16[8,5,144,128]{3,2,1,0:T(8,128)(2,1)} %get-tuple-element.104), calls=%async_computation.2 | async-start | bytes 2949120 | tf_op jit(solution)/shard_map/all_to_all | solution.py:93
  154.9 27.4 %block_1.1 = (bf16[10,144,1024]{2,1,0:T(8,128)(2,1)}, bf16[10,144,1024]{2,1,0:T(8,128)(2,1)}, bf16[10,144,1024]{2,1,0:T(8,128)(2,1)}, bf16[10,144,1024]{2,1,0:T(...) custom-call(s32[3]{0:T(128)} %copy-done.1, ...), custom_call_target="tpu_custom_call", output_to_operand_aliasing={{0}: (13, {}), {1}: (14, {}), {2}: (15, {}), {3}: (16, {})} | custom-call | flops 6039797760 | bytes 20185088 | tf_op jit(solution)/shard_map/block_1/pallas_call | solution.py:437
  185.1 3.7 %all-to-all-start.4 = ((bf16[16,5,144,128]{3,2,1,0:T(8,128)(2,1)}), bf16[16,5,144,128]{3,2,1,0:T(8,128)(2,1)S(1)}, u32[]{:S(2)}, u32[]{:S(2)}) async-start(bf16[16,5,144,128]{3,2,1,0:T(8,128)(2,1)} %route_back.2), calls=%async_computation.4 | async-start | bytes 5898240 | tf_op jit(solution)/shard_map/all_to_all | solution.py:702
  188.9 15.0 %weight_terms.1 = (bf16[4,16,8,2688]{3,2,1,0:T(8,128)(2,1)}, bf16[4,16,8,2688]{3,2,1,0:T(8,128)(2,1)}) custom-call(s32[3]{0:T(128)} %copy-done.1, bf16[10,144,1024]{2,1,0:T(8,128)(2,1)} %get-tuple-element.129.normed, bf16[10,144,1024]{2,1,0:T(8,128)(2,1)} %get-tuple-element.130.scaled, bf16[10,144,1024]{2,1,0:T(8,128)(2,1)} %get-tuple-element.131.hidden, ...), custom_call_target="tpu_custom_call" | custom-call | flops 6039797760 | bytes 11796480 | tf_op jit(solution)/shard_map/weight_terms/pallas_call | solution.py:555
  204.5 3.2 %collective-permute-start.10 = (bf16[5,144,128]{2,1,0:T(8,128)(2,1)}, bf16[5,144,128]{2,1,0:T(8,128)(2,1)S(1)}, u32[]{:S(2)}, u32[]{:S(2)}) collective-permute-start(bf16[5,144,128]{2,1,0:T(8,128)(2,1)} %get-tuple-element.125), channel_id=1, source_target_pairs={{0,4},{1,5},{2,6},{3,7},{4,0},{5,1},{6,2},{7,3},{8,12},{9,13},{10,... | collective-permute-start | bytes 552968 | tf_op jit(solution)/shard_map/ppermute | solution.py:94
  207.7 2.9 collective-permute-start.12
  211.2 2.5 collective-permute-done.10.rest_4_
  213.7 2.7 collective-permute-done.11.rest_5_
  218.2 3.6 %collective-permute-done.12.rest_6_ = bf16[5,144,128]{2,1,0:T(8,128)(2,1)S(1)} collective-permute-done((bf16[5,144,128]{2,1,0:T(8,128)(2,1)}, bf16[5,144,128]{2,1,0:T(8,128)(2,1)S(1)}, u32[]{:S(2)}, u32[]{:S(2)}) %collective-permute-start.12) | collective-permute-done | bytes 184352 | tf_op jit(solution)/shard_map/ppermute | solution.py:94
  224.8 4.6 %collective-permute-done.9.rest_3_ = bf16[5,144,128]{2,1,0:T(8,128)(2,1)S(1)} collective-permute-done((bf16[5,144,128]{2,1,0:T(8,128)(2,1)S(1)}, bf16[5,144,128]{2,1,0:T(8,128)(2,1)S(1)}, u32[]{:S(2)}, u32[]{:S(2)}) %collective-permute-start.9) | collective-permute-done | bytes 184352 | tf_op jit(solution)/shard_map/ppermute | solution.py:94
  231.1 4.9 %all-to-all-done.4.rest_0_ = bf16[16,5,144,128]{3,2,1,0:T(8,128)(2,1)S(1)} async-done(((bf16[16,5,144,128]{3,2,1,0:T(8,128)(2,1)}), bf16[16,5,144,128]{3,2,1,0:T(8,128)(2,1)S(1)}, u32[]{:S(2)}, u32[]{:S(2)}) %all-to-all-start.4) | async-done | bytes 2949152 | tf_op jit(solution)/shard_map/all_to_all | solution.py:702
  236.1 4.5 %all-to-all-start.5 = ((bf16[16,5,144,128]{3,2,1,0:T(8,128)(2,1)}), bf16[16,5,144,128]{3,2,1,0:T(8,128)(2,1)}, u32[]{:S(2)}, u32[]{:S(2)}) async-start(bf16[16,5,144,128]{3,2,1,0:T(8,128)(2,1)} %route_back.3), calls=%async_computation.5 | async-start | bytes 5898240 | tf_op jit(solution)/shard_map/all_to_all | solution.py:702
  240.5 2.6 fusion.4
  244.2 2.7 collective-permute-start.16
  248.4 14.8 %collective-permute-done.15 = bf16[16,8,2688]{2,1,0:T(8,128)(2,1)S(1)} collective-permute-done((bf16[16,8,2688]{2,1,0:T(8,128)(2,1)S(1)}, bf16[16,8,2688]{2,1,0:T(8,128)(2,1)S(1)}, u32[]{:S(2)}, u32[]{:S(2)}) %collective-permute-start.15) | collective-permute-done | bytes 688160 | tf_op jit(solution)/shard_map/ppermute | solution.py:710
  263.2 13.0 %collective-permute-done.16 = bf16[16,8,2688]{2,1,0:T(8,128)(2,1)S(1)} collective-permute-done((bf16[16,8,2688]{2,1,0:T(8,128)(2,1)S(1)}, bf16[16,8,2688]{2,1,0:T(8,128)(2,1)S(1)}, u32[]{:S(2)}, u32[]{:S(2)}) %collective-permute-start.16) | collective-permute-done | bytes 688160 | tf_op jit(solution)/shard_map/ppermute | solution.py:710
  276.9 2.6 fusion.2
  279.5 6.0 %all-to-all-done.5.rest_1_ = bf16[16,5,144,128]{3,2,1,0:T(8,128)(2,1)} async-done(((bf16[16,5,144,128]{3,2,1,0:T(8,128)(2,1)}), bf16[16,5,144,128]{3,2,1,0:T(8,128)(2,1)}, u32[]{:S(2)}, u32[]{:S(2)}) %all-to-all-start.5) | async-done | bytes 2949152 | tf_op jit(solution)/shard_map/all_to_all | solution.py:702
  285.5 4.4 %all-to-all-start.6 = ((bf16[16,8,2688]{2,1,0:T(8,128)(2,1)}), bf16[16,8,2688]{2,1,0:T(8,128)(2,1)}, u32[]{:S(2)}, u32[]{:S(2)}) async-start(bf16[16,8,2688]{2,1,0:T(8,128)(2,1)} %fusion.2), calls=%async_computation.6 | async-start | bytes 1376256 | tf_op jit(solution)/shard_map/all_to_all | solution.py:713
  289.9 7.9 %unpack_and_spread.1 = bf16[48,24,24,128]{3,2,1,0:T(8,128)(2,1)} custom-call(s32[48]{0:T(128)S(1)} %copy-done.4, s32[48]{0:T(128)S(1)} %copy-done.5, bf16[16,5,144,128]{3,2,1,0:T(8,128)(2,1)S(1)} %all-to-all-done.4.rest_0_, bf16[16,5,144,128]{3,2,1,0:T(8,128)(2,1)} %all-to-all-done.5.rest_1_), custom_call_target="tpu_custom_call" | custom-call | bytes 8847360 | tf_op jit(solution)/shard_map/unpack_and_spread/pallas_call | solution.py:595
  297.8 4.6 %all-to-all-done.6 = bf16[16,8,2688]{2,1,0:T(8,128)(2,1)} async-done(((bf16[16,8,2688]{2,1,0:T(8,128)(2,1)}), bf16[16,8,2688]{2,1,0:T(8,128)(2,1)}, u32[]{:S(2)}, u32[]{:S(2)}) %all-to-all-start.6) | async-done | bytes 688160 | tf_op jit(solution)/shard_map/all_to_all | solution.py:713
  (118 shorter events, 44.2 us)
Async XLA Ops:
  11.1 51.6 %all-to-all-start = ((bf16[16,5,144,128]{3,2,1,0:T(8,128)(2,1)}), bf16[16,5,144,128]{3,2,1,0:T(8,128)(2,1)S(1)}, u32[]{:S(2)}, u32[]{:S(2)}) async-start(bf16[16,5,144,128]{3,2,1,0:T(8,128)(2,1)} %get-tuple-element.74), calls=%async_computation | async-start | bytes 5898240 | tf_op jit(solution)/shard_map/all_to_all | solution.py:682
  64.4 46.4 %all-to-all-start.1 = ((bf16[16,5,144,128]{3,2,1,0:T(8,128)(2,1)}), bf16[16,5,144,128]{3,2,1,0:T(8,128)(2,1)}, u32[]{:S(2)}, u32[]{:S(2)}) async-start(bf16[16,5,144,128]{3,2,1,0:T(8,128)(2,1)} %get-tuple-element.85), calls=%async_computation.1 | async-start | bytes 5898240 | tf_op jit(solution)/shard_map/all_to_all | solution.py:682
  69.8 44.1 %copy-start.1 = (s32[3]{0:T(128)}, s32[3]{0:T(128)S(1)}, u32[]{:S(2)}) copy-start(s32[3]{0:T(128)S(1)} %pad_add_fusion.info_ref) | copy-start | bytes 40
  75.1 6.8 %collective-permute-start = (bf16[5,144,128]{2,1,0:T(8,128)(2,1)S(1)}, bf16[5,144,128]{2,1,0:T(8,128)(2,1)S(1)}, u32[]{:S(2)}, u32[]{:S(2)}) collective-permute-start(bf16[5,144,128]{2,1,0:T(8,128)(2,1)S(1)} %get-tuple-element.77), channel_id=1, source_target_pairs={{0,1},{1,0},{2,3},{3,2},{4,5},{5,4},{6,7},{7,6},{8,9},{9,8},{10,11... | collective-permute-start | bytes 552968 | tf_op jit(solution)/shard_map/ppermute | solution.py:94
  75.1 9.5 %collective-permute-start.1 = (bf16[5,144,128]{2,1,0:T(8,128)(2,1)S(1)}, bf16[5,144,128]{2,1,0:T(8,128)(2,1)S(1)}, u32[]{:S(2)}, u32[]{:S(2)}) collective-permute-start(bf16[5,144,128]{2,1,0:T(8,128)(2,1)S(1)} %get-tuple-element.78), channel_id=1, source_target_pairs={{0,2},{1,3},{2,4},{3,5},{4,6},{5,7},{6,0},{7,1},{8,10},{9,11},{10,... | collective-permute-start | bytes 552968 | tf_op jit(solution)/shard_map/ppermute | solution.py:94
  77.0 36.8 %collective-permute-start.2 = (bf16[5,144,128]{2,1,0:T(8,128)(2,1)S(1)}, bf16[5,144,128]{2,1,0:T(8,128)(2,1)S(1)}, u32[]{:S(2)}, u32[]{:S(2)}) collective-permute-start(bf16[5,144,128]{2,1,0:T(8,128)(2,1)S(1)} %get-tuple-element.79), channel_id=1, source_target_pairs={{0,3},{1,2},{2,5},{3,4},{4,7},{5,6},{6,1},{7,0},{8,11},{9,10},{10,... | collective-permute-start | bytes 552968 | tf_op jit(solution)/shard_map/ppermute | solution.py:94
  78.8 35.1 %collective-permute-start.3 = (bf16[5,144,128]{2,1,0:T(8,128)(2,1)S(1)}, bf16[5,144,128]{2,1,0:T(8,128)(2,1)S(1)}, u32[]{:S(2)}, u32[]{:S(2)}) collective-permute-start(bf16[5,144,128]{2,1,0:T(8,128)(2,1)S(1)} %get-tuple-element.80), channel_id=1, source_target_pairs={{0,4},{1,5},{2,6},{3,7},{4,0},{5,1},{6,2},{7,3},{8,12},{9,13},{10,... | collective-permute-start | bytes 552968 | tf_op jit(solution)/shard_map/ppermute | solution.py:94
  80.8 33.1 %collective-permute-start.4 = (bf16[5,144,128]{2,1,0:T(8,128)(2,1)S(1)}, bf16[5,144,128]{2,1,0:T(8,128)(2,1)S(1)}, u32[]{:S(2)}, u32[]{:S(2)}) collective-permute-start(bf16[5,144,128]{2,1,0:T(8,128)(2,1)S(1)} %get-tuple-element.81), channel_id=1, source_target_pairs={{0,5},{1,4},{2,7},{3,6},{4,1},{5,0},{6,3},{7,2},{8,13},{9,12},{10,... | collective-permute-start | bytes 552968 | tf_op jit(solution)/shard_map/ppermute | solution.py:94
  81.9 31.9 %copy-start.17 = (bf16[5,144,128]{2,1,0:T(8,128)(2,1)}, bf16[5,144,128]{2,1,0:T(8,128)(2,1)S(1)}, u32[]{:S(2)}) copy-start(bf16[5,144,128]{2,1,0:T(8,128)(2,1)S(1)} %collective-permute-done.rest_1_) | copy-start | bytes 552964
  81.9 32.0 %collective-permute-start.5 = (bf16[5,144,128]{2,1,0:T(8,128)(2,1)S(1)}, bf16[5,144,128]{2,1,0:T(8,128)(2,1)S(1)}, u32[]{:S(2)}, u32[]{:S(2)}) collective-permute-start(bf16[5,144,128]{2,1,0:T(8,128)(2,1)S(1)} %get-tuple-element.82), channel_id=1, source_target_pairs={{0,6},{1,7},{2,0},{3,1},{4,2},{5,3},{6,4},{7,5},{8,14},{9,15},{10,... | collective-permute-start | bytes 552968 | tf_op jit(solution)/shard_map/ppermute | solution.py:94
  84.7 29.3 %collective-permute-start.6 = (bf16[5,144,128]{2,1,0:T(8,128)(2,1)S(1)}, bf16[5,144,128]{2,1,0:T(8,128)(2,1)S(1)}, u32[]{:S(2)}, u32[]{:S(2)}) collective-permute-start(bf16[5,144,128]{2,1,0:T(8,128)(2,1)S(1)} %get-tuple-element.83), channel_id=1, source_target_pairs={{0,7},{1,6},{2,1},{3,0},{4,3},{5,2},{6,5},{7,4},{8,15},{9,14},{10,... | collective-permute-start | bytes 552968 | tf_op jit(solution)/shard_map/ppermute | solution.py:94
  114.7 32.8 %all-to-all-start.3 = ((bf16[8,5,144,128]{3,2,1,0:T(8,128)(2,1)}), bf16[8,5,144,128]{3,2,1,0:T(8,128)(2,1)S(1)}, u32[]{:S(2)}, u32[]{:S(2)}) async-start(bf16[8,5,144,128]{3,2,1,0:T(8,128)(2,1)} %route_in.3), calls=%async_computation.3 | async-start | bytes 2949120 | tf_op jit(solution)/shard_map/all_to_all | solution.py:93
  147.5 34.8 %all-to-all-start.2 = ((bf16[8,5,144,128]{3,2,1,0:T(8,128)(2,1)}), bf16[8,5,144,128]{3,2,1,0:T(8,128)(2,1)S(1)}, u32[]{:S(2)}, u32[]{:S(2)}) async-start(bf16[8,5,144,128]{3,2,1,0:T(8,128)(2,1)} %get-tuple-element.104), calls=%async_computation.2 | async-start | bytes 2949120 | tf_op jit(solution)/shard_map/all_to_all | solution.py:93
  185.1 50.9 %all-to-all-start.4 = ((bf16[16,5,144,128]{3,2,1,0:T(8,128)(2,1)}), bf16[16,5,144,128]{3,2,1,0:T(8,128)(2,1)S(1)}, u32[]{:S(2)}, u32[]{:S(2)}) async-start(bf16[16,5,144,128]{3,2,1,0:T(8,128)(2,1)} %route_back.2), calls=%async_computation.4 | async-start | bytes 5898240 | tf_op jit(solution)/shard_map/all_to_all | solution.py:702
  188.9 32.9 %copy-start.14 = (bf16[5,144,128]{2,1,0:T(8,128)(2,1)S(1)}, bf16[5,144,128]{2,1,0:T(8,128)(2,1)}, u32[]{:S(2)}) copy-start(bf16[5,144,128]{2,1,0:T(8,128)(2,1)} %get-tuple-element.124) | copy-start | bytes 552964
  188.9 40.5 %copy-start = (bf16[5,144,128]{2,1,0:T(8,128)(2,1)S(1)}, bf16[5,144,128]{2,1,0:T(8,128)(2,1)}, u32[]{:S(2)}) copy-start(bf16[5,144,128]{2,1,0:T(8,128)(2,1)} %get-tuple-element.121.rest_0_) | copy-start | bytes 552964
  188.9 40.5 %copy-start.3 = (s32[3]{0:T(128)S(1)}, s32[3]{0:T(128)}, u32[]{:S(2)}) copy-start(s32[3]{0:T(128)} %copy-done.1) | copy-start | bytes 40
  203.9 36.6 %collective-permute-start.14 = (bf16[4,16,8,2688]{3,2,1,0:T(8,128)(2,1)}, bf16[4,16,8,2688]{3,2,1,0:T(8,128)(2,1)}, u32[]{:S(2)}, u32[]{:S(2)}) collective-permute-start(bf16[4,16,8,2688]{3,2,1,0:T(8,128)(2,1)} %get-tuple-element.139), channel_id=1, source_target_pairs={{0,1},{1,0},{2,3},{3,2},{4,5},{5,4},{6,7},{7,6},{8,9},{9,8},{10,11... | collective-permute-start | bytes 8257544 | tf_op jit(solution)/shard_map/ppermute | solution.py:707
  204.5 9.2 %collective-permute-start.10 = (bf16[5,144,128]{2,1,0:T(8,128)(2,1)}, bf16[5,144,128]{2,1,0:T(8,128)(2,1)S(1)}, u32[]{:S(2)}, u32[]{:S(2)}) collective-permute-start(bf16[5,144,128]{2,1,0:T(8,128)(2,1)} %get-tuple-element.125), channel_id=1, source_target_pairs={{0,4},{1,5},{2,6},{3,7},{4,0},{5,1},{6,2},{7,3},{8,12},{9,13},{10,... | collective-permute-start | bytes 552968 | tf_op jit(solution)/shard_map/ppermute | solution.py:94
  207.7 8.7 %collective-permute-start.11 = (bf16[5,144,128]{2,1,0:T(8,128)(2,1)}, bf16[5,144,128]{2,1,0:T(8,128)(2,1)S(1)}, u32[]{:S(2)}, u32[]{:S(2)}) collective-permute-start(bf16[5,144,128]{2,1,0:T(8,128)(2,1)} %get-tuple-element.126), channel_id=1, source_target_pairs={{0,5},{1,4},{2,7},{3,6},{4,1},{5,0},{6,3},{7,2},{8,13},{9,12},{10,... | collective-permute-start | bytes 552968 | tf_op jit(solution)/shard_map/ppermute | solution.py:94
  207.7 14.1 %collective-permute-start.12 = (bf16[5,144,128]{2,1,0:T(8,128)(2,1)}, bf16[5,144,128]{2,1,0:T(8,128)(2,1)S(1)}, u32[]{:S(2)}, u32[]{:S(2)}) collective-permute-start(bf16[5,144,128]{2,1,0:T(8,128)(2,1)} %get-tuple-element.127), channel_id=1, source_target_pairs={{0,6},{1,7},{2,0},{3,1},{4,2},{5,3},{6,4},{7,5},{8,14},{9,15},{10,... | collective-permute-start | bytes 552968 | tf_op jit(solution)/shard_map/ppermute | solution.py:94
  210.6 14.1 %collective-permute-start.13 = (bf16[5,144,128]{2,1,0:T(8,128)(2,1)}, bf16[5,144,128]{2,1,0:T(8,128)(2,1)S(1)}, u32[]{:S(2)}, u32[]{:S(2)}) collective-permute-start(bf16[5,144,128]{2,1,0:T(8,128)(2,1)} %get-tuple-element.128), channel_id=1, source_target_pairs={{0,7},{1,6},{2,1},{3,0},{4,3},{5,2},{6,5},{7,4},{8,15},{9,14},{10,... | collective-permute-start | bytes 552968 | tf_op jit(solution)/shard_map/ppermute | solution.py:94
  213.7 11.0 %collective-permute-start.7 = (bf16[5,144,128]{2,1,0:T(8,128)(2,1)S(1)}, bf16[5,144,128]{2,1,0:T(8,128)(2,1)S(1)}, u32[]{:S(2)}, u32[]{:S(2)}) collective-permute-start(bf16[5,144,128]{2,1,0:T(8,128)(2,1)S(1)} %copy-done.16), channel_id=1, source_target_pairs={{0,1},{1,0},{2,3},{3,2},{4,5},{5,4},{6,7},{7,6},{8,9},{9,8},{10,11... | collective-permute-start | bytes 552968 | tf_op jit(solution)/shard_map/ppermute | solution.py:94
  216.4 8.4 %collective-permute-start.8 = (bf16[5,144,128]{2,1,0:T(8,128)(2,1)S(1)}, bf16[5,144,128]{2,1,0:T(8,128)(2,1)S(1)}, u32[]{:S(2)}, u32[]{:S(2)}) collective-permute-start(bf16[5,144,128]{2,1,0:T(8,128)(2,1)S(1)} %copy-done.15), channel_id=1, source_target_pairs={{0,2},{1,3},{2,4},{3,5},{4,6},{5,7},{6,0},{7,1},{8,10},{9,11},{10,... | collective-permute-start | bytes 552968 | tf_op jit(solution)/shard_map/ppermute | solution.py:94
  221.8 7.6 %collective-permute-start.9 = (bf16[5,144,128]{2,1,0:T(8,128)(2,1)S(1)}, bf16[5,144,128]{2,1,0:T(8,128)(2,1)S(1)}, u32[]{:S(2)}, u32[]{:S(2)}) collective-permute-start(bf16[5,144,128]{2,1,0:T(8,128)(2,1)S(1)} %copy-done.14), channel_id=1, source_target_pairs={{0,3},{1,2},{2,5},{3,4},{4,7},{5,6},{6,1},{7,0},{8,11},{9,10},{10,... | collective-permute-start | bytes 552968 | tf_op jit(solution)/shard_map/ppermute | solution.py:94
  236.1 49.4 %all-to-all-start.5 = ((bf16[16,5,144,128]{3,2,1,0:T(8,128)(2,1)}), bf16[16,5,144,128]{3,2,1,0:T(8,128)(2,1)}, u32[]{:S(2)}, u32[]{:S(2)}) async-start(bf16[16,5,144,128]{3,2,1,0:T(8,128)(2,1)} %route_back.3), calls=%async_computation.5 | async-start | bytes 5898240 | tf_op jit(solution)/shard_map/all_to_all | solution.py:702
  243.2 20.1 %collective-permute-start.15 = (bf16[16,8,2688]{2,1,0:T(8,128)(2,1)S(1)}, bf16[16,8,2688]{2,1,0:T(8,128)(2,1)S(1)}, u32[]{:S(2)}, u32[]{:S(2)}) collective-permute-start(bf16[16,8,2688]{2,1,0:T(8,128)(2,1)S(1)} %get-tuple-element.150), channel_id=1, source_target_pairs={{0,2},{1,3},{2,4},{3,5},{4,6},{5,7},{6,0},{7,1},{8,10},{9,11},{10,... | collective-permute-start | bytes 2064392 | tf_op jit(solution)/shard_map/ppermute | solution.py:710
  244.2 32.0 %collective-permute-start.16 = (bf16[16,8,2688]{2,1,0:T(8,128)(2,1)S(1)}, bf16[16,8,2688]{2,1,0:T(8,128)(2,1)S(1)}, u32[]{:S(2)}, u32[]{:S(2)}) collective-permute-start(bf16[16,8,2688]{2,1,0:T(8,128)(2,1)S(1)} %get-tuple-element.152), channel_id=1, source_target_pairs={{0,4},{1,5},{2,6},{3,7},{4,0},{5,1},{6,2},{7,3},{8,12},{9,13},{10,... | collective-permute-start | bytes 2064392 | tf_op jit(solution)/shard_map/ppermute | solution.py:710
  246.9 43.0 %copy-start.4 = (s32[48]{0:T(128)S(1)}, s32[48]{0:T(128)}, u32[]{:S(2)}) copy-start(s32[48]{0:T(128)} %get-tuple-element.149.own_ref) | copy-start | bytes 580
  246.9 43.0 %copy-start.5 = (s32[48]{0:T(128)S(1)}, s32[48]{0:T(128)}, u32[]{:S(2)}) copy-start(s32[48]{0:T(128)} %and_select_fusion.pos_ref) | copy-start | bytes 580
  246.9 30.0 %collective-permute-start.17 = (bf16[16,8,2688]{2,1,0:T(8,128)(2,1)S(1)}, bf16[16,8,2688]{2,1,0:T(8,128)(2,1)S(1)}, u32[]{:S(2)}, u32[]{:S(2)}) collective-permute-start(bf16[16,8,2688]{2,1,0:T(8,128)(2,1)S(1)} %get-tuple-element.151), channel_id=1, source_target_pairs={{0,6},{1,7},{2,0},{3,1},{4,2},{5,3},{6,4},{7,5},{8,14},{9,15},{10,... | collective-permute-start | bytes 2064392 | tf_op jit(solution)/shard_map/ppermute | solution.py:710
  285.5 16.9 %all-to-all-start.6 = ((bf16[16,8,2688]{2,1,0:T(8,128)(2,1)}), bf16[16,8,2688]{2,1,0:T(8,128)(2,1)}, u32[]{:S(2)}, u32[]{:S(2)}) async-start(bf16[16,8,2688]{2,1,0:T(8,128)(2,1)} %fusion.2), calls=%async_computation.6 | async-start | bytes 1376256 | tf_op jit(solution)/shard_map/all_to_all | solution.py:713
  (17 other events, 161.4 us)
